TPU v7x, 128 devices: a whole 4x4x4 slice. The times are simulated.
128 devices in a mesh: prompt: 4 (over x), dp: 4 (over y), mp: 8 (over z, core).
Axes of the slice: x: 4, y: 4, z: 4, core: 2. Of those that a mesh axis runs over, the one named last changes fastest.
Arguments:
- prompts: bfloat16 [8, 100, 4096], P('prompt'), may hold values from -6 to 6
- target_embed: bfloat16 [4, 512, 4096], P('dp'), may hold values from -6 to 6
- labels: int32 [4, 512], P('dp'), may hold values from 0 to 16383
- lengths: int32 [4], P('dp'), may hold values from 128 to 512
- attn_gain: float32 [4096], replicated, may hold values from 0.5 to 1.5
- w_qkv: bfloat16 [3, 4096, 2048], P(None, None, 'mp'), may hold values from -4 to 4
- w_out: bfloat16 [2048, 4096], P('mp'), may hold values from -0.5 to 0.5
- final_gain: float32 [4096], replicated, may hold values from 0.5 to 1.5
- w_vocab: bfloat16 [4096, 16384], P(None, ('dp', 'mp')), may hold values from -3 to 3
Outputs:
- token_loss: float32 [8, 4, 512], P('prompt', 'dp')
- prompt_loss: float32 [8], replicated
Inputs may be any that keep to these rules, and one draw needn't show every extreme that they name: `lengths`: positions from a sequence's length on are padding.
All inputs are finite; a program needn't handle non-finite values.
Results may differ from a plain program's by a relative error of at most 0.006.
Values may be sent and summed in bfloat16 or wider, within the bound.
No kernel may reach another device: no remote copies, remote signals or barrier semaphores. Data moves between devices by JAX's collectives and lax.ppermute only.
A program may use at most 128 MiB of HBM per device.

v0:
```python
import math

import jax
import jax.numpy as jnp
from jax import lax
from jax.sharding import Mesh
from jax.sharding import PartitionSpec as P

HD = 128
MP = ("mp_0", "mp_1")
DP_MP = ("dp", "mp_0", "mp_1")


EPSILON = 1e-05
BASE_THETA = 10000.0


def collected_together(value, axis):
    leaves = jax.tree.leaves(value)
    order = sorted(range(len(leaves)), key=lambda k: -leaves[k].size)
    width = (1, *leaves[order[0]].shape)[-1]
    lines = [
        jnp.pad(leaves[k].reshape(-1), (0, -leaves[k].size % width)).reshape(-1, width)
        for k in order
    ]
    both, at, found = (lax.all_gather(jnp.concatenate(lines), axis), 0, {})
    for k, line in zip(order, lines):
        slab = both[:, at : at + len(line)].reshape(len(both), -1)
        found[k] = slab[:, : leaves[k].size].reshape(-1, *leaves[k].shape)
        at += len(line)
    numbers = iter(range(len(leaves)))
    return jax.tree.map(lambda _: found[next(numbers)], value)


def merged_by_axis(value, axes, combine):
    for axis in axes:
        pieces = collected_together(
            jax.tree.map(
                lambda part, kind: part.astype(kind),
                value,
                jax.tree.map(lambda a: jnp.bfloat16 if a.dtype == jnp.float32 else a.dtype, value),
            ),
            axis,
        )
        widened = [
            jax.tree.map(lambda part, own: part[k].astype(own.dtype), pieces, value)
            for k in range(lax.axis_size(axis))
        ]
        value = widened[0]
        for other in widened[1:]:
            value = combine(value, other)
    return value


def sent_to_all(value, axis):
    copies = jnp.broadcast_to(value, (lax.axis_size(axis), *value.shape))
    return lax.all_to_all(copies, axis, split_axis=0, concat_axis=0, tiled=True)


def of_everyone(value, axis):
    everything = sent_to_all(value, axis)
    return jnp.sum(everything, axis=0)


def rms_scaled(values, gain_vec):
    widened = values.astype(jnp.float32)
    return (
        widened
        * lax.rsqrt(jnp.mean(widened * widened, axis=-1, keepdims=True) + EPSILON)
        * gain_vec
    )


def rotate(values, offset, head_dim):
    number_rows = values.shape[-2]
    full_width = values.shape[-1]
    per_head = values.reshape(values.shape[:-1] + (full_width // head_dim, head_dim))
    half_dim = head_dim // 2
    positions = (offset + jnp.arange(number_rows, dtype=jnp.int32)).astype(jnp.float32)
    indices_f = jnp.arange(half_dim, dtype=jnp.int32).astype(jnp.float32)
    frequency = jnp.exp(indices_f * (-2.0 * math.log(BASE_THETA) / head_dim))
    angles = positions[:, None] * frequency[None, :]
    cosine = jnp.cos(angles)[:, None, :]
    sine_part = jnp.sin(angles)[:, None, :]
    first_half = per_head[..., :half_dim]
    second_half = per_head[..., half_dim:]
    turned = jnp.concatenate(
        [
            first_half * cosine - second_half * sine_part,
            second_half * cosine + first_half * sine_part,
        ],
        axis=-1,
    )
    return turned.reshape(values.shape)


def project(normed, weights, offset, rotated_count):
    lead_shape = normed.shape[:-1]
    flat_rows = normed.reshape(-1, normed.shape[-1])
    stacked = jnp.einsum("nd,cde->cne", flat_rows, weights, preferred_element_type=jnp.float32)
    stacked = stacked.reshape((weights.shape[0],) + lead_shape + (weights.shape[2],))
    results = []
    for index_w in range(weights.shape[0]):
        product = stacked[index_w]
        if index_w < rotated_count:
            product = rotate(product, offset, HD)
        results.append(product.astype(jnp.bfloat16))
    return tuple(results)


def attend(prompt_keys, prompt_vals, target_q, target_k, target_v):
    seq_count = target_q.shape[0]
    target_len = target_q.shape[1]
    prompt_len = prompt_keys.shape[0]
    heads_here = target_q.shape[2] // HD
    keys_all = jnp.concatenate([prompt_keys[None], target_k], axis=1)
    vals_all = jnp.concatenate([prompt_vals[None], target_v], axis=1)
    query_h = target_q.reshape(seq_count, target_len, heads_here, HD)
    key_h = keys_all.reshape(seq_count, prompt_len + target_len, heads_here, HD)
    val_h = vals_all.reshape(seq_count, prompt_len + target_len, heads_here, HD)
    scores = jnp.einsum(
        "bqhe,bkhe->bhqk", query_h, key_h, preferred_element_type=jnp.float32
    ) * HD ** (-0.5)
    key_index = jnp.arange(prompt_len + target_len, dtype=jnp.int32)
    query_pos = prompt_len + jnp.arange(target_len, dtype=jnp.int32)
    allowed = key_index[None, :] <= query_pos[:, None]
    scores = jnp.where(allowed[None, None], scores, -1e30)
    top_val = jnp.max(scores, axis=-1, keepdims=True)
    expo = jnp.exp(scores - top_val)
    probs = (expo / jnp.sum(expo, axis=-1, keepdims=True)).astype(jnp.bfloat16)
    context = jnp.einsum("bhqk,bkhe->bqhe", probs, val_h, preferred_element_type=jnp.float32)
    return context.astype(jnp.bfloat16).reshape(seq_count, target_len, heads_here * HD)


def block_stats(normed_rows, label_ids, columns, column_ids):
    logits = jnp.dot(normed_rows, columns, preferred_element_type=jnp.float32)
    top_val = jnp.max(logits, axis=1)
    sum_exp = jnp.sum(jnp.exp(logits - top_val[:, None]), axis=1)
    picked = jnp.sum(jnp.where(column_ids[None, :] == label_ids[:, None], logits, 0.0), axis=1)
    return (top_val, sum_exp, picked)


def combine_stats(earlier, later):
    top_val = jnp.maximum(earlier[0], later[0])
    sum_exp = earlier[1] * jnp.exp(earlier[0] - top_val) + later[1] * jnp.exp(later[0] - top_val)
    return (top_val, sum_exp, earlier[2] + later[2])


def shards(prompts, target_embed, labels, lengths, attn_gain, w_qkv, w_out, final_gain, w_vocab):
    n_prompt = lax.axis_size("prompt")
    n_model = lax.axis_size(MP)
    prompts_here = prompts.shape[0]
    prompt_len = prompts.shape[1]
    seq_count = target_embed.shape[0]
    target_len = target_embed.shape[1]
    model_width = target_embed.shape[2]
    normed_target = rms_scaled(target_embed, attn_gain).astype(jnp.bfloat16)
    target_q, target_k, target_v = project(normed_target, w_qkv, prompt_len, 2)
    normed_prompts = rms_scaled(prompts, attn_gain).astype(jnp.bfloat16)
    prompt_k, prompt_v = project(normed_prompts, w_qkv[1:], 0, 1)

    def one_prompt(pair):
        return attend(pair[0], pair[1], target_q, target_k, target_v)

    contexts = lax.map(one_prompt, (prompt_k, prompt_v))
    ctx_rows = contexts.reshape(-1, contexts.shape[-1])
    total_rows = ctx_rows.shape[0]
    keep_rows = total_rows // n_model
    row_context = lax.all_to_all(ctx_rows, MP, split_axis=0, concat_axis=1, tiled=True)
    full_out = lax.all_gather(w_out, MP, axis=0, tiled=True)
    group_width = w_out.shape[0]
    grouped = jnp.einsum(
        "rgk,gkd->rgd",
        row_context.reshape(keep_rows, n_model, group_width),
        full_out.reshape(n_model, group_width, model_width),
        preferred_element_type=jnp.float32,
    )
    attn_part = jnp.sum(grouped.astype(jnp.bfloat16).astype(jnp.float32), axis=1)
    my_start = lax.axis_index(MP) * keep_rows
    embed_rows = jnp.tile(target_embed.reshape(-1, model_width), (prompts_here, 1))
    residual = lax.dynamic_slice_in_dim(embed_rows, my_start, keep_rows, 0).astype(jnp.float32)
    label_rows = lax.dynamic_slice_in_dim(
        jnp.tile(labels.reshape(-1), prompts_here), my_start, keep_rows, 0
    )
    hidden = residual + attn_part
    normed_out = rms_scaled(hidden, final_gain).astype(jnp.bfloat16)
    vocab_cols = w_vocab.shape[1]
    every_rows, every_labels = (
        lax.all_gather(normed_out, DP_MP, axis=0, tiled=True),
        lax.all_gather(label_rows, DP_MP, axis=0, tiled=True),
    )
    block_index = lax.axis_index("dp") * n_model + lax.axis_index(MP)
    column_ids = block_index * vocab_cols + jnp.arange(vocab_cols, dtype=jnp.int32)
    local_stats = block_stats(every_rows, every_labels, w_vocab, column_ids)
    merged = merged_by_axis(local_stats, DP_MP, combine_stats)
    group_start = lax.axis_index("dp") * total_rows
    merged = tuple(
        (lax.dynamic_slice_in_dim(member, group_start, total_rows, 0) for member in merged)
    )
    losses = (merged[0] + jnp.log(merged[1]) - merged[2]).reshape(
        prompts_here, seq_count, target_len
    )
    valid = jnp.arange(target_len, dtype=jnp.int32)[None, :] < lengths[:, None]
    token_loss = jnp.where(valid[None], losses, 0.0)
    prompt_sums = jnp.sum(token_loss, axis=(1, 2))
    all_prompts = prompts_here * n_prompt
    slot_ids = lax.axis_index("prompt") * prompts_here + jnp.arange(prompts_here, dtype=jnp.int32)
    placed = jnp.sum(
        jnp.where(
            jnp.arange(all_prompts, dtype=jnp.int32)[:, None] == slot_ids[None, :],
            prompt_sums[None, :],
            0.0,
        ),
        axis=1,
    )
    valid_here = jnp.sum(lengths).astype(jnp.float32)
    totals, counted = (
        of_everyone(placed, ("prompt", "dp")),
        of_everyone(valid_here, ("prompt", "dp")),
    )
    prompt_loss = totals * float(n_prompt) / counted
    return (token_loss, prompt_loss)


def solution(mesh):
    finer = Mesh(
        mesh.devices.reshape(mesh.shape["prompt"], mesh.shape["dp"], 4, 2),
        ("prompt", "dp", "mp_0", "mp_1"),
    )
    return jax.shard_map(
        shards,
        mesh=finer,
        in_specs=(
            P("prompt", None, None),
            P("dp", None, None),
            P("dp", None),
            P("dp"),
            P(),
            P(None, None, MP),
            P(MP, None),
            P(),
            P(None, DP_MP),
        ),
        out_specs=(P("prompt", "dp", None), P()),
        check_vma=False,
    )
```

profile of v0, /device:TPU:0, one launch (start us, length us, event | category | flops | bytes accessed | tf_op | source)
XLA Modules:
  0.0 313.7 jit_solution(16696660986336960218)
XLA Ops:
  7.9 3.2 %fusion.36 = f32[2,100]{0,1:T(8,128)S(1)} fusion(bf16[2,100,4096]{2,0,1:T(2,128)(2,1)} %param.11), kind=kLoop, calls=%fused_computation.40 | loop fusion | flops 2457400 | bytes 1639200 | tf_op jit(solution)/shard_map/reduce_sum | solution.py:69
  11.2 2.4 fusion.38
  13.6 1.0 copy.72
  14.9 3.2 %fusion.42 = f32[2,200,256]{2,1,0:T(8,128)S(1)} fusion(bf16[200,4096,1]{1,0,2:T(8,128)(2,1)S(1)} %reshape.1004, bf16[3,4096,256]{2,1,0:T(8,128)(2,1)} %param.16), kind=kOutput, calls=%fused_computation.47 | convolution fusion | flops 838860800 | bytes 6242304 | tf_op jit(solution)/shard_map/nd,cde->cne/dot_general | solution.py:100
  18.2 3.2 %fusion.26 = f32[512]{0:T(512)S(1)} fusion(bf16[1,512,4096]{2,1,0:T(8,128)(2,1)} %param.12), kind=kLoop, calls=%fused_computation.27 | loop fusion | flops 6290944 | bytes 4196352 | tf_op jit(solution)/shard_map/reduce_sum | solution.py:69
  21.5 0.7 copy-done.1
  22.2 6.4 %fusion.39 = f32[3,512,256]{1,2,0:T(8,128)S(1)} fusion(bf16[3,4096,256]{2,1,0:T(8,128)(2,1)} %param.16, bf16[1,512,4096]{2,1,0:T(8,128)(2,1)S(1)} %copy-done.1, f32[4096]{0:T(1024)S(1)} %copy-done.7, f32[512]{0:T(512)S(1)} %add_rsqrt_fusion.1), kind=kOutput, calls=%fused_computation.46 | convolution fusion | flops 3229614080 | bytes 12077056 | tf_op jit(solution)/shard_map/nd,cde->cne/dot_general | solution.py:100
  31.1 8.7 %while.11 = (s32[]{:T(128)}, bf16[2,1,512,256]{3,2,0,1:T(8,128)(2,1)}, bf16[2,100,256]{2,1,0:T(8,128)(2,1)S(1)}, bf16[1,512,256]{1,2,0:T(8,128)(2,1)S(1)}, bf16[...) while((s32[]{:T(128)}, ...), condition=%wide.wide.region_5.6_spmd, body=%wide.wide.region_2.5_spmd.sunk | while | flops 488637120 | bytes 5288549 | solution.py:165
  31.8 1.2 fusion.133
  33.0 1.6 fusion.134
  34.7 0.7 constant_dynamic-update-slice_fusion.3
  36.1 1.2 fusion.133
  37.3 1.6 fusion.134
  39.0 0.7 constant_dynamic-update-slice_fusion.3
  39.7 5.8 %all-to-all-start = ((bf16[8,128,256]{2,1,0:T(8,128)(2,1)}), bf16[8,128,256]{2,1,0:T(8,128)(2,1)S(1)}, u32[]{:S(2)}, u32[]{:S(2)}) async-start(bf16[8,128,256]{2,1,0:T(8,128)(2,1)} %bitcast.18), calls=%async_computation | async-start | bytes 1048576 | tf_op jit(solution)/shard_map/all_to_all | solution.py:169
  45.6 16.2 %all-to-all-done = bf16[8,128,256]{2,1,0:T(8,128)(2,1)S(1)} async-done(((bf16[8,128,256]{2,1,0:T(8,128)(2,1)}), bf16[8,128,256]{2,1,0:T(8,128)(2,1)S(1)}, u32[]{:S(2)}, u32[]{:S(2)}) %all-to-all-start) | async-done | bytes 524320 | tf_op jit(solution)/shard_map/all_to_all | solution.py:169
  61.8 41.2 %all-gather.10.cloned.1.call-done = bf16[2048,4096]{1,0:T(8,128)(2,1)} async-done(((bf16[256,4096]{1,0:T(8,128)(2,1)}), bf16[2048,4096]{1,0:T(8,128)(2,1)}) %all-gather.10.cloned.1.call-update) | async-done | bytes 16777232 | tf_op jit(solution)/shard_map/all_gather | solution.py:170
  103.0 8.6 %convert_reduce_fusion = f32[128,4096]{1,0:T(8,128)S(1)} fusion(bf16[8,256,4096]{2,1,0:T(8,128)(2,1)} %bitcast.276, bf16[8,128,256]{2,1,0:T(8,128)(2,1)} %copy-done.4), kind=kOutput, calls=%fused_computation.24 | convolution fusion | flops 2159542272 | bytes 19398656 | tf_op jit(solution)/shard_map/rgk,gkd->rgd/dot_general | solution.py:172
  111.7 4.3 %tile.21 = bf16[2,512,4096]{2,1,0:T(8,128)(2,1)} broadcast(bf16[512,4096]{1,0:T(8,128)(2,1)S(1)} %bitcast.275), dimensions={1,2} | broadcast | bytes 12582912 | tf_op jit(solution)/shard_map/tile | solution.py:180
  116.0 1.6 multiply_reduce_fusion
  117.6 2.6 multiply_convert_fusion
  121.5 6.8 %all-to-all-start.2 = ((f32[16,1,1]{2,1,0:T(1,128)}), f32[16,1,1]{2,1,0:T(1,128)S(1)}, u32[]{:S(2)}, u32[]{:S(2)}) async-start(f32[16,1,1]{2,1,0:T(1,128)} %broadcast_in_dim.64), calls=%async_computation.2 | async-start | bytes 16384 | tf_op jit(solution)/shard_map/all_to_all | solution.py:57
  128.4 21.5 %all-gather.3 = s32[32,1,128]{2,1,0:T(1,128)S(1)} all-gather(s32[1,1,128]{2,1,0:T(1,128)S(1)} %dynamic-slice_bitcast_fusion), channel_id=1, replica_groups=mesh['prompt'=4,'dp'=4,'mp_0'=4,'mp_1'=2] {'dp','mp_0','mp_1'}, dimensions={0}, use_global_device_ids=true | all-gather | bytes 16896 | tf_op jit(solution)/shard_map/all_gather | solution.py:190
  149.9 84.9 %all-gather.12.cloned.1.call-done = bf16[4096,4096]{1,0:T(8,128)(2,1)} async-done(((bf16[128,4096]{1,0:T(8,128)(2,1)}), bf16[4096,4096]{1,0:T(8,128)(2,1)}) %all-gather.12.cloned.1.call-update) | async-done | bytes 33554448 | tf_op jit(solution)/shard_map/all_gather | solution.py:189
  234.8 24.1 %fusion.105 = (f32[4096]{0:T(1024)S(1)}, f32[4096,512]{0,1:T(8,128)}) fusion(bf16[4096,4096]{1,0:T(8,128)(2,1)} %all-gather.12.cloned.1.call-done, bf16[4096,512]{1,0:T(8,128)(2,1)} %param.19), kind=kOutput, calls=%fused_computation.174 | convolution fusion | flops 17181962240 | bytes 46153728 | tf_op jit(solution)/shard_map/dot_general | solution.py:136
  258.9 4.6 %exponential_reduce_fusion = (bf16[4096]{0:T(1024)(128)(2,1)S(1)}, bf16[4096]{0:T(1024)(128)(2,1)S(1)}) fusion(f32[4096,512]{0,1:T(8,128)} %get-tuple-element.134, f32[4096]{0:T(1024)S(1)} %get-tuple-element.133, s32[4096]{0:T(1024)S(1)} %bitcast.292, s32[512]{0:T(512)S(1)} %iota_add_fusion.1), kind=kLoop, calls=%fused_computation.31 | loop fusion | flops 10477568 | bytes 8439808 | tf_op jit(solution)/shard_map/reduce_sum | solution.py:138
  263.5 12.3 %all-gather.4 = bf16[4,3,4096]{2,1,0:T(4,128)(2,1)S(1)} all-gather(bf16[1,3,4096]{2,1,0:T(4,128)(2,1)S(1)} %maximum_bitcast_fusion), channel_id=2, replica_groups=mesh['prompt'=4,'dp'=4,'mp_0'=4,'mp_1'=2] {'dp'}, dimensions={0}, use_global_device_ids=true | all-gather | bytes 122880 | tf_op jit(solution)/shard_map/all_gather | solution.py:26
  276.2 12.0 %all-gather.5 = bf16[4,3,4096]{2,1,0:T(4,128)(2,1)S(1)} all-gather(bf16[1,3,4096]{2,1,0:T(4,128)(2,1)S(1)} %maximum_bitcast_fusion.1), channel_id=3, replica_groups=mesh['prompt'=4,'dp'=4,'mp_0'=4,'mp_1'=2] {'mp_0'}, dimensions={0}, use_global_device_ids=true | all-gather | bytes 122880 | tf_op jit(solution)/shard_map/all_gather | solution.py:26
  288.5 1.9 all-gather.6
  291.8 6.3 %all-to-all-start.1 = ((f32[16,1,8]{2,1,0:T(1,128)}), f32[16,1,8]{2,1,0:T(1,128)S(1)}, u32[]{:S(2)}, u32[]{:S(2)}) async-start(f32[16,1,8]{2,1,0:T(1,128)} %broadcast_in_dim.59), calls=%async_computation.1 | async-start | bytes 16384 | tf_op jit(solution)/shard_map/all_to_all | solution.py:57
  298.8 6.9 %all-to-all-done.1 = f32[16,1,8]{2,1,0:T(1,128)S(1)} async-done(((f32[16,1,8]{2,1,0:T(1,128)}), f32[16,1,8]{2,1,0:T(1,128)S(1)}, u32[]{:S(2)}, u32[]{:S(2)}) %all-to-all-start.1) | async-done | bytes 544 | tf_op jit(solution)/shard_map/all_to_all | solution.py:57
  305.8 1.1 multiply_divide_fusion
  (87 shorter events, 8.6 us)
Async XLA Ops:
  7.2 121.1 %copy-start = (s32[1,512]{1,0:T(1,128)S(1)}, s32[1,512]{1,0:T(1,128)}, u32[]{:S(2)}) copy-start(s32[1,512]{1,0:T(1,128)} %param.13) | copy-start | bytes 6148
  7.2 4.0 %copy-start.3 = (bf16[2,100,4096]{2,0,1:T(2,128)(2,1)S(1)}, bf16[2,100,4096]{2,0,1:T(2,128)(2,1)}, u32[]{:S(2)}) copy-start(bf16[2,100,4096]{2,0,1:T(2,128)(2,1)} %param.11) | copy-start | bytes 4915204
  7.2 4.0 %copy-start.7 = (f32[4096]{0:T(1024)S(1)}, f32[4096]{0:T(1024)}, u32[]{:S(2)}) copy-start(f32[4096]{0:T(1024)} %param.15) | copy-start | bytes 49156
  7.2 95.8 %all-gather.10.cloned.1.call-start = ((), (), s32[]{:S(2)}) async-start(), calls=%async_computation.3 | async-start | bytes 18874368 | tf_op jit(solution)/shard_map/all_gather | solution.py:170
  18.2 10.5 %copy-start.6 = (f32[2,200,256]{2,1,0:T(8,128)}, f32[2,200,256]{2,1,0:T(8,128)S(1)}, u32[]{:S(2)}) copy-start(f32[2,200,256]{2,1,0:T(8,128)S(1)} %fusion.42) | copy-start | bytes 1228804
  18.2 4.0 %copy-start.1 = (bf16[1,512,4096]{2,1,0:T(8,128)(2,1)S(1)}, bf16[1,512,4096]{2,1,0:T(8,128)(2,1)}, u32[]{:S(2)}) copy-start(bf16[1,512,4096]{2,1,0:T(8,128)(2,1)} %param.12) | copy-start | bytes 12582916
  28.7 1.1 slice-start
  29.7 1.4 copy-start.5
  39.7 22.1 %all-to-all-start = ((bf16[8,128,256]{2,1,0:T(8,128)(2,1)}), bf16[8,128,256]{2,1,0:T(8,128)(2,1)S(1)}, u32[]{:S(2)}, u32[]{:S(2)}) async-start(bf16[8,128,256]{2,1,0:T(8,128)(2,1)} %bitcast.18), calls=%async_computation | async-start | bytes 1048576 | tf_op jit(solution)/shard_map/all_to_all | solution.py:169
  45.5 189.3 %all-gather.12.cloned.1.call-start = ((), (), s32[]{:S(2)}) async-start(), calls=%async_computation.4 | async-start | bytes 34603008 | tf_op jit(solution)/shard_map/all_gather | solution.py:189
  61.8 41.2 %copy-start.4 = (bf16[8,128,256]{2,1,0:T(8,128)(2,1)}, bf16[8,128,256]{2,1,0:T(8,128)(2,1)S(1)}, u32[]{:S(2)}) copy-start(bf16[8,128,256]{2,1,0:T(8,128)(2,1)S(1)} %all-to-all-done) | copy-start | bytes 1572868
  103.0 8.6 %copy-start.2 = (bf16[1,512,4096]{2,1,0:T(8,128)(2,1)S(1)}, bf16[1,512,4096]{2,1,0:T(8,128)(2,1)}, u32[]{:S(2)}) copy-start(bf16[1,512,4096]{2,1,0:T(8,128)(2,1)} %param.12) | copy-start | bytes 12582916
  111.7 5.9 %copy-start.8 = (f32[4096]{0:T(1024)S(1)}, f32[4096]{0:T(1024)}, u32[]{:S(2)}) copy-start(f32[4096]{0:T(1024)} %param.18) | copy-start | bytes 49156
  121.5 169.7 %all-to-all-start.2 = ((f32[16,1,1]{2,1,0:T(1,128)}), f32[16,1,1]{2,1,0:T(1,128)S(1)}, u32[]{:S(2)}, u32[]{:S(2)}) async-start(f32[16,1,1]{2,1,0:T(1,128)} %broadcast_in_dim.64), calls=%async_computation.2 | async-start | bytes 16384 | tf_op jit(solution)/shard_map/all_to_all | solution.py:57
  291.8 13.9 %all-to-all-start.1 = ((f32[16,1,8]{2,1,0:T(1,128)}), f32[16,1,8]{2,1,0:T(1,128)S(1)}, u32[]{:S(2)}, u32[]{:S(2)}) async-start(f32[16,1,8]{2,1,0:T(1,128)} %broadcast_in_dim.59), calls=%async_computation.1 | async-start | bytes 16384 | tf_op jit(solution)/shard_map/all_to_all | solution.py:57
Sparse Core Ops, SparseCore 0:
  9.7 93.2 all-gather.9
  120.4 114.3 all-gather.11
where the time goes:
time: 314 us
  waiting for transfers between devices  150 us (48%)
  matrix products  47.8 us (15%)
  blocking collectives  47.6 us (15%)
  other arithmetic  23.8 us (8%)
  starting transfers between devices  19 us (6%)
  between operations  15.1 us (5%)
  local copies, waits for them, and re-layouts  10.3 us (3%)
    all_gather x1, waiting for transfers between devices, shards(): lax.all_gather(normed_out, DP_MP, axis=0, tiled=True)  84.9 us
    all_gather x1, waiting for transfers between devices, shards(): full_out = lax.all_gather(w_out, MP, axis=0, tiled=True)  41.2 us
    all_gather x3, blocking collectives, collected_together(): both, at, found = (lax.all_gather(jnp.concatenate(lines), axis), 0, {})  26.1 us
    dot_general x1, matrix products, block_stats(): logits = jnp.dot(normed_rows, columns, preferred_element_type=jnp.float32)  24.1 us
    all_gather x1, blocking collectives, shards(): lax.all_gather(label_rows, DP_MP, axis=0, tiled=True)  21.5 us
    all_to_all x1, waiting for transfers between devices, shards(): lax.all_to_all(ctx_rows, MP, split_axis=0, concat_axis=1, tiled=True)  16.2 us
    all_to_all x2, starting transfers between devices, sent_to_all(): return lax.all_to_all(copies, axis, split_axis=0, concat_axis=0, tiled=True)  13.1 us
    dot_general x2, matrix products, project(): jnp.einsum('nd,cde->cne', flat_rows, weights, preferred_element_type=jnp....  9.64 us
  transfers between devices with their start and end apart: 5, of which 4 were waited for; matrix products, arithmetic and copies ran while one was open for 20% of the time, Pallas kernels for 0%

commit v1 on v0

v1 whole, which is shorter than its diff:
```python
import math

import jax
import jax.numpy as jnp
from jax import lax
from jax.sharding import Mesh
from jax.sharding import PartitionSpec as P

HD = 128
MP = ("mp_0", "mp_1")
DP_MP = ("dp", "mp_0", "mp_1")


EPSILON = 1e-05
BASE_THETA = 10000.0


def of_everyone(value, axis):
    copies = jnp.broadcast_to(value, (lax.axis_size(axis), *value.shape))
    everything = lax.all_to_all(copies, axis, split_axis=0, concat_axis=0, tiled=True)
    return jnp.sum(everything, axis=0)


def shifted(value, axis, shift):
    n = lax.axis_size(axis)
    return lax.ppermute(value, axis, [(i, (i + shift) % n) for i in range(n)])


def ring_of_four(block, axis):
    half = block.shape[0] // 2
    before = shifted(block, axis, 1)
    after = shifted(block, axis, -1)
    far_low = shifted(before[:half], axis, 1)
    far_high = shifted(after[half:], axis, -1)
    return [block, before, after, jnp.concatenate([far_low, far_high], axis=0)]


RING = (0, 3, 1, 2)


def rms_scaled(values, gain_vec):
    widened = values.astype(jnp.float32)
    return (
        widened
        * lax.rsqrt(jnp.mean(widened * widened, axis=-1, keepdims=True) + EPSILON)
        * gain_vec
    )


def rotate(values, offset, head_dim):
    number_rows = values.shape[-2]
    full_width = values.shape[-1]
    per_head = values.reshape(values.shape[:-1] + (full_width // head_dim, head_dim))
    half_dim = head_dim // 2
    positions = (offset + jnp.arange(number_rows, dtype=jnp.int32)).astype(jnp.float32)
    indices_f = jnp.arange(half_dim, dtype=jnp.int32).astype(jnp.float32)
    frequency = jnp.exp(indices_f * (-2.0 * math.log(BASE_THETA) / head_dim))
    angles = positions[:, None] * frequency[None, :]
    cosine = jnp.cos(angles)[:, None, :]
    sine_part = jnp.sin(angles)[:, None, :]
    first_half = per_head[..., :half_dim]
    second_half = per_head[..., half_dim:]
    turned = jnp.concatenate(
        [
            first_half * cosine - second_half * sine_part,
            second_half * cosine + first_half * sine_part,
        ],
        axis=-1,
    )
    return turned.reshape(values.shape)


def project(normed, weights, offset, rotated_count):
    lead_shape = normed.shape[:-1]
    flat_rows = normed.reshape(-1, normed.shape[-1])
    stacked = jnp.einsum("nd,cde->cne", flat_rows, weights, preferred_element_type=jnp.float32)
    stacked = stacked.reshape((weights.shape[0],) + lead_shape + (weights.shape[2],))
    results = []
    for index_w in range(weights.shape[0]):
        product = stacked[index_w]
        if index_w < rotated_count:
            product = rotate(product, offset, HD)
        results.append(product.astype(jnp.bfloat16))
    return tuple(results)


def attend(prompt_keys, prompt_vals, target_q, target_k, target_v):
    seq_count = target_q.shape[0]
    target_len = target_q.shape[1]
    prompt_len = prompt_keys.shape[0]
    heads_here = target_q.shape[2] // HD
    keys_all = jnp.concatenate([prompt_keys[None], target_k], axis=1)
    vals_all = jnp.concatenate([prompt_vals[None], target_v], axis=1)
    query_h = target_q.reshape(seq_count, target_len, heads_here, HD)
    key_h = keys_all.reshape(seq_count, prompt_len + target_len, heads_here, HD)
    val_h = vals_all.reshape(seq_count, prompt_len + target_len, heads_here, HD)
    scores = jnp.einsum(
        "bqhe,bkhe->bhqk", query_h, key_h, preferred_element_type=jnp.float32
    ) * HD ** (-0.5)
    key_index = jnp.arange(prompt_len + target_len, dtype=jnp.int32)
    query_pos = prompt_len + jnp.arange(target_len, dtype=jnp.int32)
    allowed = key_index[None, :] <= query_pos[:, None]
    scores = jnp.where(allowed[None, None], scores, -1e30)
    top_val = jnp.max(scores, axis=-1, keepdims=True)
    expo = jnp.exp(scores - top_val)
    probs = (expo / jnp.sum(expo, axis=-1, keepdims=True)).astype(jnp.bfloat16)
    context = jnp.einsum("bhqk,bkhe->bqhe", probs, val_h, preferred_element_type=jnp.float32)
    return context.astype(jnp.bfloat16).reshape(seq_count, target_len, heads_here * HD)


def shards(prompts, target_embed, labels, lengths, attn_gain, w_qkv, w_out, final_gain, w_vocab):
    n_prompt = lax.axis_size("prompt")
    n_dp = lax.axis_size("dp")
    n_model = lax.axis_size(MP)
    prompts_here = prompts.shape[0]
    prompt_len = prompts.shape[1]
    target_len = target_embed.shape[1]
    model_width = target_embed.shape[2]
    vocab_cols = w_vocab.shape[1]
    heads_width = w_out.shape[0]
    z_index = lax.axis_index("mp_0")
    core = lax.axis_index("mp_1")
    part = model_width // n_model
    places = [((z_index + r) % 4) * 2 + (core + k) % 2 for r in RING for k in range(2)]

    my_places = ((z_index + jnp.take(jnp.array(RING), lax.axis_index("prompt"))) % 4) * 2
    piece = jnp.concatenate(
        [
            lax.dynamic_slice_in_dim(w_vocab, (my_places + (core + k) % 2) * part, part, 0)
            for k in range(2)
        ],
        axis=0,
    )
    vocab_all = lax.all_gather(piece, ("dp", "prompt"), axis=0, tiled=True)
    vocab_all = vocab_all.reshape(n_dp, model_width, vocab_cols)

    out_cols = lax.all_to_all(
        w_out.reshape(heads_width, n_model, part), MP, split_axis=1, concat_axis=0, tiled=True
    ).reshape(n_model * heads_width, part)
    out_cols = jnp.concatenate(
        [lax.dynamic_slice_in_dim(out_cols, p * heads_width, heads_width, 0) for p in places],
        axis=0,
    )

    normed_target = rms_scaled(target_embed, attn_gain).astype(jnp.bfloat16)
    target_q, target_k, target_v = project(normed_target, w_qkv, prompt_len, 2)
    normed_prompts = rms_scaled(prompts, attn_gain).astype(jnp.bfloat16)
    prompt_k, prompt_v = project(normed_prompts, w_qkv[1:], 0, 1)
    contexts = [
        attend(prompt_k[p], prompt_v[p], target_q, target_k, target_v) for p in range(prompts_here)
    ]
    ctx = jnp.concatenate(contexts, axis=0).reshape(prompts_here * target_len, heads_width)

    def whole_row(block):
        blocks = ring_of_four(block, "mp_0")
        return jnp.concatenate(
            [b for mine in blocks for b in (mine, shifted(mine, "mp_1", 1))], axis=1
        )

    ctx_all = whole_row(ctx)
    attn_part = jnp.dot(ctx_all, out_cols, preferred_element_type=jnp.float32)
    my_place = places[0] * part
    residual = lax.dynamic_slice_in_dim(target_embed[0], my_place, part, 1).astype(jnp.float32)
    hidden = residual[None] + attn_part.reshape(prompts_here, target_len, part)
    gain = lax.dynamic_slice_in_dim(final_gain, my_place, part, 0)
    scaled = (hidden * gain).astype(jnp.bfloat16).reshape(prompts_here * target_len, part)
    rows = whole_row(scaled)
    gain_ring = jnp.concatenate(
        [lax.dynamic_slice_in_dim(final_gain, p * part, part, 0) for p in places], axis=0
    )
    unscaled = rows.astype(jnp.float32) / gain_ring
    inverse = lax.rsqrt(jnp.mean(unscaled * unscaled, axis=-1) + EPSILON)

    row_labels = jnp.tile(labels.reshape(-1), prompts_here)
    my_block = lax.axis_index(MP)
    tops, sums, picks = [], [], []
    for d in range(n_dp):
        column_ids = (d * n_model + my_block) * vocab_cols + jnp.arange(vocab_cols, dtype=jnp.int32)
        logits = jnp.dot(rows, vocab_all[d], preferred_element_type=jnp.float32) * inverse[:, None]
        top_val = jnp.max(logits, axis=1)
        tops.append(top_val)
        sums.append(jnp.sum(jnp.exp(logits - top_val[:, None]), axis=1))
        picks.append(
            jnp.sum(jnp.where(column_ids[None, :] == row_labels[:, None], logits, 0.0), axis=1)
        )

    def total(tops, sums):
        top_val = jnp.max(tops, axis=0)
        return top_val + jnp.log(jnp.sum(sums * jnp.exp(tops - top_val), axis=0))

    here = jnp.stack([total(jnp.stack(tops), jnp.stack(sums)), sum(picks)])
    every = lax.all_gather(here, MP)
    log_total = total(every[:, 0], jnp.ones_like(every[:, 0]))
    losses = (log_total - jnp.sum(every[:, 1], axis=0)).reshape(prompts_here, 1, target_len)
    valid = jnp.arange(target_len, dtype=jnp.int32)[None, :] < lengths[:, None]
    token_loss = jnp.where(valid[None], losses, 0.0)
    prompt_sums = jnp.sum(token_loss, axis=(1, 2))
    all_prompts = prompts_here * n_prompt
    slot_ids = lax.axis_index("prompt") * prompts_here + jnp.arange(prompts_here, dtype=jnp.int32)
    placed = jnp.sum(
        jnp.where(
            jnp.arange(all_prompts, dtype=jnp.int32)[:, None] == slot_ids[None, :],
            prompt_sums[None, :],
            0.0,
        ),
        axis=1,
    )
    valid_here = jnp.sum(lengths).astype(jnp.float32).reshape(1)
    totals = of_everyone(jnp.concatenate([placed, valid_here]), ("prompt", "dp"))
    prompt_loss = totals[:all_prompts] * float(n_prompt) / totals[all_prompts]
    return (token_loss, prompt_loss)


def solution(mesh):
    finer = Mesh(
        mesh.devices.reshape(mesh.shape["prompt"], mesh.shape["dp"], 4, 2),
        ("prompt", "dp", "mp_0", "mp_1"),
    )
    return jax.shard_map(
        shards,
        mesh=finer,
        in_specs=(
            P("prompt", None, None),
            P("dp", None, None),
            P("dp", None),
            P("dp"),
            P(),
            P(None, None, MP),
            P(MP, None),
            P(),
            P(None, DP_MP),
        ),
        out_specs=(P("prompt", "dp", None), P()),
        check_vma=False,
    )
```

time: 314 us -> 264 us (0.84); the launches traced: 314 us -> 260 us
  waiting for transfers between devices: 150 us -> 58.9 us
  local copies, waits for them, and re-layouts: 10.3 us -> 56.2 us
  blocking collectives: 47.6 us -> 28 us
  matrix products: 47.8 us -> 53.8 us
    all_gather x2 -> x1, waiting for transfers between devices: 126 us -> 0.02 us  [shards(): vocab_all = lax.all_gather(piece, ('dp', 'prompt'), axis=0, tiled=True)]
    ppermute x0 -> x16, waiting for transfers between devices: none -> 58.8 us  [shifted(): return lax.ppermute(value, axis, [(i, (i + shift) % n) for i in range(n)])]
    unnamed x21 -> x67, local copies, waits for them, and re-layouts: 0.88 us -> 35 us
    all_gather x4 -> x1, blocking collectives: 47.6 us -> 13.6 us  [shards(): every = lax.all_gather(here, MP)]
    all_to_all x3 -> x1, waiting for transfers between devices: 23.2 us -> 0.01 us  [shards(): lax.all_to_all(w_out.reshape(heads_width, n_model, part), MP, split_axis=...]
    ppermute x0 -> x16, starting transfers between devices: none -> 15.7 us  [shifted(): return lax.ppermute(value, axis, [(i, (i + shift) % n) for i in range(n)])]
    all_to_all x0 -> x1, blocking collectives: none -> 14.4 us  [of_everyone(): lax.all_to_all(copies, axis, split_axis=0, concat_axis=0, tiled=True)]
    all_to_all x3 -> x1, starting transfers between devices: 18.9 us -> 4.78 us  [shards(): lax.all_to_all(w_out.reshape(heads_width, n_model, part), MP, split_axis=...]
  transfers between devices with their start and end apart: 5 -> 18, of which waited for: 4 -> 5; matrix products, arithmetic and copies ran while one was open for 20% -> 36% of each run, Pallas kernels for 0% -> 0%
where the time goes in v1:
time: 264 us; the launch traced here: 260 us
  waiting for transfers between devices  58.9 us (22%)
  local copies, waits for them, and re-layouts  56.2 us (21%)
  matrix products  53.8 us (20%)
  blocking collectives  28 us (11%)
  other arithmetic  26.6 us (10%)
  starting transfers between devices  20.5 us (8%)
  between operations  16.2 us (6%)
    ppermute x16, waiting for transfers between devices, shifted(): return lax.ppermute(value, axis, [(i, (i + shift) % n) for i in range(n)])  58.8 us
    unnamed x67, local copies, waits for them, and re-layouts  35 us
    dot_general x4, matrix products, shards(): jnp.dot(rows, vocab_all[d], preferred_element_type=jnp.float32)  30.2 us
    ppermute x16, starting transfers between devices, shifted(): return lax.ppermute(value, axis, [(i, (i + shift) % n) for i in range(n)])  15.7 us
    all_to_all x1, blocking collectives, of_everyone(): lax.all_to_all(copies, axis, split_axis=0, concat_axis=0, tiled=True)  14.4 us
    all_gather x1, blocking collectives, shards(): every = lax.all_gather(here, MP)  13.6 us
    dot_general x2, matrix products, project(): jnp.einsum('nd,cde->cne', flat_rows, weights, preferred_element_type=jnp....  9.9 us
    dot_general x1, matrix products, shards(): attn_part = jnp.dot(ctx_all, out_cols, preferred_element_type=jnp.float32)  5.93 us
  transfers between devices with their start and end apart: 18, of which 5 were waited for; matrix products, arithmetic and copies ran while one was open for 36% of the time, Pallas kernels for 0%

profile of v1, /device:TPU:0, one launch (start us, length us, event | category | flops | bytes accessed | tf_op | source)
XLA Modules:
  0.0 260.2 jit_solution(671899415837840228)
XLA Ops:
  11.6 3.2 %fusion.2 = f32[512]{0:T(512)S(1)} fusion(bf16[1,512,4096]{2,1,0:T(8,128)(2,1)} %param.11), kind=kLoop, calls=%fused_computation.5 | loop fusion | flops 6290944 | bytes 4196352 | tf_op jit(solution)/shard_map/reduce_sum | solution.py:45
  15.1 6.1 %fusion.25 = f32[3,512,256]{1,2,0:T(8,128)S(1)} fusion(bf16[3,4096,256]{2,1,0:T(8,128)(2,1)} %param.15, bf16[1,512,4096]{2,1,0:T(8,128)(2,1)S(1)} %copy-done.4, f32[4096]{0:T(1024)S(1)} %copy-done.11, f32[512]{0:T(512)S(1)} %add_rsqrt_fusion.2), kind=kOutput, calls=%fused_computation.48 | convolution fusion | flops 3229614080 | bytes 12077056 | tf_op jit(solution)/shard_map/nd,cde->cne/dot_general | solution.py:76
  25.4 2.0 copy.173
  29.1 3.2 %fusion.22 = bf16[2,100,4096]{2,0,1:T(2,128)(2,1)S(1)} fusion(bf16[2,100,4096]{2,0,1:T(2,128)(2,1)S(1)} %copy-done.3, f32[4096]{0:T(1024)} %param.14, f32[2,100]{0,1:T(8,128)S(1)} %add_rsqrt_fusion), kind=kLoop, calls=%fused_computation.26 | loop fusion | flops 3276800 | bytes 3293984 | tf_op jit(solution)/shard_map/convert_element_type | solution.py:147
  34.8 3.8 %fusion.106 = (bf16[2,200,256]{2,1,0:T(8,128)(2,1)S(1)}, f32[2,200,256]{2,1,0:T(8,128)S(1)}) fusion(bf16[200,4096,1]{1,0,2:T(8,128)(2,1)} %reshape.573, bf16[3,4096,256]{2,1,0:T(8,128)(2,1)} %param.15), kind=kOutput, calls=%fused_computation.190 | convolution fusion | flops 838963200 | bytes 6447104 | tf_op jit(solution)/shard_map/nd,cde->cne/dot_general | solution.py:76
  43.5 2.1 fusion.40
  46.9 3.4 %fusion.39 = bf16[2,128,512]{2,1,0:T(8,128)(2,1)} fusion(f32[2,512]{1,0:T(2,128)S(1)} %fusion.103, bf16[1,100,2,128]{3,1,2,0:T(8,128)(2,1)S(1)} %copy.158, bf16[1,512,2,128]{3,1,2,0:T(8,128)(2,1)} %copy.151, pred[512,612]{0,1:T(8,128)(4,1)S(1)} %iota_compare_fusion, bf16[512,2,128]{2,0,1:T(8,128)(2,1)S(1)} %pad_maximum_fusion.6, ...), kind=kOutput, calls=%fused_computation.59 | convolution fusion | flops 325697120 | bytes 1570816 | tf_op jit(solution)/shard_map/bhqk,bkhe->bqhe/dot_general | solution.py:107
  52.3 2.1 collective-permute-start.1
  54.3 2.5 copy.162
  56.8 4.8 %all-to-all-start = ((bf16[256,8,512]{0,2,1:T(8,128)(2,1)}), bf16[256,8,512]{0,2,1:T(8,128)(2,1)S(1)}, u32[]{:S(2)}, u32[]{:S(2)}) async-start(bf16[256,8,512]{0,2,1:T(8,128)(2,1)} %bitcast.130), calls=%async_computation | async-start | bytes 4194304 | tf_op jit(solution)/shard_map/all_to_all | solution.py:137
  61.6 3.2 %collective-permute-start.3 = (bf16[1024,256]{1,0:T(8,128)(2,1)}, bf16[1024,256]{1,0:T(8,128)(2,1)S(1)}, u32[]{:S(2)}, u32[]{:S(2)}) collective-permute-start(bf16[1024,256]{1,0:T(8,128)(2,1)} %bitcast.21), channel_id=1, source_target_pairs={{0,6},{2,0},{4,2},{6,4},{1,7},{3,1},{5,3},{7,5},{8,14},{10,8},{12,... | collective-permute-start | bytes 1572872 | tf_op jit(solution)/shard_map/ppermute | solution.py:26
  64.8 2.2 bitcast_convert_fusion
  67.0 3.1 %collective-permute-done.1 = bf16[1024,256]{1,0:T(8,128)(2,1)} collective-permute-done((bf16[1024,256]{1,0:T(8,128)(2,1)}, bf16[1024,256]{1,0:T(8,128)(2,1)}, u32[]{:S(2)}, u32[]{:S(2)}) %collective-permute-start.1) | collective-permute-done | bytes 524320 | tf_op jit(solution)/shard_map/ppermute | solution.py:26
  74.9 23.7 %collective-permute-done.3 = bf16[1024,256]{1,0:T(8,128)(2,1)S(1)} collective-permute-done((bf16[1024,256]{1,0:T(8,128)(2,1)}, bf16[1024,256]{1,0:T(8,128)(2,1)S(1)}, u32[]{:S(2)}, u32[]{:S(2)}) %collective-permute-start.3) | collective-permute-done | bytes 524320 | tf_op jit(solution)/shard_map/ppermute | solution.py:26
  105.1 2.0 constant_dynamic-update-slice_fusion.6
  118.8 2.9 %copy.163 = bf16[8,256,1,512]{3,1,0,2:T(8,128)(2,1)S(1)} copy(bf16[8,256,1,512]{1,3,0,2:T(8,128)(2,1)} %bitcast.129) | data formatting | bytes 4194304 | tf_op jit(solution)/shard_map/all_to_all | solution.py:137
  123.3 5.9 %constant_dynamic-update-slice_fusion.15 = (bf16[1024,4096]{0,1:T(8,128)(2,1)}, bf16[1024,512]{0,1:T(8,128)(2,1)}) fusion(f32[512]{0:T(512)S(1)} %get-tuple-element.45, f32[1024,512]{0,1:T(8,128)S(1)} %bitcast.132, bf16[1024,2048]{1,0:T(8,128)(2,1)} %constant_dynamic-update-slice_fusion, bf16[2048,512]{1,0:T(8,128)(2,1)S(1)} %dynamic-slice_dynamic-update-slice_fusion), kind=kOutput, calls=%fused_computation.122 | convolution fusion | flops 2149056512 | bytes 10487808 | tf_op jit(solution)/shard_map/dot_general | solution.py:161
  129.8 2.7 %collective-permute-start.11 = (bf16[1024,512]{0,1:T(8,128)(2,1)}, bf16[1024,512]{0,1:T(8,128)(2,1)S(1)}, u32[]{:S(2)}, u32[]{:S(2)}) collective-permute-start(bf16[1024,512]{0,1:T(8,128)(2,1)} %get-tuple-element.74), channel_id=1, source_target_pairs={{0,6},{2,0},{4,2},{6,4},{1,7},{3,1},{5,3},{7,5},{8,14},{10,8},{12,... | collective-permute-start | bytes 3145736 | tf_op jit(solution)/shard_map/ppermute | solution.py:26
  133.7 22.0 %collective-permute-done.9 = bf16[1024,512]{0,1:T(8,128)(2,1)S(1)} collective-permute-done((bf16[1024,512]{0,1:T(8,128)(2,1)}, bf16[1024,512]{0,1:T(8,128)(2,1)S(1)}, u32[]{:S(2)}, u32[]{:S(2)}) %collective-permute-start.9) | collective-permute-done | bytes 1048608 | tf_op jit(solution)/shard_map/ppermute | solution.py:26
  157.4 3.2 %collective-permute-start.14 = (bf16[512,512]{0,1:T(8,128)(2,1)}, bf16[512,512]{0,1:T(8,128)(2,1)S(1)}, u32[]{:S(2)}, u32[]{:S(2)}) collective-permute-start(bf16[512,512]{0,1:T(8,128)(2,1)} %slice.148), channel_id=1, source_target_pairs={{0,6},{2,0},{4,2},{6,4},{1,7},{3,1},{5,3},{7,5},{8,14},{10,8},{12,... | collective-permute-start | bytes 1572872 | tf_op jit(solution)/shard_map/ppermute | solution.py:26
  161.2 9.8 %collective-permute-done.13 = bf16[512,512]{0,1:T(8,128)(2,1)S(1)} collective-permute-done((bf16[512,512]{0,1:T(8,128)(2,1)}, bf16[512,512]{0,1:T(8,128)(2,1)S(1)}, u32[]{:S(2)}, u32[]{:S(2)}) %collective-permute-start.13) | collective-permute-done | bytes 524320 | tf_op jit(solution)/shard_map/ppermute | solution.py:26
  171.4 2.3 constant_dynamic-update-slice_fusion.14
  174.8 2.3 constant_dynamic-update-slice_fusion.12
  178.1 2.3 constant_dynamic-update-slice_fusion.10
  183.2 5.6 %multiply_reduce_fusion = f32[1024]{0:T(1024)S(1)} fusion(bf16[1024,4096]{0,1:T(8,128)(2,1)} %constant_dynamic-update-slice_fusion.8, f32[4096]{0:T(1024)S(1)} %constant_dynamic-update-slice_fusion.23), kind=kLoop, calls=%fused_computation.2 | loop fusion | flops 16776192 | bytes 8409088 | tf_op jit(solution)/shard_map/reduce_sum | solution.py:172
  188.9 8.4 %fusion.10 = f32[1024,512]{0,1:T(8,128)S(1)} fusion(bf16[1024,4096]{0,1:T(8,128)(2,1)} %constant_dynamic-update-slice_fusion.8, bf16[16384,512]{1,0:T(8,128)(2,1)} %all-gather.4.cloned.1.call-done), kind=kOutput, calls=%fused_computation.12 | convolution fusion | flops 4294967296 | bytes 14680064 | tf_op jit(solution)/shard_map/dot_general | solution.py:179
  197.3 8.4 %fusion.12 = f32[1024,512]{0,1:T(8,128)S(1)} fusion(bf16[1024,4096]{0,1:T(8,128)(2,1)} %constant_dynamic-update-slice_fusion.8, bf16[16384,512]{1,0:T(8,128)(2,1)} %all-gather.4.cloned.1.call-done), kind=kOutput, calls=%fused_computation.14 | convolution fusion | flops 4294967296 | bytes 14680064 | tf_op jit(solution)/shard_map/dot_general | solution.py:179
  205.7 6.5 %fusion.8 = f32[1024,512]{0,1:T(8,128)S(1)} fusion(bf16[1024,4096]{0,1:T(8,128)(2,1)S(1)} %bitcast.128, bf16[16384,512]{1,0:T(8,128)(2,1)} %all-gather.4.cloned.1.call-done), kind=kOutput, calls=%fused_computation.10 | convolution fusion | flops 4294967296 | bytes 14680064 | tf_op jit(solution)/shard_map/dot_general | solution.py:179
  212.2 6.9 %multiply_reduce_fusion.4 = (f32[1024]{0:T(1024)S(1)}, f32[1024]{0:T(1024)S(1)}, f32[1024]{0:T(1024)S(1)}, f32[1024]{0:T(1024)S(1)}, f32[1024,512]{0,1:T(8,128)S(1)}) fusion(f32[1024]{0:T(1024)S(1)} %add_rsqrt_fusion.1, f32[1024,512]{0,1:T(8,128)S(1)} %fusion.12, f32[1024,512]{0,1:T(8,128)S(1)} %fusion.10, f32[1024,512]{0,1:T(8,128)S(1)} %fusion.8, ...), kind=kOutput, calls=%fused_computation.47 | convolution fusion | flops 4299157504 | bytes 20992000 | tf_op jit(solution)/shard_map/dot_general | solution.py:179
  219.1 3.1 %exponential_reduce_fusion = (f32[1024]{0:T(1024)S(1)}, f32[1024]{0:T(1024)S(1)}, f32[1024]{0:T(1024)S(1)}, f32[1024]{0:T(1024)S(1)}, f32[1024]{0:T(1024)S(1)}, ...) fusion(f32[1024,512]{0,1:T(8,128)S(1)} %fusion.8, f32[1024]{0:T(1024)S(1)} %get-tuple-element.41, ...), kind=kLoop, calls=%fused_computation.37 | loop fusion | flops 12574720 | bytes 8454144 | tf_op jit(solution)/shard_map/reduce_sum | solution.py:182
  222.3 13.6 %all-gather.1 = f32[8,2,1024]{2,1,0:T(2,128)S(1)} all-gather(f32[1,2,1024]{2,1,0:T(2,128)S(1)} %maximum_bitcast_fusion.14), channel_id=2, replica_groups=mesh['prompt'=4,'dp'=4,'mp_0'=4,'mp_1'=2] {'mp_0','mp_1'}, dimensions={0}, use_global_device_ids=true | all-gather | bytes 73728 | tf_op jit(solution)/shard_map/all_gather | solution.py:192
  236.8 14.4 %all_to_all.21 = f32[16,1,9]{2,1,0:T(1,128)S(1)} all-to-all(f32[16,1,9]{2,1,0:T(1,128)S(1)} %broadcast_in_dim.55), channel_id=1, replica_groups=mesh['prompt'=4,'dp'=4,'mp_0'=4,'mp_1'=2] {'prompt','dp'}, dimensions={0} | all-to-all | bytes 1152 | tf_op jit(solution)/shard_map/all_to_all | solution.py:20
  (162 shorter events, 56.5 us)
Async XLA Ops:
  7.2 153.5 %copy-start = (s32[1,512]{1,0:T(1,128)S(1)}, s32[1,512]{1,0:T(1,128)}, u32[]{:S(2)}) copy-start(s32[1,512]{1,0:T(1,128)} %param.12) | copy-start | bytes 6148
  7.2 181.7 %all-gather.4.cloned.1.call-start = ((), (), s32[]{:S(2)}) async-start(), calls=%async_computation.2 | async-start | bytes 17825792 | tf_op jit(solution)/shard_map/all_gather | solution.py:134
  11.6 3.3 %copy-start.11 = (f32[4096]{0:T(1024)S(1)}, f32[4096]{0:T(1024)}, u32[]{:S(2)}) copy-start(f32[4096]{0:T(1024)} %param.14) | copy-start | bytes 49156
  11.6 3.5 %copy-start.4 = (bf16[1,512,4096]{2,1,0:T(8,128)(2,1)S(1)}, bf16[1,512,4096]{2,1,0:T(8,128)(2,1)}, u32[]{:S(2)}) copy-start(bf16[1,512,4096]{2,1,0:T(8,128)(2,1)} %param.11) | copy-start | bytes 12582916
  21.3 6.1 %copy-start.3 = (bf16[2,100,4096]{2,0,1:T(2,128)(2,1)S(1)}, bf16[2,100,4096]{2,0,1:T(2,128)(2,1)}, u32[]{:S(2)}) copy-start(bf16[2,100,4096]{2,0,1:T(2,128)(2,1)} %param.10) | copy-start | bytes 4915204
  38.6 2.8 %copy-start.5 = (f32[1,512,2,64]{3,1,2,0:T(8,128)S(1)}, f32[1,512,2,64]{3,1,2,0:T(8,128)}, u32[]{:S(2)}) copy-start(f32[1,512,2,64]{3,1,2,0:T(8,128)} %copy.173) | copy-start | bytes 786436
  46.9 7.4 %copy-start.6 = (bf16[256,4096]{1,0:T(8,128)(2,1)S(1)}, bf16[256,4096]{1,0:T(8,128)(2,1)}, u32[]{:S(2)}) copy-start(bf16[256,4096]{1,0:T(8,128)(2,1)} %param.16) | copy-start | bytes 6291460
  52.3 17.8 %collective-permute-start.1 = (bf16[1024,256]{1,0:T(8,128)(2,1)}, bf16[1024,256]{1,0:T(8,128)(2,1)}, u32[]{:S(2)}, u32[]{:S(2)}) collective-permute-start(bf16[1024,256]{1,0:T(8,128)(2,1)} %bitcast.21), channel_id=1, source_target_pairs={{0,2},{2,4},{4,6},{6,0},{1,3},{3,5},{5,7},{7,1},{8,10},{10,12},{12... | collective-permute-start | bytes 1572872 | tf_op jit(solution)/shard_map/ppermute | solution.py:26
  56.8 60.6 %all-to-all-start = ((bf16[256,8,512]{0,2,1:T(8,128)(2,1)}), bf16[256,8,512]{0,2,1:T(8,128)(2,1)S(1)}, u32[]{:S(2)}, u32[]{:S(2)}) async-start(bf16[256,8,512]{0,2,1:T(8,128)(2,1)} %bitcast.130), calls=%async_computation | async-start | bytes 4194304 | tf_op jit(solution)/shard_map/all_to_all | solution.py:137
  61.6 39.3 %copy-start.12 = (f32[4096]{0:T(1024)S(1)}, f32[4096]{0:T(1024)}, u32[]{:S(2)}) copy-start(f32[4096]{0:T(1024)} %param.17) | copy-start | bytes 49156
  61.6 37.0 %collective-permute-start.3 = (bf16[1024,256]{1,0:T(8,128)(2,1)}, bf16[1024,256]{1,0:T(8,128)(2,1)S(1)}, u32[]{:S(2)}, u32[]{:S(2)}) collective-permute-start(bf16[1024,256]{1,0:T(8,128)(2,1)} %bitcast.21), channel_id=1, source_target_pairs={{0,6},{2,0},{4,2},{6,4},{1,7},{3,1},{5,3},{7,5},{8,14},{10,8},{12,... | collective-permute-start | bytes 1572872 | tf_op jit(solution)/shard_map/ppermute | solution.py:26
  64.8 40.2 %collective-permute-start = (bf16[1024,256]{1,0:T(8,128)(2,1)}, bf16[1024,256]{1,0:T(8,128)(2,1)}, u32[]{:S(2)}, u32[]{:S(2)}) collective-permute-start(bf16[1024,256]{1,0:T(8,128)(2,1)} %bitcast.21), channel_id=1, source_target_pairs={{0,1},{1,0},{2,3},{3,2},{4,5},{5,4},{6,7},{7,6},{8,9},{9,8},{10,11... | collective-permute-start | bytes 1572872 | tf_op jit(solution)/shard_map/ppermute | solution.py:26
  70.1 40.4 %collective-permute-start.2 = (bf16[1024,256]{1,0:T(8,128)(2,1)}, bf16[1024,256]{1,0:T(8,128)(2,1)}, u32[]{:S(2)}, u32[]{:S(2)}) collective-permute-start(bf16[1024,256]{1,0:T(8,128)(2,1)} %collective-permute-done.1), channel_id=1, source_target_pairs={{0,1},{1,0},{2,3},{3,2},{4,5},{5,4},{6,7},{7,6},{8,9},{9,8},{10,11... | collective-permute-start | bytes 1572872 | tf_op jit(solution)/shard_map/ppermute | solution.py:26
  73.7 35.2 %collective-permute-start.5 = (bf16[512,256]{1,0:T(8,128)(2,1)}, bf16[512,256]{1,0:T(8,128)(2,1)S(1)}, u32[]{:S(2)}, u32[]{:S(2)}) collective-permute-start(bf16[512,256]{1,0:T(8,128)(2,1)} %slice.145), channel_id=1, source_target_pairs={{0,2},{2,4},{4,6},{6,0},{1,3},{3,5},{5,7},{7,1},{8,10},{10,12},{12... | collective-permute-start | bytes 786440 | tf_op jit(solution)/shard_map/ppermute | solution.py:26
  98.6 2.4 copy-start.8
  99.3 9.6 %collective-permute-start.6 = (bf16[512,256]{1,0:T(8,128)(2,1)}, bf16[512,256]{1,0:T(8,128)(2,1)}, u32[]{:S(2)}, u32[]{:S(2)}) collective-permute-start(bf16[512,256]{1,0:T(8,128)(2,1)} %slice.146), channel_id=1, source_target_pairs={{0,6},{2,0},{4,2},{6,4},{1,7},{3,1},{5,3},{7,5},{8,14},{10,8},{12,... | collective-permute-start | bytes 786440 | tf_op jit(solution)/shard_map/ppermute | solution.py:26
  103.3 1.8 copy-start.9
  105.0 8.2 %collective-permute-start.4 = (bf16[1024,256]{1,0:T(8,128)(2,1)S(1)}, bf16[1024,256]{1,0:T(8,128)(2,1)S(1)}, u32[]{:S(2)}, u32[]{:S(2)}) collective-permute-start(bf16[1024,256]{1,0:T(8,128)(2,1)S(1)} %copy-done.9), channel_id=1, source_target_pairs={{0,1},{1,0},{2,3},{3,2},{4,5},{5,4},{6,7},{7,6},{8,9},{9,8},{10,11... | collective-permute-start | bytes 1572872 | tf_op jit(solution)/shard_map/ppermute | solution.py:26
  109.9 6.7 %collective-permute-start.7 = (bf16[1024,256]{1,0:T(8,128)(2,1)S(1)}, bf16[1024,256]{1,0:T(8,128)(2,1)S(1)}, u32[]{:S(2)}, u32[]{:S(2)}) collective-permute-start(bf16[1024,256]{1,0:T(8,128)(2,1)S(1)} %pad_maximum_fusion.3), channel_id=1, source_target_pairs={{0,1},{1,0},{2,3},{3,2},{4,5},{5,4},{6,7},{7,6},{8,9},{9,8},{10,11... | collective-permute-start | bytes 1572872 | tf_op jit(solution)/shard_map/ppermute | solution.py:26
  117.5 1.4 copy-start.2
  121.7 1.6 copy-start.7
  129.2 26.5 %collective-permute-start.9 = (bf16[1024,512]{0,1:T(8,128)(2,1)}, bf16[1024,512]{0,1:T(8,128)(2,1)S(1)}, u32[]{:S(2)}, u32[]{:S(2)}) collective-permute-start(bf16[1024,512]{0,1:T(8,128)(2,1)} %get-tuple-element.74), channel_id=1, source_target_pairs={{0,2},{2,4},{4,6},{6,0},{1,3},{3,5},{5,7},{7,1},{8,10},{10,12},{12... | collective-permute-start | bytes 3145736 | tf_op jit(solution)/shard_map/ppermute | solution.py:26
  129.8 26.8 %collective-permute-start.11 = (bf16[1024,512]{0,1:T(8,128)(2,1)}, bf16[1024,512]{0,1:T(8,128)(2,1)S(1)}, u32[]{:S(2)}, u32[]{:S(2)}) collective-permute-start(bf16[1024,512]{0,1:T(8,128)(2,1)} %get-tuple-element.74), channel_id=1, source_target_pairs={{0,6},{2,0},{4,2},{6,4},{1,7},{3,1},{5,3},{7,5},{8,14},{10,8},{12,... | collective-permute-start | bytes 3145736 | tf_op jit(solution)/shard_map/ppermute | solution.py:26
  132.8 38.7 %collective-permute-start.8 = (bf16[1024,512]{0,1:T(8,128)(2,1)}, bf16[1024,512]{0,1:T(8,128)(2,1)}, u32[]{:S(2)}, u32[]{:S(2)}) collective-permute-start(bf16[1024,512]{0,1:T(8,128)(2,1)} %get-tuple-element.74), channel_id=1, source_target_pairs={{0,1},{1,0},{2,3},{3,2},{4,5},{5,4},{6,7},{7,6},{8,9},{9,8},{10,11... | collective-permute-start | bytes 3145736 | tf_op jit(solution)/shard_map/ppermute | solution.py:26
  156.5 14.4 %collective-permute-start.13 = (bf16[512,512]{0,1:T(8,128)(2,1)}, bf16[512,512]{0,1:T(8,128)(2,1)S(1)}, u32[]{:S(2)}, u32[]{:S(2)}) collective-permute-start(bf16[512,512]{0,1:T(8,128)(2,1)} %slice.147), channel_id=1, source_target_pairs={{0,2},{2,4},{4,6},{6,0},{1,3},{3,5},{5,7},{7,1},{8,10},{10,12},{12... | collective-permute-start | bytes 1572872 | tf_op jit(solution)/shard_map/ppermute | solution.py:26
  157.4 13.8 %collective-permute-start.14 = (bf16[512,512]{0,1:T(8,128)(2,1)}, bf16[512,512]{0,1:T(8,128)(2,1)S(1)}, u32[]{:S(2)}, u32[]{:S(2)}) collective-permute-start(bf16[512,512]{0,1:T(8,128)(2,1)} %slice.148), channel_id=1, source_target_pairs={{0,6},{2,0},{4,2},{6,4},{1,7},{3,1},{5,3},{7,5},{8,14},{10,8},{12,... | collective-permute-start | bytes 1572872 | tf_op jit(solution)/shard_map/ppermute | solution.py:26
  160.6 14.2 %collective-permute-start.10 = (bf16[1024,512]{0,1:T(8,128)(2,1)S(1)}, bf16[1024,512]{0,1:T(8,128)(2,1)}, u32[]{:S(2)}, u32[]{:S(2)}) collective-permute-start(bf16[1024,512]{0,1:T(8,128)(2,1)S(1)} %collective-permute-done.9), channel_id=1, source_target_pairs={{0,1},{1,0},{2,3},{3,2},{4,5},{5,4},{6,7},{7,6},{8,9},{9,8},{10,11... | collective-permute-start | bytes 3145736 | tf_op jit(solution)/shard_map/ppermute | solution.py:26
  160.6 17.5 %collective-permute-start.12 = (bf16[1024,512]{0,1:T(8,128)(2,1)S(1)}, bf16[1024,512]{0,1:T(8,128)(2,1)}, u32[]{:S(2)}, u32[]{:S(2)}) collective-permute-start(bf16[1024,512]{0,1:T(8,128)(2,1)S(1)} %collective-permute-done.11), channel_id=1, source_target_pairs={{0,1},{1,0},{2,3},{3,2},{4,5},{5,4},{6,7},{7,6},{8,9},{9,8},{10,11... | collective-permute-start | bytes 3145736 | tf_op jit(solution)/shard_map/ppermute | solution.py:26
  171.3 10.9 %collective-permute-start.15 = (bf16[1024,512]{0,1:T(8,128)(2,1)S(1)}, bf16[1024,512]{0,1:T(8,128)(2,1)S(1)}, u32[]{:S(2)}, u32[]{:S(2)}) collective-permute-start(bf16[1024,512]{0,1:T(8,128)(2,1)S(1)} %pad_maximum_fusion), channel_id=1, source_target_pairs={{0,1},{1,0},{2,3},{3,2},{4,5},{5,4},{6,7},{7,6},{8,9},{9,8},{10,11... | collective-permute-start | bytes 3145736 | tf_op jit(solution)/shard_map/ppermute | solution.py:26
  188.9 16.8 %slice-start = ((s8[8388608]{0:T(1024)(128)(4,1)}), s8[4194304]{0:T(1024)(128)(4,1)S(1)}, s32[]{:S(2)}) async-start(s8[8388608]{0:T(1024)(128)(4,1)} %bitcast.127), calls=%async_computation.3 | async-start | bytes 8388608
  197.3 8.4 %slice-start.1 = ((s8[8388608]{0:T(1024)(128)(4,1)}), s8[4194304]{0:T(1024)(128)(4,1)S(1)}, s32[]{:S(2)}) async-start(s8[8388608]{0:T(1024)(128)(4,1)} %bitcast.127), calls=%async_computation.4 | async-start | bytes 8388608
  219.1 34.0 %copy-start.1 = (s32[1,512]{1,0:T(1,128)S(1)}, s32[1,512]{1,0:T(1,128)}, u32[]{:S(2)}) copy-start(s32[1,512]{1,0:T(1,128)} %param.12) | copy-start | bytes 6148
  (1 other events, 1.2 us)
Sparse Core Ops, SparseCore 0:
  11.7 113.6 all-gather.3

commit v2 on v1

v2 whole, which is shorter than its diff:
```python
import math

import jax
import jax.numpy as jnp
from jax import lax
from jax.experimental import pallas as pl
from jax.experimental.pallas import tpu as pltpu
from jax.sharding import Mesh
from jax.sharding import PartitionSpec as P

HD = 128
MP = ("mp_0", "mp_1")
RING = (0, 3, 1, 2)
EPSILON = 1e-05
BASE_THETA = 10000.0
MASKED = -1e30
VMEM_LIMIT = 56 << 20
CHUNKS = (384, 128)


def of_everyone(value, axis):
    copies = jnp.broadcast_to(value, (lax.axis_size(axis), *value.shape))
    everything = lax.all_to_all(copies, axis, split_axis=0, concat_axis=0, tiled=True)
    return jnp.sum(everything, axis=0)


def shifted(value, axis, shift):
    n = lax.axis_size(axis)
    return lax.ppermute(value, axis, [(i, (i + shift) % n) for i in range(n)])


def whole_row(left, right):
    ring = "mp_0"
    left_before = shifted(left, ring, 1)
    right_after = shifted(right, ring, -1)
    right_before = shifted(right, ring, 1)
    left_after = shifted(left, ring, -1)
    left_far = shifted(left_before, ring, 1)
    right_far = shifted(right_after, ring, -1)
    pairs = [
        (left, right),
        (left_before, right_before),
        (left_after, right_after),
        (left_far, right_far),
    ]
    return [b for pair in pairs for b in (*pair, *(shifted(half, "mp_1", 1) for half in pair))]


def rope_tables(number_rows, offset):
    positions = (offset + jnp.arange(number_rows, dtype=jnp.int32)).astype(jnp.float32)
    indices_f = jnp.arange(HD // 2, dtype=jnp.int32).astype(jnp.float32)
    frequency = jnp.exp(indices_f * (-2.0 * math.log(BASE_THETA) / HD))
    angles = positions[:, None] * frequency[None, :]
    cosine, sine = jnp.cos(angles), jnp.sin(angles)
    return jnp.concatenate([cosine, cosine], axis=1), jnp.concatenate([-sine, sine], axis=1)


def attention_kernel(
    target_ref, prompt_ref, gain_ref, w_ref, cos_t, sin_t, cos_p, sin_p, left_ref, right_ref,
    acc_t, acc_p, sq_t, sq_p, q_s, k_s, v_s, kp_s, vp_s,
):
    step = pl.program_id(0)
    n_prompts = prompt_ref.shape[0]

    @pl.when(step == 0)
    def _():
        acc_t[...] = jnp.zeros_like(acc_t)
        acc_p[...] = jnp.zeros_like(acc_p)
        sq_t[...] = jnp.zeros_like(sq_t)
        sq_p[...] = jnp.zeros_like(sq_p)

    gain = gain_ref[...]

    def lanes_of_squares(x):
        square = x * x
        return sum(square[:, i : i + 128] for i in range(0, square.shape[1], 128))

    x = target_ref[0].astype(jnp.float32)
    sq_t[...] += lanes_of_squares(x)
    scaled = (x * gain).astype(jnp.bfloat16)
    for c in range(3):
        acc_t[c] += jnp.dot(scaled, w_ref[c], preferred_element_type=jnp.float32)
    for p in range(n_prompts):
        x = prompt_ref[p].astype(jnp.float32)
        sq_p[p] += lanes_of_squares(x)
        scaled = (x * gain).astype(jnp.bfloat16)
        for c in range(2):
            acc_p[p, c] += jnp.dot(scaled, w_ref[c + 1], preferred_element_type=jnp.float32)

    @pl.when(step == pl.num_programs(0) - 1)
    def _():
        width = pl.num_programs(0) * target_ref.shape[2]
        heads = q_s.shape[1] // HD

        def inverse(square):
            return lax.rsqrt(jnp.sum(square, axis=1, keepdims=True) / width + EPSILON)

        def turned(values, cos, sin):
            return values * cos + pltpu.roll(values, HD // 2, 1) * sin

        scale_t = inverse(sq_t[...])
        for h in range(heads):
            at = slice(h * HD, (h + 1) * HD)
            q_s[:, at] = turned(acc_t[0, :, at] * scale_t, cos_t[...], sin_t[...]).astype(jnp.bfloat16)
            k_s[:, at] = turned(acc_t[1, :, at] * scale_t, cos_t[...], sin_t[...]).astype(jnp.bfloat16)
            v_s[:, at] = (acc_t[2, :, at] * scale_t).astype(jnp.bfloat16)
            for p in range(n_prompts):
                scale_p = inverse(sq_p[p])
                kp_s[p, :, at] = turned(
                    acc_p[p, 0, :, at] * scale_p, cos_p[...], sin_p[...]
                ).astype(jnp.bfloat16)
                vp_s[p, :, at] = (acc_p[p, 1, :, at] * scale_p).astype(jnp.bfloat16)
        target_len = q_s.shape[0]
        tile = target_len // 2
        transposed = (((1,), (1,)), ((), ()))
        for p in range(n_prompts):
            for h in range(heads):
                at = slice(h * HD, (h + 1) * HD)
                for first in range(0, target_len, tile):
                    seen = first + tile
                    q = q_s[first:seen, at]
                    near = lax.dot_general(
                        q, kp_s[p, :, at], transposed, preferred_element_type=jnp.float32
                    ) * HD ** (-0.5)
                    own = lax.dot_general(
                        q, k_s[:seen, at], transposed, preferred_element_type=jnp.float32
                    ) * HD ** (-0.5)
                    row = first + lax.broadcasted_iota(jnp.int32, own.shape, 0)
                    key = lax.broadcasted_iota(jnp.int32, own.shape, 1)
                    own = jnp.where(key <= row, own, MASKED)
                    top = jnp.maximum(
                        jnp.max(near, axis=1, keepdims=True), jnp.max(own, axis=1, keepdims=True)
                    )
                    near = jnp.exp(near - top)
                    own = jnp.exp(own - top)
                    norm = 1.0 / (
                        jnp.sum(near, axis=1, keepdims=True) + jnp.sum(own, axis=1, keepdims=True)
                    )
                    context = jnp.dot(
                        (near * norm).astype(jnp.bfloat16),
                        vp_s[p, :, at],
                        preferred_element_type=jnp.float32,
                    ) + jnp.dot(
                        (own * norm).astype(jnp.bfloat16),
                        v_s[:seen, at],
                        preferred_element_type=jnp.float32,
                    )
                    out_ref = (left_ref, right_ref)[h]
                    out_ref[p * target_len + first : p * target_len + seen, :] = context.astype(
                        jnp.bfloat16
                    )


def attention(target_embed, prompts, attn_gain, w_qkv):
    n_prompts, prompt_len, width = prompts.shape
    target_len = target_embed.shape[1]
    inner = w_qkv.shape[2]
    chunk = 512
    tables = (*rope_tables(target_len, prompt_len), *rope_tables(prompt_len, 0))
    whole = lambda shape: pl.BlockSpec(shape, lambda k: (0,) * len(shape))
    rows = n_prompts * target_len
    return pl.pallas_call(
        attention_kernel,
        out_shape=[jax.ShapeDtypeStruct((rows, inner // 2), jnp.bfloat16)] * 2,
        grid=(width // chunk,),
        in_specs=[
            pl.BlockSpec((1, target_len, chunk), lambda k: (0, 0, k)),
            pl.BlockSpec((n_prompts, prompt_len, chunk), lambda k: (0, 0, k)),
            pl.BlockSpec((1, chunk), lambda k: (0, k)),
            pl.BlockSpec((3, chunk, inner), lambda k: (0, k, 0)),
            *(whole(t.shape) for t in tables),
        ],
        out_specs=[whole((rows, inner // 2))] * 2,
        scratch_shapes=[
            pltpu.VMEM((3, target_len, inner), jnp.float32),
            pltpu.VMEM((n_prompts, 2, prompt_len, inner), jnp.float32),
            pltpu.VMEM((target_len, 128), jnp.float32),
            pltpu.VMEM((n_prompts, prompt_len, 128), jnp.float32),
            *(pltpu.VMEM((target_len, inner), jnp.bfloat16) for _ in range(3)),
            *(pltpu.VMEM((n_prompts, prompt_len, inner), jnp.bfloat16) for _ in range(2)),
        ],
        compiler_params=pltpu.CompilerParams(vmem_limit_bytes=VMEM_LIMIT),
        cost_estimate=pl.CostEstimate(
            flops=8 * 10**9, bytes_accessed=12 * 10**6, transcendentals=2 * 10**6
        ),
        name="attention",
    )(target_embed, prompts, attn_gain.reshape(1, -1), w_qkv, *tables)


def output_kernel(places_ref, *refs):
    *ctx_refs, w_ref, embed_ref, gain_ref, left_ref, right_ref, ctx_s, w_s = refs
    width = w_ref.shape[1]
    at = 0
    for ref in ctx_refs:
        ctx_s[:, at : at + ref.shape[1]] = ref[...]
        at += ref.shape[1]

    @pl.when(pl.program_id(0) == 0)
    def _():
        for group in range(w_ref.shape[0]):
            w_s[group * width : (group + 1) * width, :] = w_ref[places_ref[group]]

    total = embed_ref[0].astype(jnp.float32) + jnp.dot(
        ctx_s[...], w_s[...], preferred_element_type=jnp.float32
    )
    scaled = (total * gain_ref[...]).astype(jnp.bfloat16)
    half = scaled.shape[1] // 2
    left_ref[...] = scaled[:, :half]
    right_ref[...] = scaled[:, half:]


def output_part(places, contexts, out_cols, target_embed, final_gain):
    rows = contexts[0].shape[0]
    groups, group_width, part = out_cols.shape
    target_len = target_embed.shape[1]
    return pl.pallas_call(
        output_kernel,
        out_shape=[jax.ShapeDtypeStruct((rows, part // 2), jnp.bfloat16)] * 2,
        grid_spec=pltpu.PrefetchScalarGridSpec(
            num_scalar_prefetch=1,
            grid=(rows // target_len,),
            in_specs=[
                *(pl.BlockSpec((target_len, c.shape[1]), lambda i, at: (i, 0)) for c in contexts),
                pl.BlockSpec(out_cols.shape, lambda i, at: (0, 0, 0)),
                pl.BlockSpec((1, target_len, part), lambda i, at: (0, 0, at[0])),
                pl.BlockSpec((1, part), lambda i, at: (0, at[0])),
            ],
            out_specs=[pl.BlockSpec((target_len, part // 2), lambda i, at: (i, 0))] * 2,
            scratch_shapes=[
                pltpu.VMEM((target_len, groups * group_width), jnp.bfloat16),
                pltpu.VMEM((groups * group_width, part), jnp.bfloat16),
            ],
        ),
        compiler_params=pltpu.CompilerParams(vmem_limit_bytes=VMEM_LIMIT),
        cost_estimate=pl.CostEstimate(
            flops=2 * 10**9, bytes_accessed=8 * 10**6, transcendentals=0
        ),
        name="output_part",
    )(places, *contexts, out_cols, target_embed, final_gain.reshape(1, -1))


def vocab_kernel(first_ref, *refs, n_rows, at_column, per_vocab, last):
    row_refs, refs = refs[:n_rows], refs[n_rows:]
    if at_column:
        prior_ref, refs = refs[0], refs[1:]
    degain_ref, label_ref, w_ref, out_ref, rows_s, top_s, sum_s, pick_s, scale_s = refs
    step, tile_id = pl.program_id(0), pl.program_id(1)
    tile = rows_s.shape[0]
    at = pl.ds(pl.multiple_of(tile_id * tile, tile), tile)
    blocks, _, columns = w_ref.shape

    k = 0
    for ref in row_refs:
        rows_s[:, k : k + ref.shape[1]] = ref[...]
        k += ref.shape[1]

    @pl.when(step == 0)
    def _():
        if at_column:
            top_s[at, :] = prior_ref[at, 0:1]
            sum_s[at, :] = jnp.ones((tile, 1), jnp.float32)
            pick_s[at, :] = prior_ref[at, 1:2]
            scale_s[at, :] = prior_ref[at, 2:3]
        else:
            top_s[at, :] = jnp.full((tile, 1), MASKED, jnp.float32)
            sum_s[at, :] = jnp.zeros((tile, 1), jnp.float32)
            pick_s[at, :] = jnp.zeros((tile, 1), jnp.float32)
            squares = jnp.zeros((tile, 128), jnp.float32)
            for i in range(0, rows_s.shape[1], 128):
                x = rows_s[:, i : i + 128].astype(jnp.float32) * degain_ref[:, i : i + 128]
                squares += x * x
            mean = jnp.sum(squares, axis=1, keepdims=True) / rows_s.shape[1]
            scale_s[at, :] = lax.rsqrt(mean + EPSILON)

    weights = jnp.concatenate([w_ref[i] for i in range(blocks)], axis=1)
    logits = jnp.dot(rows_s[...], weights, preferred_element_type=jnp.float32) * scale_s[at, :]
    lane = lax.broadcasted_iota(jnp.int32, (1, blocks * columns), 1)
    column = first_ref[0] + at_column + step * blocks * per_vocab
    column = column + (lane // columns) * per_vocab + lane % columns
    old = top_s[at, :]
    top = jnp.maximum(old, jnp.max(logits, axis=1, keepdims=True))
    sum_s[at, :] = sum_s[at, :] * jnp.exp(old - top) + jnp.sum(
        jnp.exp(logits - top), axis=1, keepdims=True
    )
    pick_s[at, :] += jnp.sum(
        jnp.where(column == label_ref[at, :], logits, 0.0), axis=1, keepdims=True
    )
    top_s[at, :] = top

    @pl.when(step == pl.num_programs(0) - 1)
    def _():
        total = top_s[at, :] + jnp.log(sum_s[at, :])
        lane = lax.broadcasted_iota(jnp.int32, (tile, 128), 1)
        three = jnp.where(lane == 0, total, jnp.where(lane == 1, pick_s[at, :], scale_s[at, :]))
        if last:
            out_ref[...] = three.T[:8, :]
        else:
            out_ref[...] = three


def vocab_stats(first, row_blocks, degain, row_labels, chunk, at_column, per_vocab, prior, last):
    rows = row_blocks[0].shape[0]
    n_blocks, width, columns = chunk.shape
    together = max(1, min(n_blocks, 768 // columns))
    tile = 512
    whole = lambda a: pl.BlockSpec(a.shape, lambda j, i, f: (0, 0))
    priors = [] if prior is None else [prior]
    kernel = lambda *refs: vocab_kernel(
        *refs, n_rows=len(row_blocks), at_column=at_column, per_vocab=per_vocab, last=last
    )
    final_tile = n_blocks // together - 1
    held = lambda j, i: jnp.where(j == final_tile, i, 0)
    return pl.pallas_call(
        kernel,
        out_shape=jax.ShapeDtypeStruct((8, rows) if last else (rows, 128), jnp.float32),
        grid_spec=pltpu.PrefetchScalarGridSpec(
            num_scalar_prefetch=1,
            grid=(n_blocks // together, rows // tile),
            in_specs=[
                *(pl.BlockSpec((tile, b.shape[1]), lambda j, i, f: (i, 0)) for b in row_blocks),
                *(whole(p) for p in priors),
                whole(degain),
                whole(row_labels),
                pl.BlockSpec((together, width, columns), lambda j, i, f: (j, 0, 0)),
            ],
            out_specs=pl.BlockSpec((8, tile), lambda j, i, f: (0, held(j, i)))
            if last
            else pl.BlockSpec((tile, 128), lambda j, i, f: (held(j, i), 0)),
            scratch_shapes=[
                pltpu.VMEM((tile, width), jnp.bfloat16),
                *(pltpu.VMEM((rows, 1), jnp.float32) for _ in range(4)),
            ],
        ),
        compiler_params=pltpu.CompilerParams(vmem_limit_bytes=VMEM_LIMIT),
        cost_estimate=pl.CostEstimate(
            flops=2 * rows * width * n_blocks * columns,
            bytes_accessed=rows * width * 2 + n_blocks * width * columns * 2,
            transcendentals=rows * n_blocks * columns,
        ),
        name="vocab_stats",
    )(first, *row_blocks, *priors, degain, row_labels, chunk)


def pieces_kernel(pair_ref, w_ref, *out_refs):
    at = 0
    for ref in out_refs:
        ref[...] = w_ref[:, at : at + ref.shape[1]]
        at += ref.shape[1]


def vocab_pieces(pair, w_vocab, part):
    return pl.pallas_call(
        pieces_kernel,
        out_shape=[jax.ShapeDtypeStruct((2 * part, c), w_vocab.dtype) for c in CHUNKS],
        grid_spec=pltpu.PrefetchScalarGridSpec(
            num_scalar_prefetch=1,
            grid=(2,),
            in_specs=[pl.BlockSpec((part, w_vocab.shape[1]), lambda i, pair: (pair[i], 0))],
            out_specs=[pl.BlockSpec((part, c), lambda i, pair: (i, 0)) for c in CHUNKS],
        ),
        cost_estimate=pl.CostEstimate(flops=0, bytes_accessed=2 << 20, transcendentals=0),
        name="vocab_pieces",
    )(pair, w_vocab)


def split_kernel(w_ref, out_ref):
    part = out_ref.shape[2]
    for i in range(out_ref.shape[0]):
        out_ref[i] = w_ref[:, i * part : (i + 1) * part]


def split_columns(w, n):
    rows, columns = w.shape
    part = columns // n
    return pl.pallas_call(
        split_kernel,
        out_shape=jax.ShapeDtypeStruct((n, rows, part), w.dtype),
        grid=(2,),
        in_specs=[pl.BlockSpec((rows, columns // 2), lambda i: (0, i))],
        out_specs=pl.BlockSpec((n // 2, rows, part), lambda i: (i, 0, 0)),
        cost_estimate=pl.CostEstimate(flops=0, bytes_accessed=4 << 20, transcendentals=0),
        name="split_columns",
    )(w)


def shards(prompts, target_embed, labels, lengths, attn_gain, w_qkv, w_out, final_gain, w_vocab):
    n_prompt = lax.axis_size("prompt")
    n_dp = lax.axis_size("dp")
    n_model = lax.axis_size(MP)
    prompts_here = prompts.shape[0]
    target_len = target_embed.shape[1]
    model_width = target_embed.shape[2]
    vocab_cols = w_vocab.shape[1]
    heads_width = w_out.shape[0]
    z_index = lax.axis_index("mp_0")
    core = lax.axis_index("mp_1")
    part = model_width // n_model
    places = [((z_index + r) % 4) * 2 + (core + k) % 2 for r in RING for k in range(2)]

    x_index = lax.axis_index("prompt")
    turn = jnp.where(x_index == 0, 0, jnp.where(x_index == 1, 3, x_index - 1))
    my_pair = ((z_index + turn) % 4) * 2
    pair = jnp.stack([my_pair + core, my_pair + 1 - core]).astype(jnp.int32)
    chunks = [
        lax.all_gather(p, ("dp", "prompt"), axis=0, tiled=True).reshape(n_dp, model_width, -1)
        for p in vocab_pieces(pair, w_vocab, part)
    ]

    out_cols = lax.all_to_all(
        split_columns(w_out, n_model), MP, split_axis=0, concat_axis=0, tiled=True
    )

    halves = attention(target_embed, prompts, attn_gain, w_qkv)
    place_ids = jnp.stack(places).astype(jnp.int32)
    halves = output_part(place_ids, whole_row(*halves), out_cols, target_embed, final_gain)
    row_blocks = whole_row(*halves)

    degain = 1.0 / jnp.concatenate(
        [lax.dynamic_slice_in_dim(final_gain, p * part, part, 0) for p in places], axis=0
    ).reshape(1, -1)
    row_labels = jnp.tile(labels.reshape(-1, 1), (prompts_here, 1))
    first = (lax.axis_index(MP) * vocab_cols).astype(jnp.int32).reshape(1)
    here, at_column = None, 0
    for i, chunk in enumerate(chunks):
        here = vocab_stats(
            first, row_blocks, degain, row_labels, chunk, at_column, n_model * vocab_cols, here,
            i == len(chunks) - 1,
        )
        at_column += CHUNKS[i]
    here = here[:2]

    every = lax.all_gather(here, MP)
    top_val = jnp.max(every[:, 0], axis=0)
    log_total = top_val + jnp.log(jnp.sum(jnp.exp(every[:, 0] - top_val), axis=0))
    losses = (log_total - jnp.sum(every[:, 1], axis=0)).reshape(prompts_here, 1, target_len)
    valid = jnp.arange(target_len, dtype=jnp.int32)[None, :] < lengths[:, None]
    token_loss = jnp.where(valid[None], losses, 0.0)
    prompt_sums = jnp.sum(token_loss, axis=(1, 2))
    all_prompts = prompts_here * n_prompt
    slot_ids = lax.axis_index("prompt") * prompts_here + jnp.arange(prompts_here, dtype=jnp.int32)
    placed = jnp.sum(
        jnp.where(
            jnp.arange(all_prompts, dtype=jnp.int32)[:, None] == slot_ids[None, :],
            prompt_sums[None, :],
            0.0,
        ),
        axis=1,
    )
    valid_here = jnp.sum(lengths).astype(jnp.float32).reshape(1)
    totals = of_everyone(jnp.concatenate([placed, valid_here]), ("prompt", "dp"))
    prompt_loss = totals[:all_prompts] * float(n_prompt) / totals[all_prompts]
    return (token_loss, prompt_loss)


def solution(mesh):
    finer = Mesh(
        mesh.devices.reshape(mesh.shape["prompt"], mesh.shape["dp"], 4, 2),
        ("prompt", "dp", "mp_0", "mp_1"),
    )
    return jax.shard_map(
        shards,
        mesh=finer,
        in_specs=(
            P("prompt", None, None),
            P("dp", None, None),
            P("dp", None),
            P("dp"),
            P(),
            P(None, None, MP),
            P(MP, None),
            P(),
            P(None, ("dp", "mp_0", "mp_1")),
        ),
        out_specs=(P("prompt", "dp", None), P()),
        check_vma=False,
    )
```

time: 264 us -> 206 us (0.78); the launches traced: 260 us -> 205 us
  Pallas kernels: 0 us -> 68.4 us
  matrix products: 53.8 us -> 0 us
  local copies, waits for them, and re-layouts: 56.2 us -> 9.09 us
  other arithmetic: 26.6 us -> 6.35 us
  starting transfers between devices: 20.5 us -> 26.3 us
  waiting for transfers between devices: 58.9 us -> 54.2 us
    pallas_call x0 -> x6, Pallas kernels: none -> 68.4 us  [the longest x2 40.2 us: vocab_stats(): pl.pallas_call(kernel, out_shape=jax.ShapeDtypeStruct((8, rows) if last e...]
    dot_general x9 -> x0, matrix products: 51.5 us -> none  [the longest x4 30.2 us: shards(): jnp.dot(rows, vocab_all[d], preferred_element_type=jnp.float32)]
    unnamed x67 -> x54, local copies, waits for them, and re-layouts: 35 us -> 7.7 us
    reduce_sum x6 -> x1, other arithmetic: 13.7 us -> 0.03 us  [shards(): jnp.sum(jnp.exp(every[:, 0] - top_val), axis=0)]
    ppermute x16 -> x28, waiting for transfers between devices: 58.8 us -> 51 us  [shifted(): return lax.ppermute(value, axis, [(i, (i + shift) % n) for i in range(n)])]
    slice x11 -> x0, local copies, waits for them, and re-layouts: 6.12 us -> none  [the longest x2 2.52 us: ring_of_four(): far_low = shifted(before[:half], axis, 1)]
    ppermute x16 -> x28, starting transfers between devices: 15.7 us -> 20.8 us  [shifted(): return lax.ppermute(value, axis, [(i, (i + shift) % n) for i in range(n)])]
    convert_element_type x3 -> x2, other arithmetic: 3.16 us -> 0.01 us  [rope_tables(): (offset + jnp.arange(number_rows, dtype=jnp.int32)).astype(jnp.float32)]
  transfers between devices with their start and end apart: 18 -> 31, of which waited for: 5 -> 10; matrix products, arithmetic and copies ran while one was open for 36% -> 4% of each run, Pallas kernels for 0% -> 26%
where the time goes in v2:
time: 206 us; the launch traced here: 205 us
  Pallas kernels  68.4 us (33%)
  waiting for transfers between devices  54.2 us (26%)
  starting transfers between devices  26.3 us (13%)
  blocking collectives  25.8 us (13%)
  between operations  15.2 us (7%)
  local copies, waits for them, and re-layouts  9.09 us (4%)
  other arithmetic  6.35 us (3%)
    ppermute x28, waiting for transfers between devices, shifted(): return lax.ppermute(value, axis, [(i, (i + shift) % n) for i in range(n)])  51 us
    pallas_call x2, Pallas kernels, vocab_stats(): pl.pallas_call(kernel, out_shape=jax.ShapeDtypeStruct((8, rows) if last e...  40.2 us
    ppermute x28, starting transfers between devices, shifted(): return lax.ppermute(value, axis, [(i, (i + shift) % n) for i in range(n)])  20.8 us
    pallas_call x1, Pallas kernels, attention(): pl.pallas_call(attention_kernel, out_shape=[jax.ShapeDtypeStruct((rows, i...  14.9 us
    all_gather x1, blocking collectives, shards(): every = lax.all_gather(here, MP)  13.2 us
    all_to_all x1, blocking collectives, of_everyone(): lax.all_to_all(copies, axis, split_axis=0, concat_axis=0, tiled=True)  12.6 us
    pallas_call x1, Pallas kernels, output_part(): pl.pallas_call(output_kernel, out_shape=[jax.ShapeDtypeStruct((rows, part...  7.91 us
    unnamed x54, local copies, waits for them, and re-layouts  7.7 us
  transfers between devices with their start and end apart: 31, of which 10 were waited for; matrix products, arithmetic and copies ran while one was open for 4% of the time, Pallas kernels for 26%

profile of v2, /device:TPU:0, one launch (start us, length us, event | category | flops | bytes accessed | tf_op | source)
XLA Modules:
  0.0 205.3 jit_solution(6535271109108268585)
XLA Ops:
  7.9 2.8 %vocab_pieces.1 = (bf16[1024,384]{1,0:T(8,128)(2,1)}, bf16[1024,128]{1,0:T(8,128)(2,1)}) custom-call(s32[2]{0:T(128)} %pad_add_fusion.pair_ref, bf16[4096,512]{1,0:T(8,128)(2,1)} %w_ref.5), custom_call_target="tpu_custom_call" | custom-call | bytes 2097152 | tf_op jit(solution)/shard_map/vocab_pieces/pallas_call | solution.py:352
  11.5 2.6 %split_columns.1 = bf16[8,256,512]{2,1,0:T(8,128)(2,1)} custom-call(bf16[256,4096]{1,0:T(8,128)(2,1)} %w_ref.4), custom_call_target="tpu_custom_call" | custom-call | bytes 4194304 | tf_op jit(solution)/shard_map/split_columns/pallas_call | solution.py:375
  14.1 5.4 %all-to-all-start = ((bf16[8,256,512]{2,1,0:T(8,128)(2,1)}), bf16[8,256,512]{2,1,0:T(8,128)(2,1)S(1)}, u32[]{:S(2)}, u32[]{:S(2)}) async-start(bf16[8,256,512]{2,1,0:T(8,128)(2,1)} %split_columns.1), calls=%async_computation | async-start | bytes 4194304 | tf_op jit(solution)/shard_map/all_to_all | solution.py:409
  19.5 3.6 %copy.25.prompt_ref = bf16[2,100,4096]{2,1,0:T(8,128)(2,1)} copy(bf16[2,100,4096]{2,0,1:T(2,128)(2,1)} %param.9) | data formatting | bytes 3276800 | tf_op args[0]
  23.4 1.0 fusion
  25.2 1.0 pad_maximum_fusion
  26.2 14.9 %attention.1 = (bf16[1024,128]{1,0:T(8,128)(2,1)}, bf16[1024,128]{1,0:T(8,128)(2,1)}) custom-call(bf16[1,512,4096]{2,1,0:T(8,128)(2,1)} %refs_17_.1, bf16[2,100,4096]{2,1,0:T(8,128)(2,1)} %copy.25.prompt_ref, f32[1,4096]{1,0:T(1,128)} %bitcast.59, bf16[3,4096,256]{2,1,0:T(8,128)(2,1)} %w_ref.3, f32[512,128]{1,0:T(8,128)} %get-tuple-element.33.cos_t, ...), custom_call_target="tpu_custom_call" | custom-call | flops 8000000000 | bytes 12000000 | tf_op jit(solution)/shard_map/attention/pallas_call | solution.py:162
  41.0 2.1 %collective-permute-start.2 = (bf16[1024,128]{1,0:T(8,128)(2,1)}, bf16[1024,128]{1,0:T(8,128)(2,1)S(1)}, u32[]{:S(2)}, u32[]{:S(2)}) collective-permute-start(bf16[1024,128]{1,0:T(8,128)(2,1)} %get-tuple-element.8.refs_0_), channel_id=1, source_target_pairs={{0,2},{2,4},{4,6},{6,0},{1,3},{3,5},{5,7},{7,1},{8,10},{10,12},{12... | collective-permute-start | bytes 786440 | tf_op jit(solution)/shard_map/ppermute | solution.py:29
  43.1 1.3 collective-permute-start.7
  45.1 2.5 %collective-permute-start.6 = (bf16[1024,128]{1,0:T(8,128)(2,1)}, bf16[1024,128]{1,0:T(8,128)(2,1)S(1)}, u32[]{:S(2)}, u32[]{:S(2)}) collective-permute-start(bf16[1024,128]{1,0:T(8,128)(2,1)} %get-tuple-element.8.refs_0_), channel_id=1, source_target_pairs={{0,6},{2,0},{4,2},{6,4},{1,7},{3,1},{5,3},{7,5},{8,14},{10,8},{12,... | collective-permute-start | bytes 786440 | tf_op jit(solution)/shard_map/ppermute | solution.py:29
  47.6 4.7 %collective-permute-done.2.refs_4_ = bf16[1024,128]{1,0:T(8,128)(2,1)S(1)} collective-permute-done((bf16[1024,128]{1,0:T(8,128)(2,1)}, bf16[1024,128]{1,0:T(8,128)(2,1)S(1)}, u32[]{:S(2)}, u32[]{:S(2)}) %collective-permute-start.2) | collective-permute-done | bytes 262176 | tf_op jit(solution)/shard_map/ppermute | solution.py:29
  52.5 1.5 collective-permute-start.10
  54.0 4.0 %collective-permute-done.3.refs_5_ = bf16[1024,128]{1,0:T(8,128)(2,1)S(1)} collective-permute-done((bf16[1024,128]{1,0:T(8,128)(2,1)}, bf16[1024,128]{1,0:T(8,128)(2,1)S(1)}, u32[]{:S(2)}, u32[]{:S(2)}) %collective-permute-start.3) | collective-permute-done | bytes 262176 | tf_op jit(solution)/shard_map/ppermute | solution.py:29
  58.0 1.3 collective-permute-start.11
  60.0 3.6 %collective-permute-done.10.refs_12_ = bf16[1024,128]{1,0:T(8,128)(2,1)} collective-permute-done((bf16[1024,128]{1,0:T(8,128)(2,1)S(1)}, bf16[1024,128]{1,0:T(8,128)(2,1)}, u32[]{:S(2)}, u32[]{:S(2)}) %collective-permute-start.10) | collective-permute-done | bytes 262176 | tf_op jit(solution)/shard_map/ppermute | solution.py:29
  63.7 2.7 %collective-permute-done.11.refs_13_ = bf16[1024,128]{1,0:T(8,128)(2,1)} collective-permute-done((bf16[1024,128]{1,0:T(8,128)(2,1)S(1)}, bf16[1024,128]{1,0:T(8,128)(2,1)}, u32[]{:S(2)}, u32[]{:S(2)}) %collective-permute-start.11) | collective-permute-done | bytes 262176 | tf_op jit(solution)/shard_map/ppermute | solution.py:29
  66.9 1.0 copy.34
  69.6 1.3 copy-done.1
  70.9 7.9 %output_part.1 = (bf16[1024,256]{1,0:T(8,128)(2,1)}, bf16[1024,256]{1,0:T(8,128)(2,1)}) custom-call(s32[8]{0:T(128)} %stack.44.places_ref, bf16[1024,128]{1,0:T(8,128)(2,1)} %get-tuple-element.8.refs_0_, bf16[1024,128]{1,0:T(8,128)(2,1)} %get-tuple-element.9.refs_1_, bf16[1024,128]{1,0:T(8,128)(2,1)} %copy-done.6, ...), custom_call_target="tpu_custom_call" | custom-call | flops 2000000000 | bytes 8000000 | tf_op jit(solution)/shard_map/output_part/pallas_call | solution.py:216
  78.8 1.7 collective-permute-start.21
  80.9 3.2 %collective-permute-start.20 = (bf16[1024,256]{1,0:T(8,128)(2,1)}, bf16[1024,256]{1,0:T(8,128)(2,1)S(1)}, u32[]{:S(2)}, u32[]{:S(2)}) collective-permute-start(bf16[1024,256]{1,0:T(8,128)(2,1)} %get-tuple-element.10.refs_1_), channel_id=1, source_target_pairs={{0,6},{2,0},{4,2},{6,4},{1,7},{3,1},{5,3},{7,5},{8,14},{10,8},{12,... | collective-permute-start | bytes 1572872 | tf_op jit(solution)/shard_map/ppermute | solution.py:29
  84.3 22.5 %collective-permute-done.16.refs_5_ = bf16[1024,256]{1,0:T(8,128)(2,1)S(1)} collective-permute-done((bf16[1024,256]{1,0:T(8,128)(2,1)}, bf16[1024,256]{1,0:T(8,128)(2,1)S(1)}, u32[]{:S(2)}, u32[]{:S(2)}) %collective-permute-start.16) | collective-permute-done | bytes 524320 | tf_op jit(solution)/shard_map/ppermute | solution.py:29
  107.3 2.9 %collective-permute-start.25 = (bf16[1024,256]{1,0:T(8,128)(2,1)S(1)}, bf16[1024,256]{1,0:T(8,128)(2,1)S(1)}, u32[]{:S(2)}, u32[]{:S(2)}) collective-permute-start(bf16[1024,256]{1,0:T(8,128)(2,1)S(1)} %collective-permute-done.21.refs_10_), channel_id=1, source_target_pairs={{0,6},{2,0},{4,2},{6,4},{1,7},{3,1},{5,3},{7,5},{8,14},{10,8},{12,... | collective-permute-start | bytes 1572872 | tf_op jit(solution)/shard_map/ppermute | solution.py:29
  110.9 11.4 %collective-permute-done.24.refs_13_ = bf16[1024,256]{1,0:T(8,128)(2,1)S(1)} collective-permute-done((bf16[1024,256]{1,0:T(8,128)(2,1)S(1)}, bf16[1024,256]{1,0:T(8,128)(2,1)S(1)}, u32[]{:S(2)}, u32[]{:S(2)}) %collective-permute-start.24) | collective-permute-done | bytes 524320 | tf_op jit(solution)/shard_map/ppermute | solution.py:29
  124.2 1.5 collective-permute-done.26.refs_15_
  125.7 0.8 copy-done.20
  126.6 27.5 %vocab_stats.2.refs_17_ = f32[1024,128]{1,0:T(8,128)} custom-call(s32[1]{0:T(128)} %bitcast.1.refs_0_, bf16[1024,256]{1,0:T(8,128)(2,1)} %get-tuple-element.10.refs_1_, bf16[1024,256]{1,0:T(8,128)(2,1)} %get-tuple-element.11.refs_2_, bf16[1024,256]{1,0:T(8,128)(2,1)} %copy-done.12, bf16[1024,256]{1,0:T(8,128)(2,1)} %copy-done.13, ...), custom_call_target="tpu_custom_call" | custom-call | flops 12884901888 | bytes 20971520 | tf_op jit(solution)/shard_map/vocab_stats/pallas_call | solution.py:313
  154.1 2.4 %all-gather.7.cloned.1.call-done = bf16[16384,128]{1,0:T(8,128)(2,1)} async-done(((bf16[1024,128]{1,0:T(8,128)(2,1)}), bf16[16384,128]{1,0:T(8,128)(2,1)}) %all-gather.7.cloned.1.call-update) | async-done | bytes 4194320 | tf_op jit(solution)/shard_map/all_gather | solution.py:405
  156.5 12.7 %vocab_stats.3 = f32[8,1024]{1,0:T(8,128)} custom-call(s32[1]{0:T(128)} %bitcast.1.refs_0_, bf16[1024,256]{1,0:T(8,128)(2,1)} %get-tuple-element.10.refs_1_, bf16[1024,256]{1,0:T(8,128)(2,1)} %get-tuple-element.11.refs_2_, bf16[1024,256]{1,0:T(8,128)(2,1)} %copy-done.12, bf16[1024,256]{1,0:T(8,128)(2,1)} %copy-done.13, bf16[1024,256]{1,0:T(8,128)(2,1)} %copy-done.10, ...), custom_call_target="tpu_custom_call" | custom-call | flops 4294967296 | bytes 12582912 | tf_op jit(solution)/shard_map/vocab_stats/pallas_call | solution.py:313
  169.9 13.2 %all-gather.1 = f32[8,2,1024]{2,1,0:T(2,128)S(1)} all-gather(f32[1,2,1024]{2,1,0:T(2,128)S(1)} %slice_bitcast_fusion), channel_id=2, replica_groups=mesh['prompt'=4,'dp'=4,'mp_0'=4,'mp_1'=2] {'mp_0','mp_1'}, dimensions={0}, use_global_device_ids=true | all-gather | bytes 73728 | tf_op jit(solution)/shard_map/all_gather | solution.py:432
  184.0 12.6 %all_to_all.11 = f32[16,1,9]{2,1,0:T(1,128)S(1)} all-to-all(f32[16,1,9]{2,1,0:T(1,128)S(1)} %broadcast_in_dim.42), channel_id=1, replica_groups=mesh['prompt'=4,'dp'=4,'mp_0'=4,'mp_1'=2] {'prompt','dp'}, dimensions={0} | all-to-all | bytes 1152 | tf_op jit(solution)/shard_map/all_to_all | solution.py:23
  197.3 1.2 multiply_divide_fusion
  (118 shorter events, 11.3 us)
Async XLA Ops:
  7.2 59.8 %copy-start = (s32[1,512]{1,0:T(1,128)S(1)}, s32[1,512]{1,0:T(1,128)}, u32[]{:S(2)}) copy-start(s32[1,512]{1,0:T(1,128)} %param.11) | copy-start | bytes 6148
  7.2 119.4 %all-gather.5.cloned.1.call-start = ((), (), s32[]{:S(2)}) async-start(), calls=%async_computation.2 | async-start | bytes 13369344 | tf_op jit(solution)/shard_map/all_gather | solution.py:405
  10.7 145.8 %all-gather.7.cloned.1.call-start = ((), (), s32[]{:S(2)}) async-start(), calls=%async_computation.3 | async-start | bytes 4456448 | tf_op jit(solution)/shard_map/all_gather | solution.py:405
  14.1 55.4 %all-to-all-start = ((bf16[8,256,512]{2,1,0:T(8,128)(2,1)}), bf16[8,256,512]{2,1,0:T(8,128)(2,1)S(1)}, u32[]{:S(2)}, u32[]{:S(2)}) async-start(bf16[8,256,512]{2,1,0:T(8,128)(2,1)} %split_columns.1), calls=%async_computation | async-start | bytes 4194304 | tf_op jit(solution)/shard_map/all_to_all | solution.py:409
  41.0 11.3 %collective-permute-start.2 = (bf16[1024,128]{1,0:T(8,128)(2,1)}, bf16[1024,128]{1,0:T(8,128)(2,1)S(1)}, u32[]{:S(2)}, u32[]{:S(2)}) collective-permute-start(bf16[1024,128]{1,0:T(8,128)(2,1)} %get-tuple-element.8.refs_0_), channel_id=1, source_target_pairs={{0,2},{2,4},{4,6},{6,0},{1,3},{3,5},{5,7},{7,1},{8,10},{10,12},{12... | collective-permute-start | bytes 786440 | tf_op jit(solution)/shard_map/ppermute | solution.py:29
  43.1 9.4 %collective-permute-start.7 = (bf16[1024,128]{1,0:T(8,128)(2,1)}, bf16[1024,128]{1,0:T(8,128)(2,1)S(1)}, u32[]{:S(2)}, u32[]{:S(2)}) collective-permute-start(bf16[1024,128]{1,0:T(8,128)(2,1)} %get-tuple-element.9.refs_1_), channel_id=1, source_target_pairs={{0,6},{2,0},{4,2},{6,4},{1,7},{3,1},{5,3},{7,5},{8,14},{10,8},{12,... | collective-permute-start | bytes 786440 | tf_op jit(solution)/shard_map/ppermute | solution.py:29
  44.4 13.6 %collective-permute-start.3 = (bf16[1024,128]{1,0:T(8,128)(2,1)}, bf16[1024,128]{1,0:T(8,128)(2,1)S(1)}, u32[]{:S(2)}, u32[]{:S(2)}) collective-permute-start(bf16[1024,128]{1,0:T(8,128)(2,1)} %get-tuple-element.9.refs_1_), channel_id=1, source_target_pairs={{0,2},{2,4},{4,6},{6,0},{1,3},{3,5},{5,7},{7,1},{8,10},{10,12},{12... | collective-permute-start | bytes 786440 | tf_op jit(solution)/shard_map/ppermute | solution.py:29
  45.1 14.1 %collective-permute-start.6 = (bf16[1024,128]{1,0:T(8,128)(2,1)}, bf16[1024,128]{1,0:T(8,128)(2,1)S(1)}, u32[]{:S(2)}, u32[]{:S(2)}) collective-permute-start(bf16[1024,128]{1,0:T(8,128)(2,1)} %get-tuple-element.8.refs_0_), channel_id=1, source_target_pairs={{0,6},{2,0},{4,2},{6,4},{1,7},{3,1},{5,3},{7,5},{8,14},{10,8},{12,... | collective-permute-start | bytes 786440 | tf_op jit(solution)/shard_map/ppermute | solution.py:29
  47.6 11.8 %collective-permute-start = (bf16[1024,128]{1,0:T(8,128)(2,1)}, bf16[1024,128]{1,0:T(8,128)(2,1)S(1)}, u32[]{:S(2)}, u32[]{:S(2)}) collective-permute-start(bf16[1024,128]{1,0:T(8,128)(2,1)} %get-tuple-element.8.refs_0_), channel_id=1, source_target_pairs={{0,1},{1,0},{2,3},{3,2},{4,5},{5,4},{6,7},{7,6},{8,9},{9,8},{10,11... | collective-permute-start | bytes 786440 | tf_op jit(solution)/shard_map/ppermute | solution.py:29
  52.3 7.4 %collective-permute-start.1 = (bf16[1024,128]{1,0:T(8,128)(2,1)}, bf16[1024,128]{1,0:T(8,128)(2,1)}, u32[]{:S(2)}, u32[]{:S(2)}) collective-permute-start(bf16[1024,128]{1,0:T(8,128)(2,1)} %get-tuple-element.9.refs_1_), channel_id=1, source_target_pairs={{0,1},{1,0},{2,3},{3,2},{4,5},{5,4},{6,7},{7,6},{8,9},{9,8},{10,11... | collective-permute-start | bytes 786440 | tf_op jit(solution)/shard_map/ppermute | solution.py:29
  52.5 11.1 %collective-permute-start.10 = (bf16[1024,128]{1,0:T(8,128)(2,1)S(1)}, bf16[1024,128]{1,0:T(8,128)(2,1)}, u32[]{:S(2)}, u32[]{:S(2)}) collective-permute-start(bf16[1024,128]{1,0:T(8,128)(2,1)S(1)} %collective-permute-done.2.refs_4_), channel_id=1, source_target_pairs={{0,2},{2,4},{4,6},{6,0},{1,3},{3,5},{5,7},{7,1},{8,10},{10,12},{12... | collective-permute-start | bytes 786440 | tf_op jit(solution)/shard_map/ppermute | solution.py:29
  58.0 8.5 %collective-permute-start.11 = (bf16[1024,128]{1,0:T(8,128)(2,1)S(1)}, bf16[1024,128]{1,0:T(8,128)(2,1)}, u32[]{:S(2)}, u32[]{:S(2)}) collective-permute-start(bf16[1024,128]{1,0:T(8,128)(2,1)S(1)} %collective-permute-done.7.refs_9_), channel_id=1, source_target_pairs={{0,6},{2,0},{4,2},{6,4},{1,7},{3,1},{5,3},{7,5},{8,14},{10,8},{12,... | collective-permute-start | bytes 786440 | tf_op jit(solution)/shard_map/ppermute | solution.py:29
  59.3 7.2 %collective-permute-start.4 = (bf16[1024,128]{1,0:T(8,128)(2,1)S(1)}, bf16[1024,128]{1,0:T(8,128)(2,1)}, u32[]{:S(2)}, u32[]{:S(2)}) collective-permute-start(bf16[1024,128]{1,0:T(8,128)(2,1)S(1)} %collective-permute-done.2.refs_4_), channel_id=1, source_target_pairs={{0,1},{1,0},{2,3},{3,2},{4,5},{5,4},{6,7},{7,6},{8,9},{9,8},{10,11... | collective-permute-start | bytes 786440 | tf_op jit(solution)/shard_map/ppermute | solution.py:29
  59.4 10.0 %collective-permute-start.9 = (bf16[1024,128]{1,0:T(8,128)(2,1)S(1)}, bf16[1024,128]{1,0:T(8,128)(2,1)}, u32[]{:S(2)}, u32[]{:S(2)}) collective-permute-start(bf16[1024,128]{1,0:T(8,128)(2,1)S(1)} %collective-permute-done.7.refs_9_), channel_id=1, source_target_pairs={{0,1},{1,0},{2,3},{3,2},{4,5},{5,4},{6,7},{7,6},{8,9},{9,8},{10,11... | collective-permute-start | bytes 786440 | tf_op jit(solution)/shard_map/ppermute | solution.py:29
  59.8 9.7 %collective-permute-start.5 = (bf16[1024,128]{1,0:T(8,128)(2,1)S(1)}, bf16[1024,128]{1,0:T(8,128)(2,1)}, u32[]{:S(2)}, u32[]{:S(2)}) collective-permute-start(bf16[1024,128]{1,0:T(8,128)(2,1)S(1)} %collective-permute-done.3.refs_5_), channel_id=1, source_target_pairs={{0,1},{1,0},{2,3},{3,2},{4,5},{5,4},{6,7},{7,6},{8,9},{9,8},{10,11... | collective-permute-start | bytes 786440 | tf_op jit(solution)/shard_map/ppermute | solution.py:29
  63.6 5.8 %collective-permute-start.8 = (bf16[1024,128]{1,0:T(8,128)(2,1)S(1)}, bf16[1024,128]{1,0:T(8,128)(2,1)}, u32[]{:S(2)}, u32[]{:S(2)}) collective-permute-start(bf16[1024,128]{1,0:T(8,128)(2,1)S(1)} %collective-permute-done.6.refs_8_), channel_id=1, source_target_pairs={{0,1},{1,0},{2,3},{3,2},{4,5},{5,4},{6,7},{7,6},{8,9},{9,8},{10,11... | collective-permute-start | bytes 786440 | tf_op jit(solution)/shard_map/ppermute | solution.py:29
  66.4 3.0 %collective-permute-start.12 = (bf16[1024,128]{1,0:T(8,128)(2,1)}, bf16[1024,128]{1,0:T(8,128)(2,1)}, u32[]{:S(2)}, u32[]{:S(2)}) collective-permute-start(bf16[1024,128]{1,0:T(8,128)(2,1)} %collective-permute-done.10.refs_12_), channel_id=1, source_target_pairs={{0,1},{1,0},{2,3},{3,2},{4,5},{5,4},{6,7},{7,6},{8,9},{9,8},{10,11... | collective-permute-start | bytes 786440 | tf_op jit(solution)/shard_map/ppermute | solution.py:29
  66.4 3.1 %collective-permute-start.13 = (bf16[1024,128]{1,0:T(8,128)(2,1)}, bf16[1024,128]{1,0:T(8,128)(2,1)}, u32[]{:S(2)}, u32[]{:S(2)}) collective-permute-start(bf16[1024,128]{1,0:T(8,128)(2,1)} %collective-permute-done.11.refs_13_), channel_id=1, source_target_pairs={{0,1},{1,0},{2,3},{3,2},{4,5},{5,4},{6,7},{7,6},{8,9},{9,8},{10,11... | collective-permute-start | bytes 786440 | tf_op jit(solution)/shard_map/ppermute | solution.py:29
  78.8 27.9 %collective-permute-start.21 = (bf16[1024,256]{1,0:T(8,128)(2,1)}, bf16[1024,256]{1,0:T(8,128)(2,1)S(1)}, u32[]{:S(2)}, u32[]{:S(2)}) collective-permute-start(bf16[1024,256]{1,0:T(8,128)(2,1)} %get-tuple-element.11.refs_2_), channel_id=1, source_target_pairs={{0,6},{2,0},{4,2},{6,4},{1,7},{3,1},{5,3},{7,5},{8,14},{10,8},{12,... | collective-permute-start | bytes 1572872 | tf_op jit(solution)/shard_map/ppermute | solution.py:29
  80.5 26.3 %collective-permute-start.17 = (bf16[1024,256]{1,0:T(8,128)(2,1)}, bf16[1024,256]{1,0:T(8,128)(2,1)S(1)}, u32[]{:S(2)}, u32[]{:S(2)}) collective-permute-start(bf16[1024,256]{1,0:T(8,128)(2,1)} %get-tuple-element.11.refs_2_), channel_id=1, source_target_pairs={{0,2},{2,4},{4,6},{6,0},{1,3},{3,5},{5,7},{7,1},{8,10},{10,12},{12... | collective-permute-start | bytes 1572872 | tf_op jit(solution)/shard_map/ppermute | solution.py:29
  80.9 25.8 %collective-permute-start.16 = (bf16[1024,256]{1,0:T(8,128)(2,1)}, bf16[1024,256]{1,0:T(8,128)(2,1)S(1)}, u32[]{:S(2)}, u32[]{:S(2)}) collective-permute-start(bf16[1024,256]{1,0:T(8,128)(2,1)} %get-tuple-element.10.refs_1_), channel_id=1, source_target_pairs={{0,2},{2,4},{4,6},{6,0},{1,3},{3,5},{5,7},{7,1},{8,10},{10,12},{12... | collective-permute-start | bytes 1572872 | tf_op jit(solution)/shard_map/ppermute | solution.py:29
  80.9 26.4 %collective-permute-start.20 = (bf16[1024,256]{1,0:T(8,128)(2,1)}, bf16[1024,256]{1,0:T(8,128)(2,1)S(1)}, u32[]{:S(2)}, u32[]{:S(2)}) collective-permute-start(bf16[1024,256]{1,0:T(8,128)(2,1)} %get-tuple-element.10.refs_1_), channel_id=1, source_target_pairs={{0,6},{2,0},{4,2},{6,4},{1,7},{3,1},{5,3},{7,5},{8,14},{10,8},{12,... | collective-permute-start | bytes 1572872 | tf_op jit(solution)/shard_map/ppermute | solution.py:29
  84.2 26.1 %collective-permute-start.14 = (bf16[1024,256]{1,0:T(8,128)(2,1)}, bf16[1024,256]{1,0:T(8,128)(2,1)S(1)}, u32[]{:S(2)}, u32[]{:S(2)}) collective-permute-start(bf16[1024,256]{1,0:T(8,128)(2,1)} %get-tuple-element.10.refs_1_), channel_id=1, source_target_pairs={{0,1},{1,0},{2,3},{3,2},{4,5},{5,4},{6,7},{7,6},{8,9},{9,8},{10,11... | collective-permute-start | bytes 1572872 | tf_op jit(solution)/shard_map/ppermute | solution.py:29
  106.7 3.7 %collective-permute-start.15 = (bf16[1024,256]{1,0:T(8,128)(2,1)}, bf16[1024,256]{1,0:T(8,128)(2,1)S(1)}, u32[]{:S(2)}, u32[]{:S(2)}) collective-permute-start(bf16[1024,256]{1,0:T(8,128)(2,1)} %get-tuple-element.11.refs_2_), channel_id=1, source_target_pairs={{0,1},{1,0},{2,3},{3,2},{4,5},{5,4},{6,7},{7,6},{8,9},{9,8},{10,11... | collective-permute-start | bytes 1572872 | tf_op jit(solution)/shard_map/ppermute | solution.py:29
  106.7 15.6 %collective-permute-start.24 = (bf16[1024,256]{1,0:T(8,128)(2,1)S(1)}, bf16[1024,256]{1,0:T(8,128)(2,1)S(1)}, u32[]{:S(2)}, u32[]{:S(2)}) collective-permute-start(bf16[1024,256]{1,0:T(8,128)(2,1)S(1)} %collective-permute-done.16.refs_5_), channel_id=1, source_target_pairs={{0,2},{2,4},{4,6},{6,0},{1,3},{3,5},{5,7},{7,1},{8,10},{10,12},{12... | collective-permute-start | bytes 1572872 | tf_op jit(solution)/shard_map/ppermute | solution.py:29
  106.8 16.0 %collective-permute-start.18 = (bf16[1024,256]{1,0:T(8,128)(2,1)S(1)}, bf16[1024,256]{1,0:T(8,128)(2,1)S(1)}, u32[]{:S(2)}, u32[]{:S(2)}) collective-permute-start(bf16[1024,256]{1,0:T(8,128)(2,1)S(1)} %collective-permute-done.16.refs_5_), channel_id=1, source_target_pairs={{0,1},{1,0},{2,3},{3,2},{4,5},{5,4},{6,7},{7,6},{8,9},{9,8},{10,11... | collective-permute-start | bytes 1572872 | tf_op jit(solution)/shard_map/ppermute | solution.py:29
  107.3 15.0 %collective-permute-start.25 = (bf16[1024,256]{1,0:T(8,128)(2,1)S(1)}, bf16[1024,256]{1,0:T(8,128)(2,1)S(1)}, u32[]{:S(2)}, u32[]{:S(2)}) collective-permute-start(bf16[1024,256]{1,0:T(8,128)(2,1)S(1)} %collective-permute-done.21.refs_10_), channel_id=1, source_target_pairs={{0,6},{2,0},{4,2},{6,4},{1,7},{3,1},{5,3},{7,5},{8,14},{10,8},{12,... | collective-permute-start | bytes 1572872 | tf_op jit(solution)/shard_map/ppermute | solution.py:29
  110.3 13.9 %collective-permute-start.23 = (bf16[1024,256]{1,0:T(8,128)(2,1)S(1)}, bf16[1024,256]{1,0:T(8,128)(2,1)S(1)}, u32[]{:S(2)}, u32[]{:S(2)}) collective-permute-start(bf16[1024,256]{1,0:T(8,128)(2,1)S(1)} %collective-permute-done.21.refs_10_), channel_id=1, source_target_pairs={{0,1},{1,0},{2,3},{3,2},{4,5},{5,4},{6,7},{7,6},{8,9},{9,8},{10,11... | collective-permute-start | bytes 1572872 | tf_op jit(solution)/shard_map/ppermute | solution.py:29
  110.4 13.3 %collective-permute-start.19 = (bf16[1024,256]{1,0:T(8,128)(2,1)S(1)}, bf16[1024,256]{1,0:T(8,128)(2,1)S(1)}, u32[]{:S(2)}, u32[]{:S(2)}) collective-permute-start(bf16[1024,256]{1,0:T(8,128)(2,1)S(1)} %collective-permute-done.17.refs_6_), channel_id=1, source_target_pairs={{0,1},{1,0},{2,3},{3,2},{4,5},{5,4},{6,7},{7,6},{8,9},{9,8},{10,11... | collective-permute-start | bytes 1572872 | tf_op jit(solution)/shard_map/ppermute | solution.py:29
  122.3 1.9 collective-permute-start.22
  122.3 3.4 %collective-permute-start.26 = (bf16[1024,256]{1,0:T(8,128)(2,1)S(1)}, bf16[1024,256]{1,0:T(8,128)(2,1)S(1)}, u32[]{:S(2)}, u32[]{:S(2)}) collective-permute-start(bf16[1024,256]{1,0:T(8,128)(2,1)S(1)} %collective-permute-done.24.refs_13_), channel_id=1, source_target_pairs={{0,1},{1,0},{2,3},{3,2},{4,5},{5,4},{6,7},{7,6},{8,9},{9,8},{10,11... | collective-permute-start | bytes 1572872 | tf_op jit(solution)/shard_map/ppermute | solution.py:29
  122.8 3.7 %collective-permute-start.27 = (bf16[1024,256]{1,0:T(8,128)(2,1)S(1)}, bf16[1024,256]{1,0:T(8,128)(2,1)}, u32[]{:S(2)}, u32[]{:S(2)}) collective-permute-start(bf16[1024,256]{1,0:T(8,128)(2,1)S(1)} %collective-permute-done.25.refs_14_), channel_id=1, source_target_pairs={{0,1},{1,0},{2,3},{3,2},{4,5},{5,4},{6,7},{7,6},{8,9},{9,8},{10,11... | collective-permute-start | bytes 1572872 | tf_op jit(solution)/shard_map/ppermute | solution.py:29
  (20 other events, 235.0 us)
Sparse Core Ops, SparseCore 0:
  10.8 92.3 all-gather.4
  105.3 51.1 all-gather.6

commit v3 on v2

v3 whole, which is shorter than its diff:
```python
import math

import jax
import jax.numpy as jnp
import numpy as np
from jax import lax
from jax.experimental import pallas as pl
from jax.experimental.pallas import tpu as pltpu
from jax.sharding import Mesh
from jax.sharding import PartitionSpec as P

HD = 128
MP = ("mp_0", "mp_1")
RING = (0, 3, 1, 2)
EPSILON = 1e-05
BASE_THETA = 10000.0
MASKED = -1e30
VMEM_LIMIT = 56 << 20
LOG2E = math.log2(math.e)


def of_everyone(value, axis):
    copies = jnp.broadcast_to(value, (lax.axis_size(axis), *value.shape))
    everything = lax.all_to_all(copies, axis, split_axis=0, concat_axis=0, tiled=True)
    return jnp.sum(everything, axis=0)


def shifted(value, axis, shift):
    n = lax.axis_size(axis)
    return lax.ppermute(value, axis, [(i, (i + shift) % n) for i in range(n)])


def ring_pairs(left, right, axis):
    left_before = shifted(left, axis, 1)
    right_after = shifted(right, axis, -1)
    right, left_before, right_after = lax.optimization_barrier((right, left_before, right_after))
    left_far = shifted(left_before, axis, 1)
    right_far = shifted(right_after, axis, -1)
    right_before = shifted(right, axis, 1)
    left_after = shifted(left, axis, -1)
    return [
        (left, right),
        (left_before, right_before),
        (left_after, right_after),
        (left_far, right_far),
    ]


def whole_row(left, right):
    pairs = ring_pairs(left, right, "mp_0")
    return [b for pair in pairs for b in (*pair, *(shifted(half, "mp_1", 1) for half in pair))]


def rope_tables(number_rows, offset):
    positions = np.arange(offset, offset + number_rows, dtype=np.float32)
    indices_f = np.arange(HD // 2, dtype=np.float32)
    frequency = np.exp(indices_f * np.float32(-2.0 * math.log(BASE_THETA) / HD))
    angles = positions[:, None] * frequency[None, :]
    return jnp.asarray(np.cos(angles)), jnp.asarray(np.sin(angles))


def attention_kernel(
    target_ref, prompt_ref, gain_ref, w_ref, cos_t, sin_t, cos_p, sin_p, left_ref, right_ref,
    acc_t, acc_p, sq_t, sq_p, q_s, k_s, v_s, kp_s, vp_s,
):
    step = pl.program_id(0)
    n_prompts = prompt_ref.shape[0]

    @pl.when(step == 0)
    def _():
        acc_t[...] = jnp.zeros_like(acc_t)
        acc_p[...] = jnp.zeros_like(acc_p)
        sq_t[...] = jnp.zeros_like(sq_t)
        sq_p[...] = jnp.zeros_like(sq_p)

    gain = gain_ref[...]

    def lanes_of_squares(x):
        square = x * x
        return sum(square[:, i : i + 128] for i in range(0, square.shape[1], 128))

    x = target_ref[0].astype(jnp.float32)
    sq_t[...] += lanes_of_squares(x)
    scaled = (x * gain).astype(jnp.bfloat16)
    for c in range(3):
        acc_t[c] += jnp.dot(scaled, w_ref[c], preferred_element_type=jnp.float32)
    for p in range(n_prompts):
        x = prompt_ref[p].astype(jnp.float32)
        sq_p[p] += lanes_of_squares(x)
        scaled = (x * gain).astype(jnp.bfloat16)
        for c in range(2):
            acc_p[p, c] += jnp.dot(scaled, w_ref[c + 1], preferred_element_type=jnp.float32)

    @pl.when(step == pl.num_programs(0) - 1)
    def _():
        width = pl.num_programs(0) * target_ref.shape[2]
        heads = q_s.shape[1] // HD

        def inverse(square):
            return lax.rsqrt(jnp.sum(square, axis=1, keepdims=True) / width + EPSILON)

        def turned(values, cos, sin):
            cos = jnp.concatenate([cos, cos], axis=1)
            sin = jnp.concatenate([-sin, sin], axis=1)
            return values * cos + pltpu.roll(values, HD // 2, 1) * sin

        scale_t = inverse(sq_t[...])
        for h in range(heads):
            at = slice(h * HD, (h + 1) * HD)
            q_s[:, at] = turned(acc_t[0, :, at] * scale_t, cos_t[...], sin_t[...]).astype(jnp.bfloat16)
            k_s[:, at] = turned(acc_t[1, :, at] * scale_t, cos_t[...], sin_t[...]).astype(jnp.bfloat16)
            v_s[:, at] = (acc_t[2, :, at] * scale_t).astype(jnp.bfloat16)
            for p in range(n_prompts):
                scale_p = inverse(sq_p[p])
                kp_s[p, :, at] = turned(
                    acc_p[p, 0, :, at] * scale_p, cos_p[...], sin_p[...]
                ).astype(jnp.bfloat16)
                vp_s[p, :, at] = (acc_p[p, 1, :, at] * scale_p).astype(jnp.bfloat16)
        target_len = q_s.shape[0]
        tile = target_len // 2
        transposed = (((1,), (1,)), ((), ()))
        def one_prompt(p, carry):
            for h in range(heads):
                at = slice(h * HD, (h + 1) * HD)
                for first in range(0, target_len, tile):
                    seen = first + tile
                    q = q_s[first:seen, at]
                    near = lax.dot_general(
                        q, kp_s[p, :, at], transposed, preferred_element_type=jnp.float32
                    ) * HD ** (-0.5)
                    own = lax.dot_general(
                        q, k_s[:seen, at], transposed, preferred_element_type=jnp.float32
                    ) * HD ** (-0.5)
                    row = first + lax.broadcasted_iota(jnp.int32, own.shape, 0)
                    key = lax.broadcasted_iota(jnp.int32, own.shape, 1)
                    own = jnp.where(key <= row, own, MASKED)
                    top = jnp.maximum(
                        jnp.max(near, axis=1, keepdims=True), jnp.max(own, axis=1, keepdims=True)
                    )
                    near = jnp.exp(near - top)
                    own = jnp.exp(own - top)
                    norm = 1.0 / (
                        jnp.sum(near, axis=1, keepdims=True) + jnp.sum(own, axis=1, keepdims=True)
                    )
                    context = jnp.dot(
                        (near * norm).astype(jnp.bfloat16),
                        vp_s[p, :, at],
                        preferred_element_type=jnp.float32,
                    ) + jnp.dot(
                        (own * norm).astype(jnp.bfloat16),
                        v_s[:seen, at],
                        preferred_element_type=jnp.float32,
                    )
                    out_ref = (left_ref, right_ref)[h]
                    rows = pl.ds(pl.multiple_of(p * target_len + first, tile), tile)
                    out_ref[rows, :] = context.astype(jnp.bfloat16)
            return carry

        lax.fori_loop(0, n_prompts, one_prompt, 0)


def attention(target_embed, prompts, attn_gain, w_qkv):
    n_prompts, prompt_len, width = prompts.shape
    target_len = target_embed.shape[1]
    inner = w_qkv.shape[2]
    chunk = 512
    tables = (*rope_tables(target_len, prompt_len), *rope_tables(prompt_len, 0))
    whole = lambda shape: pl.BlockSpec(shape, lambda k: (0,) * len(shape))
    rows = n_prompts * target_len
    return pl.pallas_call(
        attention_kernel,
        out_shape=[jax.ShapeDtypeStruct((rows, inner // 2), jnp.bfloat16)] * 2,
        grid=(width // chunk,),
        in_specs=[
            pl.BlockSpec((1, target_len, chunk), lambda k: (0, 0, k)),
            pl.BlockSpec((n_prompts, prompt_len, chunk), lambda k: (0, 0, k)),
            pl.BlockSpec((1, chunk), lambda k: (0, k)),
            pl.BlockSpec((3, chunk, inner), lambda k: (0, k, 0)),
            *(whole(t.shape) for t in tables),
        ],
        out_specs=[whole((rows, inner // 2))] * 2,
        scratch_shapes=[
            pltpu.VMEM((3, target_len, inner), jnp.float32),
            pltpu.VMEM((n_prompts, 2, prompt_len, inner), jnp.float32),
            pltpu.VMEM((target_len, 128), jnp.float32),
            pltpu.VMEM((n_prompts, prompt_len, 128), jnp.float32),
            *(pltpu.VMEM((target_len, inner), jnp.bfloat16) for _ in range(3)),
            *(pltpu.VMEM((n_prompts, prompt_len, inner), jnp.bfloat16) for _ in range(2)),
        ],
        compiler_params=pltpu.CompilerParams(vmem_limit_bytes=VMEM_LIMIT),
        cost_estimate=pl.CostEstimate(
            flops=8 * 10**9, bytes_accessed=12 * 10**6, transcendentals=2 * 10**6
        ),
        name="attention",
    )(target_embed, prompts, attn_gain.reshape(1, -1), w_qkv, *tables)


def output_kernel(places_ref, *refs):
    *ctx_refs, w_ref, embed_ref, gain_ref, left_ref, right_ref, ctx_s = refs
    at = 0
    for ref in ctx_refs:
        ctx_s[:, at : at + ref.shape[1]] = ref[...]
        at += ref.shape[1]

    total = embed_ref[0].astype(jnp.float32) + jnp.dot(
        ctx_s[...], w_ref[...], preferred_element_type=jnp.float32
    )
    scaled = (total * gain_ref[...]).astype(jnp.bfloat16)
    half = scaled.shape[1] // 2
    left_ref[...] = scaled[:, :half]
    right_ref[...] = scaled[:, half:]


def output_part(place, contexts, out_cols, target_embed, final_gain):
    rows = contexts[0].shape[0]
    inner, part = out_cols.shape
    target_len = target_embed.shape[1]
    tile = target_len // 2
    return pl.pallas_call(
        output_kernel,
        out_shape=[jax.ShapeDtypeStruct((rows, part // 2), jnp.bfloat16)] * 2,
        grid_spec=pltpu.PrefetchScalarGridSpec(
            num_scalar_prefetch=1,
            grid=(rows // tile,),
            in_specs=[
                *(pl.BlockSpec((tile, c.shape[1]), lambda i, at: (i, 0)) for c in contexts),
                pl.BlockSpec(out_cols.shape, lambda i, at: (0, 0)),
                pl.BlockSpec((1, tile, part), lambda i, at: (0, i % 2, at[0])),
                pl.BlockSpec((1, part), lambda i, at: (0, at[0])),
            ],
            out_specs=[pl.BlockSpec((tile, part // 2), lambda i, at: (i, 0))] * 2,
            scratch_shapes=[pltpu.VMEM((tile, inner), jnp.bfloat16)],
        ),
        compiler_params=pltpu.CompilerParams(vmem_limit_bytes=VMEM_LIMIT),
        cost_estimate=pl.CostEstimate(
            flops=2 * 10**9, bytes_accessed=8 * 10**6, transcendentals=0
        ),
        name="output_part",
    )(place, *contexts, out_cols, target_embed, final_gain.reshape(1, -1))


def assemble_kernel(*refs):
    *row_refs, degain_ref, rows_ref, scale_ref = refs
    tile, width = rows_ref.shape
    squares = jnp.zeros((tile, 128), jnp.float32)
    k = 0
    for ref in row_refs:
        rows_ref[:, k : k + ref.shape[1]] = ref[...]
        for i in range(0, ref.shape[1], 128):
            x = ref[:, i : i + 128].astype(jnp.float32) * degain_ref[:, k + i : k + i + 128]
            squares += x * x
        k += ref.shape[1]
    mean = jnp.sum(squares, axis=1, keepdims=True) / width
    scale_ref[...] = jnp.broadcast_to(lax.rsqrt(mean + EPSILON) * LOG2E, scale_ref.shape)


def assemble(row_blocks, degain):
    rows, width, tile = row_blocks[0].shape[0], degain.shape[1], 256
    by_tile = lambda columns: pl.BlockSpec((tile, columns), lambda i: (i, 0))
    return pl.pallas_call(
        assemble_kernel,
        out_shape=[
            jax.ShapeDtypeStruct((rows, width), jnp.bfloat16),
            jax.ShapeDtypeStruct((rows, 128), jnp.float32),
        ],
        grid=(rows // tile,),
        in_specs=[
            *(by_tile(b.shape[1]) for b in row_blocks),
            pl.BlockSpec(degain.shape, lambda i: (0, 0)),
        ],
        out_specs=[by_tile(width), by_tile(128)],
        compiler_params=pltpu.CompilerParams(vmem_limit_bytes=VMEM_LIMIT),
        cost_estimate=pl.CostEstimate(
            flops=4 * rows * width, bytes_accessed=4 * rows * width, transcendentals=0
        ),
        name="assemble",
    )(*row_blocks, degain)


def vocab_kernel(
    first_ref, rows_ref, scale_s, label_s, w_ref, out_ref,
    rows_s, first_s, second_s, top_s, sum_s, pick_s, sem,
):
    step = pl.program_id(0)
    rows, width = rows_s.shape
    tile, columns = first_s.shape
    n_tiles = rows // tile
    at_tile = lambda t: slice(t * tile, (t + 1) * tile)
    arrivals = [
        pltpu.make_async_copy(rows_ref.at[at_tile(t)], rows_s.at[at_tile(t)], sem.at[t])
        for t in range(n_tiles)
    ]

    @pl.when(step == 0)
    def _():
        for copy in arrivals:
            copy.start()
        top_s[...] = jnp.full_like(top_s, MASKED)
        sum_s[...] = jnp.zeros_like(sum_s)
        pick_s[...] = jnp.zeros_like(pick_s)

    lane = lax.broadcasted_iota(jnp.int32, (1, 128), 1)

    def take(at, product_ref, first_column):
        scale = scale_s[at, :]
        logits = [product_ref[:, c : c + 128] * scale for c in range(0, columns, 128)]
        old = top_s[at, :]
        top = old
        for part in logits:
            top = jnp.maximum(top, part)
        total = sum_s[at, :] * jnp.exp2(old - top)
        pick = pick_s[at, :]
        place = label_s[at, :] - (first_column + lane)
        for c, part in enumerate(logits):
            total += jnp.exp2(part - top)
            pick = jnp.where(place == c * 128, part, pick)
        top_s[at, :] = top
        sum_s[at, :] = total
        pick_s[at, :] = pick

    first_column = first_ref[0] + step * first_ref[1]
    products = (first_s, second_s)
    for t in range(n_tiles):

        @pl.when(step == 0)
        def _():
            arrivals[t].wait()

        product = jnp.dot(rows_s[at_tile(t), :], w_ref[0], preferred_element_type=jnp.float32)
        if t:
            take(at_tile(t - 1), products[(t + 1) % 2], first_column)
        products[t % 2][...] = product
    take(at_tile(n_tiles - 1), products[(n_tiles + 1) % 2], first_column)

    @pl.when(step == pl.num_programs(0) - 1)
    def _():
        top = jnp.max(top_s[...], axis=1, keepdims=True)
        total = jnp.sum(sum_s[...] * jnp.exp2(top_s[...] - top), axis=1, keepdims=True)
        total = top * (1.0 / LOG2E) + jnp.log(total)
        pick = jnp.sum(pick_s[...], axis=1, keepdims=True) * (1.0 / LOG2E)
        both = jnp.where(lane == 0, total, jnp.where(lane == 1, pick, 0.0))
        out_ref[...] = both.T[:8, :]


def vocab_stats(first, rows, scale, row_labels, vocab_all):
    n_rows, width = rows.shape
    n_blocks, _, columns = vocab_all.shape
    tile = 256
    whole = lambda shape: pl.BlockSpec(shape, lambda j, f: (0, 0))
    return pl.pallas_call(
        vocab_kernel,
        out_shape=jax.ShapeDtypeStruct((8, n_rows), jnp.float32),
        grid_spec=pltpu.PrefetchScalarGridSpec(
            num_scalar_prefetch=1,
            grid=(n_blocks,),
            in_specs=[
                pl.BlockSpec(memory_space=pl.ANY),
                whole(scale.shape),
                whole(row_labels.shape),
                pl.BlockSpec((1, width, columns), lambda j, f: (j, 0, 0)),
            ],
            out_specs=whole((8, n_rows)),
            scratch_shapes=[
                pltpu.VMEM((n_rows, width), jnp.bfloat16),
                *(pltpu.VMEM((tile, columns), jnp.float32) for _ in range(2)),
                *(pltpu.VMEM((n_rows, 128), jnp.float32) for _ in range(3)),
                pltpu.SemaphoreType.DMA((n_rows // tile,)),
            ],
        ),
        compiler_params=pltpu.CompilerParams(vmem_limit_bytes=VMEM_LIMIT),
        cost_estimate=pl.CostEstimate(
            flops=2 * n_rows * width * n_blocks * columns,
            bytes_accessed=n_rows * width * 2 + n_blocks * width * columns * 2,
            transcendentals=n_rows * n_blocks * columns,
        ),
        name="vocab_stats",
    )(first, rows, scale, row_labels, vocab_all)


def piece_kernel(row_ref, vocab_ref, piece_ref, sem):
    part = piece_ref.shape[0] // 2
    started = [
        pltpu.make_async_copy(
            vocab_ref.at[pl.ds(pl.multiple_of(row_ref[i] * part, part), part)],
            piece_ref.at[i * part : (i + 1) * part],
            sem.at[i],
        )
        for i in range(2)
    ]
    for copy in started:
        copy.start()
    for copy in started:
        copy.wait()


def vocab_piece(places, w_vocab, part):
    return pl.pallas_call(
        piece_kernel,
        out_shape=jax.ShapeDtypeStruct((2 * part, w_vocab.shape[1]), jnp.bfloat16),
        grid_spec=pltpu.PrefetchScalarGridSpec(
            num_scalar_prefetch=1,
            grid=(),
            in_specs=[pl.BlockSpec(memory_space=pl.ANY)],
            out_specs=pl.BlockSpec(memory_space=pltpu.VMEM),
            scratch_shapes=[pltpu.SemaphoreType.DMA((2,))],
        ),
        compiler_params=pltpu.CompilerParams(vmem_limit_bytes=VMEM_LIMIT),
        cost_estimate=pl.CostEstimate(flops=0, bytes_accessed=2 << 20, transcendentals=0),
        name="vocab_piece",
    )(places, w_vocab)


def split_kernel(w_ref, out_ref):
    part = out_ref.shape[2]
    for i in range(out_ref.shape[0]):
        out_ref[i] = w_ref[:, i * part : (i + 1) * part]


def split_columns(w, n):
    rows, columns = w.shape
    part = columns // n
    return pl.pallas_call(
        split_kernel,
        out_shape=jax.ShapeDtypeStruct((n, rows, part), w.dtype),
        grid=(2,),
        in_specs=[pl.BlockSpec((rows, columns // 2), lambda i: (0, i))],
        out_specs=pl.BlockSpec((n // 2, rows, part), lambda i: (i, 0, 0)),
        cost_estimate=pl.CostEstimate(flops=0, bytes_accessed=4 << 20, transcendentals=0),
        name="split_columns",
    )(w)


def order_kernel(place_ref, in_ref, out_ref, sem):
    n, width, _ = in_ref.shape
    started = [
        pltpu.make_async_copy(
            in_ref.at[place_ref[i]], out_ref.at[i * width : (i + 1) * width], sem.at[i]
        )
        for i in range(n)
    ]
    for copy in started:
        copy.start()
    for copy in started:
        copy.wait()


def in_ring_order(places, blocks):
    n, width, part = blocks.shape
    anywhere = pl.BlockSpec(memory_space=pl.ANY)
    return pl.pallas_call(
        order_kernel,
        out_shape=jax.ShapeDtypeStruct((n * width, part), blocks.dtype),
        grid_spec=pltpu.PrefetchScalarGridSpec(
            num_scalar_prefetch=1,
            grid=(),
            in_specs=[anywhere],
            out_specs=pl.BlockSpec(memory_space=pltpu.VMEM),
            scratch_shapes=[pltpu.SemaphoreType.DMA((n,))],
        ),
        compiler_params=pltpu.CompilerParams(vmem_limit_bytes=VMEM_LIMIT),
        cost_estimate=pl.CostEstimate(flops=0, bytes_accessed=4 << 20, transcendentals=0),
        name="in_ring_order",
    )(places, blocks)


def shards(prompts, target_embed, labels, lengths, attn_gain, w_qkv, w_out, final_gain, w_vocab):
    n_prompt = lax.axis_size("prompt")
    n_dp = lax.axis_size("dp")
    n_model = lax.axis_size(MP)
    prompts_here = prompts.shape[0]
    target_len = target_embed.shape[1]
    model_width = target_embed.shape[2]
    vocab_cols = w_vocab.shape[1]
    heads_width = w_out.shape[0]
    z_index = lax.axis_index("mp_0")
    core = lax.axis_index("mp_1")
    part = model_width // n_model
    places = [((z_index + r) % 4) * 2 + (core + k) % 2 for r in RING for k in range(2)]

    place_ids = jnp.stack(places).astype(jnp.int32)
    x_index = lax.axis_index("prompt")
    turn = jnp.where(x_index == 0, 0, jnp.where(x_index == 1, 3, x_index - 1))
    my_pair = ((z_index + turn) % 4) * 2
    pair = jnp.stack([my_pair + core, my_pair + 1 - core]).astype(jnp.int32)
    piece = vocab_piece(pair, w_vocab, part)
    vocab_all = lax.all_gather(piece, ("dp", "prompt"), axis=0, tiled=True)
    vocab_all = vocab_all.reshape(n_dp, model_width, vocab_cols)
    by_part = split_columns(w_out, n_model)
    out_cols = lax.all_to_all(by_part, MP, split_axis=0, concat_axis=0, tiled=True)

    halves = attention(target_embed, prompts, attn_gain, w_qkv)
    contexts = whole_row(*halves)
    out_cols = in_ring_order(place_ids, out_cols)
    halves = output_part(place_ids[:1], contexts, out_cols, target_embed, final_gain)
    row_blocks = whole_row(*halves)

    degain = 1.0 / jnp.concatenate(
        [lax.dynamic_slice_in_dim(final_gain, p * part, part, 0) for p in places], axis=0
    ).reshape(1, -1)
    row_labels = jnp.tile(labels.reshape(-1, 1), (prompts_here, 128))
    rows, scale = assemble(row_blocks, degain)
    first = jnp.stack([lax.axis_index(MP) * vocab_cols, n_model * vocab_cols]).astype(jnp.int32)
    here = vocab_stats(first, rows, scale, row_labels, vocab_all)[:2]

    every = lax.all_gather(here, MP)
    top_val = jnp.max(every[:, 0], axis=0)
    log_total = top_val + jnp.log(jnp.sum(jnp.exp(every[:, 0] - top_val), axis=0))
    losses = (log_total - jnp.sum(every[:, 1], axis=0)).reshape(prompts_here, 1, target_len)
    valid = jnp.arange(target_len, dtype=jnp.int32)[None, :] < lengths[:, None]
    token_loss = jnp.where(valid[None], losses, 0.0)
    prompt_sums = jnp.sum(token_loss, axis=(1, 2))
    all_prompts = prompts_here * n_prompt
    slot_ids = lax.axis_index("prompt") * prompts_here + jnp.arange(prompts_here, dtype=jnp.int32)
    placed = jnp.sum(
        jnp.where(
            jnp.arange(all_prompts, dtype=jnp.int32)[:, None] == slot_ids[None, :],
            prompt_sums[None, :],
            0.0,
        ),
        axis=1,
    )
    valid_here = jnp.sum(lengths).astype(jnp.float32).reshape(1)
    totals = of_everyone(jnp.concatenate([placed, valid_here]), ("prompt", "dp"))
    prompt_loss = totals[:all_prompts] * float(n_prompt) / totals[all_prompts]
    return (token_loss, prompt_loss)


def solution(mesh):
    finer = Mesh(
        mesh.devices.reshape(mesh.shape["prompt"], mesh.shape["dp"], 4, 2),
        ("prompt", "dp", "mp_0", "mp_1"),
    )
    return jax.shard_map(
        shards,
        mesh=finer,
        in_specs=(
            P("prompt", None, None),
            P("dp", None, None),
            P("dp", None),
            P("dp"),
            P(),
            P(None, None, MP),
            P(MP, None),
            P(),
            P(None, ("dp", "mp_0", "mp_1")),
        ),
        out_specs=(P("prompt", "dp", None), P()),
        check_vma=False,
    )
```

time: 206 us -> 217 us (1.053)
  waiting for transfers between devices: 54.2 us -> 66 us
  other arithmetic: 6.35 us -> 3.75 us
    ppermute x28, waiting for transfers between devices: 51 us -> 65.9 us  [shifted(): return lax.ppermute(value, axis, [(i, (i + shift) % n) for i in range(n)])]
    all_gather x2 -> x1, waiting for transfers between devices: 2.4 us -> 0.02 us  [shards(): vocab_all = lax.all_gather(piece, ('dp', 'prompt'), axis=0, tiled=True)]
    pallas_call x3 -> x4, Pallas kernels: 43 us -> 44.6 us  [the longest x1 29.4 us: vocab_stats(): pl.pallas_call(vocab_kernel, out_shape=jax.ShapeDtypeStruct((8, n_rows),...]
    unnamed x54 -> x61, local copies, waits for them, and re-layouts: 7.7 us -> 6.98 us
  transfers between devices with their start and end apart: 31 -> 30, of which waited for: 10 -> 12; matrix products, arithmetic and copies ran while one was open for 4% -> 3% of each run, Pallas kernels for 26% -> 18%
where the time goes in v3:
time: 217 us; the launch traced here: 216 us
  Pallas kernels  70.4 us (32%)
  waiting for transfers between devices  66 us (30%)
  blocking collectives  27 us (12%)
  starting transfers between devices  24.8 us (11%)
  between operations  15.1 us (7%)
  local copies, waits for them, and re-layouts  9.36 us (4%)
  other arithmetic  3.75 us (2%)
    ppermute x28, waiting for transfers between devices, shifted(): return lax.ppermute(value, axis, [(i, (i + shift) % n) for i in range(n)])  65.9 us
    pallas_call x1, Pallas kernels, vocab_stats(): pl.pallas_call(vocab_kernel, out_shape=jax.ShapeDtypeStruct((8, n_rows),...  29.4 us
    ppermute x28, starting transfers between devices, shifted(): return lax.ppermute(value, axis, [(i, (i + shift) % n) for i in range(n)])  19.3 us
    pallas_call x1, Pallas kernels, attention(): pl.pallas_call(attention_kernel, out_shape=[jax.ShapeDtypeStruct((rows, i...  16.3 us
    all_to_all x1, blocking collectives, of_everyone(): lax.all_to_all(copies, axis, split_axis=0, concat_axis=0, tiled=True)  14.2 us
    all_gather x1, blocking collectives, shards(): every = lax.all_gather(here, MP)  12.7 us
    pallas_call x1, Pallas kernels, assemble(): pl.pallas_call(assemble_kernel, out_shape=[jax.ShapeDtypeStruct((rows, wi...  8.72 us
    unnamed x61, local copies, waits for them, and re-layouts  6.98 us
  transfers between devices with their start and end apart: 30, of which 12 were waited for; matrix products, arithmetic and copies ran while one was open for 3% of the time, Pallas kernels for 18%

profile of v3, /device:TPU:0, one launch (start us, length us, event | category | flops | bytes accessed | tf_op | source)
XLA Modules:
  0.0 216.3 jit_solution(111606229494515849)
XLA Ops:
  7.8 2.9 %vocab_piece.1 = bf16[1024,512]{1,0:T(8,128)(2,1)} custom-call(s32[2]{0:T(128)} %pad_add_fusion.1.row_ref, bf16[4096,512]{1,0:T(8,128)(2,1)} %vocab_ref.1), custom_call_target="tpu_custom_call" | custom-call | bytes 2097152 | tf_op jit(solution)/shard_map/vocab_piece/pallas_call | solution.py:397
  10.7 2.7 %split_columns.1 = bf16[8,256,512]{2,1,0:T(8,128)(2,1)} custom-call(bf16[256,4096]{1,0:T(8,128)(2,1)} %w_ref.3), custom_call_target="tpu_custom_call" | custom-call | bytes 4194304 | tf_op jit(solution)/shard_map/split_columns/pallas_call | solution.py:422
  13.4 5.4 %all-to-all-start = ((bf16[8,256,512]{2,1,0:T(8,128)(2,1)}), bf16[8,256,512]{2,1,0:T(8,128)(2,1)S(1)}, u32[]{:S(2)}, u32[]{:S(2)}) async-start(bf16[8,256,512]{2,1,0:T(8,128)(2,1)} %split_columns.1), calls=%async_computation | async-start | bytes 4194304 | tf_op jit(solution)/shard_map/all_to_all | solution.py:489
  18.8 3.6 %copy.20.prompt_ref = bf16[2,100,4096]{2,1,0:T(8,128)(2,1)} copy(bf16[2,100,4096]{2,0,1:T(2,128)(2,1)} %param.13) | data formatting | bytes 3276800 | tf_op args[0]
  22.3 16.3 %attention.1 = (bf16[1024,128]{1,0:T(8,128)(2,1)}, bf16[1024,128]{1,0:T(8,128)(2,1)}) custom-call(bf16[1,512,4096]{2,1,0:T(8,128)(2,1)} %refs_17_.1, bf16[2,100,4096]{2,1,0:T(8,128)(2,1)} %copy.20.prompt_ref, f32[1,4096]{1,0:T(1,128)} %bitcast.53, bf16[3,4096,256]{2,1,0:T(8,128)(2,1)} %w_ref.2, f32[512,64]{1,0:T(8,128)} %constant.102.clone.cos_t, ...), custom_call_target="tpu_custom_call" | custom-call | flops 8000000000 | bytes 12000000 | tf_op jit(solution)/shard_map/attention/pallas_call | solution.py:170
  38.6 2.0 collective-permute-start
  40.6 1.3 collective-permute-start.1
  41.9 2.0 collective-permute-start.7
  43.9 7.7 %collective-permute-done.refs_4_ = bf16[1024,128]{1,0:T(8,128)(2,1)S(1)} collective-permute-done((bf16[1024,128]{1,0:T(8,128)(2,1)}, bf16[1024,128]{1,0:T(8,128)(2,1)S(1)}, u32[]{:S(2)}, u32[]{:S(2)}) %collective-permute-start) | collective-permute-done | bytes 262176 | tf_op jit(solution)/shard_map/ppermute | solution.py:30
  52.2 2.6 %collective-permute-start.11 = (bf16[1024,128]{1,0:T(8,128)(2,1)S(1)}, bf16[1024,128]{1,0:T(8,128)(2,1)}, u32[]{:S(2)}, u32[]{:S(2)}) collective-permute-start(bf16[1024,128]{1,0:T(8,128)(2,1)S(1)} %collective-permute-done.1.refs_9_), channel_id=1, source_target_pairs={{0,6},{2,0},{4,2},{6,4},{1,7},{3,1},{5,3},{7,5},{8,14},{10,8},{12,... | collective-permute-start | bytes 786440 | tf_op jit(solution)/shard_map/ppermute | solution.py:30
  54.9 1.3 collective-permute-done.7.refs_8_
  56.7 5.3 %collective-permute-done.10.refs_12_ = bf16[1024,128]{1,0:T(8,128)(2,1)S(1)} collective-permute-done((bf16[1024,128]{1,0:T(8,128)(2,1)S(1)}, bf16[1024,128]{1,0:T(8,128)(2,1)S(1)}, u32[]{:S(2)}, u32[]{:S(2)}) %collective-permute-start.10) | collective-permute-done | bytes 262176 | tf_op jit(solution)/shard_map/ppermute | solution.py:30
  62.5 4.3 %collective-permute-done.4.refs_5_ = bf16[1024,128]{1,0:T(8,128)(2,1)} collective-permute-done((bf16[1024,128]{1,0:T(8,128)(2,1)}, bf16[1024,128]{1,0:T(8,128)(2,1)}, u32[]{:S(2)}, u32[]{:S(2)}) %collective-permute-start.4) | collective-permute-done | bytes 262176 | tf_op jit(solution)/shard_map/ppermute | solution.py:30
  69.8 1.3 copy-done.2
  71.1 3.6 %in_ring_order.1.refs_16_ = bf16[2048,512]{1,0:T(8,128)(2,1)} custom-call(s32[8]{0:T(128)} %stack.52.place_ref, bf16[8,256,512]{2,1,0:T(8,128)(2,1)} %copy-done.2), custom_call_target="tpu_custom_call" | custom-call | bytes 4194304 | tf_op jit(solution)/shard_map/in_ring_order/pallas_call | solution.py:450
  74.8 6.9 %output_part.1 = (bf16[1024,256]{1,0:T(8,128)(2,1)}, bf16[1024,256]{1,0:T(8,128)(2,1)}) custom-call(s32[1]{0:T(128)} %bitcast.2.places_ref, bf16[1024,128]{1,0:T(8,128)(2,1)} %get-tuple-element.14.refs_0_, bf16[1024,128]{1,0:T(8,128)(2,1)} %get-tuple-element.16.refs_1_, bf16[1024,128]{1,0:T(8,128)(2,1)} %copy-done.20, bf16[1024,128]{1,0:T(8,128)(2,1)} %copy-done.22, ...), custom_call_target="tpu_custom_call" | custom-call | flops 2000000000 | bytes 8000000 | tf_op jit(solution)/shard_map/output_part/pallas_call | solution.py:219
  81.8 3.2 %collective-permute-start.21 = (bf16[1024,256]{1,0:T(8,128)(2,1)}, bf16[1024,256]{1,0:T(8,128)(2,1)S(1)}, u32[]{:S(2)}, u32[]{:S(2)}) collective-permute-start(bf16[1024,256]{1,0:T(8,128)(2,1)} %get-tuple-element.19.refs_0_), channel_id=1, source_target_pairs={{0,6},{2,0},{4,2},{6,4},{1,7},{3,1},{5,3},{7,5},{8,14},{10,8},{12,... | collective-permute-start | bytes 1572872 | tf_op jit(solution)/shard_map/ppermute | solution.py:30
  85.3 12.3 %collective-permute-done.14.refs_4_ = bf16[1024,256]{1,0:T(8,128)(2,1)S(1)} collective-permute-done((bf16[1024,256]{1,0:T(8,128)(2,1)}, bf16[1024,256]{1,0:T(8,128)(2,1)S(1)}, u32[]{:S(2)}, u32[]{:S(2)}) %collective-permute-start.14) | collective-permute-done | bytes 524320 | tf_op jit(solution)/shard_map/ppermute | solution.py:30
  97.6 10.6 %collective-permute-done.15.refs_9_ = bf16[1024,256]{1,0:T(8,128)(2,1)S(1)} collective-permute-done((bf16[1024,256]{1,0:T(8,128)(2,1)}, bf16[1024,256]{1,0:T(8,128)(2,1)S(1)}, u32[]{:S(2)}, u32[]{:S(2)}) %collective-permute-start.15) | collective-permute-done | bytes 524320 | tf_op jit(solution)/shard_map/ppermute | solution.py:30
  108.2 2.1 collective-permute-start.24
  110.5 1.9 collective-permute-start.25
  113.0 11.8 %collective-permute-done.18.refs_5_ = bf16[1024,256]{1,0:T(8,128)(2,1)S(1)} collective-permute-done((bf16[1024,256]{1,0:T(8,128)(2,1)}, bf16[1024,256]{1,0:T(8,128)(2,1)S(1)}, u32[]{:S(2)}, u32[]{:S(2)}) %collective-permute-start.18) | collective-permute-done | bytes 524320 | tf_op jit(solution)/shard_map/ppermute | solution.py:30
  124.8 10.1 %collective-permute-done.24.refs_12_ = bf16[1024,256]{1,0:T(8,128)(2,1)S(1)} collective-permute-done((bf16[1024,256]{1,0:T(8,128)(2,1)S(1)}, bf16[1024,256]{1,0:T(8,128)(2,1)S(1)}, u32[]{:S(2)}, u32[]{:S(2)}) %collective-permute-start.24) | collective-permute-done | bytes 524320 | tf_op jit(solution)/shard_map/ppermute | solution.py:30
  136.8 0.7 collective-permute-done.20.refs_7_
  139.2 0.8 copy-done.16
  139.9 8.7 %assemble.1 = (bf16[1024,4096]{1,0:T(8,128)(2,1)}, f32[1024,128]{1,0:T(8,128)}) custom-call(bf16[1024,256]{1,0:T(8,128)(2,1)} %get-tuple-element.19.refs_0_, bf16[1024,256]{1,0:T(8,128)(2,1)} %get-tuple-element.21.refs_1_, bf16[1024,256]{1,0:T(8,128)(2,1)} %copy-done.5, bf16[1024,256]{1,0:T(8,128)(2,1)} %copy-done.8, bf16[1024,256]{1,0:T(8,128)(2,1)} %copy-done.3, ...), custom_call_target="tpu_custom_call" | custom-call | flops 16777216 | bytes 16777216 | tf_op jit(solution)/shard_map/assemble/pallas_call | solution.py:260
  148.7 1.0 tile.15.label_s
  149.7 29.4 %vocab_stats.1 = f32[8,1024]{1,0:T(8,128)} custom-call(s32[2]{0:T(128)} %pad_add_fusion.first_ref, bf16[1024,4096]{1,0:T(8,128)(2,1)} %get-tuple-element.24.rows_ref, f32[1024,128]{1,0:T(8,128)} %get-tuple-element.25.scale_s, s32[1024,128]{1,0:T(8,128)} %tile.15.label_s, bf16[4,4096,512]{2,1,0:T(8,128)(2,1)} %bitcast.52), custom_call_target="tpu_custom_call" | custom-call | flops 17179869184 | bytes 25165824 | tf_op jit(solution)/shard_map/vocab_stats/pallas_call | solution.py:350
  179.2 0.8 slice_bitcast_fusion
  179.9 12.7 %all-gather.1 = f32[8,2,1024]{2,1,0:T(2,128)S(1)} all-gather(f32[1,2,1024]{2,1,0:T(2,128)S(1)} %slice_bitcast_fusion), channel_id=2, replica_groups=mesh['prompt'=4,'dp'=4,'mp_0'=4,'mp_1'=2] {'mp_0','mp_1'}, dimensions={0}, use_global_device_ids=true | all-gather | bytes 73728 | tf_op jit(solution)/shard_map/all_gather | solution.py:505
  193.6 14.2 %all_to_all.11 = f32[16,1,9]{2,1,0:T(1,128)S(1)} all-to-all(f32[16,1,9]{2,1,0:T(1,128)S(1)} %broadcast_in_dim.38), channel_id=1, replica_groups=mesh['prompt'=4,'dp'=4,'mp_0'=4,'mp_1'=2] {'prompt','dp'}, dimensions={0} | all-to-all | bytes 1152 | tf_op jit(solution)/shard_map/all_to_all | solution.py:24
  208.4 1.1 multiply_divide_fusion
  (118 shorter events, 10.7 us)
Async XLA Ops:
  7.2 61.1 %copy-start = (s32[1,512]{1,0:T(1,128)S(1)}, s32[1,512]{1,0:T(1,128)}, u32[]{:S(2)}) copy-start(s32[1,512]{1,0:T(1,128)} %param.15) | copy-start | bytes 6148
  7.2 141.5 %all-gather.4.cloned.1.call-start = ((), (), s32[]{:S(2)}) async-start(), calls=%async_computation.2 | async-start | bytes 17825792 | tf_op jit(solution)/shard_map/all_gather | solution.py:486
  13.4 56.4 %all-to-all-start = ((bf16[8,256,512]{2,1,0:T(8,128)(2,1)}), bf16[8,256,512]{2,1,0:T(8,128)(2,1)S(1)}, u32[]{:S(2)}, u32[]{:S(2)}) async-start(bf16[8,256,512]{2,1,0:T(8,128)(2,1)} %split_columns.1), calls=%async_computation | async-start | bytes 4194304 | tf_op jit(solution)/shard_map/all_to_all | solution.py:489
  38.6 13.0 %collective-permute-start = (bf16[1024,128]{1,0:T(8,128)(2,1)}, bf16[1024,128]{1,0:T(8,128)(2,1)S(1)}, u32[]{:S(2)}, u32[]{:S(2)}) collective-permute-start(bf16[1024,128]{1,0:T(8,128)(2,1)} %get-tuple-element.14.refs_0_), channel_id=1, source_target_pairs={{0,2},{2,4},{4,6},{6,0},{1,3},{3,5},{5,7},{7,1},{8,10},{10,12},{12... | collective-permute-start | bytes 786440 | tf_op jit(solution)/shard_map/ppermute | solution.py:30
  40.6 11.0 %collective-permute-start.1 = (bf16[1024,128]{1,0:T(8,128)(2,1)}, bf16[1024,128]{1,0:T(8,128)(2,1)S(1)}, u32[]{:S(2)}, u32[]{:S(2)}) collective-permute-start(bf16[1024,128]{1,0:T(8,128)(2,1)} %get-tuple-element.16.refs_1_), channel_id=1, source_target_pairs={{0,6},{2,0},{4,2},{6,4},{1,7},{3,1},{5,3},{7,5},{8,14},{10,8},{12,... | collective-permute-start | bytes 786440 | tf_op jit(solution)/shard_map/ppermute | solution.py:30
  41.9 14.3 %collective-permute-start.7 = (bf16[1024,128]{1,0:T(8,128)(2,1)}, bf16[1024,128]{1,0:T(8,128)(2,1)S(1)}, u32[]{:S(2)}, u32[]{:S(2)}) collective-permute-start(bf16[1024,128]{1,0:T(8,128)(2,1)} %get-tuple-element.14.refs_0_), channel_id=1, source_target_pairs={{0,6},{2,0},{4,2},{6,4},{1,7},{3,1},{5,3},{7,5},{8,14},{10,8},{12,... | collective-permute-start | bytes 786440 | tf_op jit(solution)/shard_map/ppermute | solution.py:30
  43.8 12.3 %collective-permute-start.2 = (bf16[1024,128]{1,0:T(8,128)(2,1)}, bf16[1024,128]{1,0:T(8,128)(2,1)S(1)}, u32[]{:S(2)}, u32[]{:S(2)}) collective-permute-start(bf16[1024,128]{1,0:T(8,128)(2,1)} %get-tuple-element.14.refs_0_), channel_id=1, source_target_pairs={{0,1},{1,0},{2,3},{3,2},{4,5},{5,4},{6,7},{7,6},{8,9},{9,8},{10,11... | collective-permute-start | bytes 786440 | tf_op jit(solution)/shard_map/ppermute | solution.py:30
  51.6 10.4 %collective-permute-start.10 = (bf16[1024,128]{1,0:T(8,128)(2,1)S(1)}, bf16[1024,128]{1,0:T(8,128)(2,1)S(1)}, u32[]{:S(2)}, u32[]{:S(2)}) collective-permute-start(bf16[1024,128]{1,0:T(8,128)(2,1)S(1)} %collective-permute-done.refs_4_), channel_id=1, source_target_pairs={{0,2},{2,4},{4,6},{6,0},{1,3},{3,5},{5,7},{7,1},{8,10},{10,12},{12... | collective-permute-start | bytes 786440 | tf_op jit(solution)/shard_map/ppermute | solution.py:30
  52.2 9.8 %collective-permute-start.11 = (bf16[1024,128]{1,0:T(8,128)(2,1)S(1)}, bf16[1024,128]{1,0:T(8,128)(2,1)}, u32[]{:S(2)}, u32[]{:S(2)}) collective-permute-start(bf16[1024,128]{1,0:T(8,128)(2,1)S(1)} %collective-permute-done.1.refs_9_), channel_id=1, source_target_pairs={{0,6},{2,0},{4,2},{6,4},{1,7},{3,1},{5,3},{7,5},{8,14},{10,8},{12,... | collective-permute-start | bytes 786440 | tf_op jit(solution)/shard_map/ppermute | solution.py:30
  54.9 12.0 %collective-permute-start.4 = (bf16[1024,128]{1,0:T(8,128)(2,1)}, bf16[1024,128]{1,0:T(8,128)(2,1)}, u32[]{:S(2)}, u32[]{:S(2)}) collective-permute-start(bf16[1024,128]{1,0:T(8,128)(2,1)} %get-tuple-element.16.refs_1_), channel_id=1, source_target_pairs={{0,2},{2,4},{4,6},{6,0},{1,3},{3,5},{5,7},{7,1},{8,10},{10,12},{12... | collective-permute-start | bytes 786440 | tf_op jit(solution)/shard_map/ppermute | solution.py:30
  56.2 10.7 %collective-permute-start.3 = (bf16[1024,128]{1,0:T(8,128)(2,1)}, bf16[1024,128]{1,0:T(8,128)(2,1)S(1)}, u32[]{:S(2)}, u32[]{:S(2)}) collective-permute-start(bf16[1024,128]{1,0:T(8,128)(2,1)} %get-tuple-element.16.refs_1_), channel_id=1, source_target_pairs={{0,1},{1,0},{2,3},{3,2},{4,5},{5,4},{6,7},{7,6},{8,9},{9,8},{10,11... | collective-permute-start | bytes 786440 | tf_op jit(solution)/shard_map/ppermute | solution.py:30
  56.2 11.2 %collective-permute-start.5 = (bf16[1024,128]{1,0:T(8,128)(2,1)S(1)}, bf16[1024,128]{1,0:T(8,128)(2,1)S(1)}, u32[]{:S(2)}, u32[]{:S(2)}) collective-permute-start(bf16[1024,128]{1,0:T(8,128)(2,1)S(1)} %collective-permute-done.refs_4_), channel_id=1, source_target_pairs={{0,1},{1,0},{2,3},{3,2},{4,5},{5,4},{6,7},{7,6},{8,9},{9,8},{10,11... | collective-permute-start | bytes 786440 | tf_op jit(solution)/shard_map/ppermute | solution.py:30
  62.0 12.7 %collective-permute-start.9 = (bf16[1024,128]{1,0:T(8,128)(2,1)S(1)}, bf16[1024,128]{1,0:T(8,128)(2,1)}, u32[]{:S(2)}, u32[]{:S(2)}) collective-permute-start(bf16[1024,128]{1,0:T(8,128)(2,1)S(1)} %collective-permute-done.1.refs_9_), channel_id=1, source_target_pairs={{0,1},{1,0},{2,3},{3,2},{4,5},{5,4},{6,7},{7,6},{8,9},{9,8},{10,11... | collective-permute-start | bytes 786440 | tf_op jit(solution)/shard_map/ppermute | solution.py:30
  62.0 12.7 %collective-permute-start.8 = (bf16[1024,128]{1,0:T(8,128)(2,1)S(1)}, bf16[1024,128]{1,0:T(8,128)(2,1)}, u32[]{:S(2)}, u32[]{:S(2)}) collective-permute-start(bf16[1024,128]{1,0:T(8,128)(2,1)S(1)} %collective-permute-done.7.refs_8_), channel_id=1, source_target_pairs={{0,1},{1,0},{2,3},{3,2},{4,5},{5,4},{6,7},{7,6},{8,9},{9,8},{10,11... | collective-permute-start | bytes 786440 | tf_op jit(solution)/shard_map/ppermute | solution.py:30
  66.9 7.9 %collective-permute-start.12 = (bf16[1024,128]{1,0:T(8,128)(2,1)S(1)}, bf16[1024,128]{1,0:T(8,128)(2,1)}, u32[]{:S(2)}, u32[]{:S(2)}) collective-permute-start(bf16[1024,128]{1,0:T(8,128)(2,1)S(1)} %collective-permute-done.10.refs_12_), channel_id=1, source_target_pairs={{0,1},{1,0},{2,3},{3,2},{4,5},{5,4},{6,7},{7,6},{8,9},{9,8},{10,11... | collective-permute-start | bytes 786440 | tf_op jit(solution)/shard_map/ppermute | solution.py:30
  66.9 7.9 %collective-permute-start.13 = (bf16[1024,128]{1,0:T(8,128)(2,1)}, bf16[1024,128]{1,0:T(8,128)(2,1)}, u32[]{:S(2)}, u32[]{:S(2)}) collective-permute-start(bf16[1024,128]{1,0:T(8,128)(2,1)} %collective-permute-done.11.refs_13_), channel_id=1, source_target_pairs={{0,1},{1,0},{2,3},{3,2},{4,5},{5,4},{6,7},{7,6},{8,9},{9,8},{10,11... | collective-permute-start | bytes 786440 | tf_op jit(solution)/shard_map/ppermute | solution.py:30
  67.6 7.2 %collective-permute-start.6 = (bf16[1024,128]{1,0:T(8,128)(2,1)}, bf16[1024,128]{1,0:T(8,128)(2,1)}, u32[]{:S(2)}, u32[]{:S(2)}) collective-permute-start(bf16[1024,128]{1,0:T(8,128)(2,1)} %collective-permute-done.4.refs_5_), channel_id=1, source_target_pairs={{0,1},{1,0},{2,3},{3,2},{4,5},{5,4},{6,7},{7,6},{8,9},{9,8},{10,11... | collective-permute-start | bytes 786440 | tf_op jit(solution)/shard_map/ppermute | solution.py:30
  81.7 15.9 %collective-permute-start.14 = (bf16[1024,256]{1,0:T(8,128)(2,1)}, bf16[1024,256]{1,0:T(8,128)(2,1)S(1)}, u32[]{:S(2)}, u32[]{:S(2)}) collective-permute-start(bf16[1024,256]{1,0:T(8,128)(2,1)} %get-tuple-element.19.refs_0_), channel_id=1, source_target_pairs={{0,2},{2,4},{4,6},{6,0},{1,3},{3,5},{5,7},{7,1},{8,10},{10,12},{12... | collective-permute-start | bytes 1572872 | tf_op jit(solution)/shard_map/ppermute | solution.py:30
  81.8 28.5 %collective-permute-start.21 = (bf16[1024,256]{1,0:T(8,128)(2,1)}, bf16[1024,256]{1,0:T(8,128)(2,1)S(1)}, u32[]{:S(2)}, u32[]{:S(2)}) collective-permute-start(bf16[1024,256]{1,0:T(8,128)(2,1)} %get-tuple-element.19.refs_0_), channel_id=1, source_target_pairs={{0,6},{2,0},{4,2},{6,4},{1,7},{3,1},{5,3},{7,5},{8,14},{10,8},{12,... | collective-permute-start | bytes 1572872 | tf_op jit(solution)/shard_map/ppermute | solution.py:30
  85.0 25.5 %collective-permute-start.16 = (bf16[1024,256]{1,0:T(8,128)(2,1)}, bf16[1024,256]{1,0:T(8,128)(2,1)S(1)}, u32[]{:S(2)}, u32[]{:S(2)}) collective-permute-start(bf16[1024,256]{1,0:T(8,128)(2,1)} %get-tuple-element.19.refs_0_), channel_id=1, source_target_pairs={{0,1},{1,0},{2,3},{3,2},{4,5},{5,4},{6,7},{7,6},{8,9},{9,8},{10,11... | collective-permute-start | bytes 1572872 | tf_op jit(solution)/shard_map/ppermute | solution.py:30
  85.0 23.2 %collective-permute-start.15 = (bf16[1024,256]{1,0:T(8,128)(2,1)}, bf16[1024,256]{1,0:T(8,128)(2,1)S(1)}, u32[]{:S(2)}, u32[]{:S(2)}) collective-permute-start(bf16[1024,256]{1,0:T(8,128)(2,1)} %get-tuple-element.21.refs_1_), channel_id=1, source_target_pairs={{0,6},{2,0},{4,2},{6,4},{1,7},{3,1},{5,3},{7,5},{8,14},{10,8},{12,... | collective-permute-start | bytes 1572872 | tf_op jit(solution)/shard_map/ppermute | solution.py:30
  108.2 16.6 %collective-permute-start.18 = (bf16[1024,256]{1,0:T(8,128)(2,1)}, bf16[1024,256]{1,0:T(8,128)(2,1)S(1)}, u32[]{:S(2)}, u32[]{:S(2)}) collective-permute-start(bf16[1024,256]{1,0:T(8,128)(2,1)} %get-tuple-element.21.refs_1_), channel_id=1, source_target_pairs={{0,2},{2,4},{4,6},{6,0},{1,3},{3,5},{5,7},{7,1},{8,10},{10,12},{12... | collective-permute-start | bytes 1572872 | tf_op jit(solution)/shard_map/ppermute | solution.py:30
  108.2 27.2 %collective-permute-start.17 = (bf16[1024,256]{1,0:T(8,128)(2,1)}, bf16[1024,256]{1,0:T(8,128)(2,1)S(1)}, u32[]{:S(2)}, u32[]{:S(2)}) collective-permute-start(bf16[1024,256]{1,0:T(8,128)(2,1)} %get-tuple-element.21.refs_1_), channel_id=1, source_target_pairs={{0,1},{1,0},{2,3},{3,2},{4,5},{5,4},{6,7},{7,6},{8,9},{9,8},{10,11... | collective-permute-start | bytes 1572872 | tf_op jit(solution)/shard_map/ppermute | solution.py:30
  108.2 26.7 %collective-permute-start.24 = (bf16[1024,256]{1,0:T(8,128)(2,1)S(1)}, bf16[1024,256]{1,0:T(8,128)(2,1)S(1)}, u32[]{:S(2)}, u32[]{:S(2)}) collective-permute-start(bf16[1024,256]{1,0:T(8,128)(2,1)S(1)} %collective-permute-done.14.refs_4_), channel_id=1, source_target_pairs={{0,2},{2,4},{4,6},{6,0},{1,3},{3,5},{5,7},{7,1},{8,10},{10,12},{12... | collective-permute-start | bytes 1572872 | tf_op jit(solution)/shard_map/ppermute | solution.py:30
  110.3 25.2 %collective-permute-start.19 = (bf16[1024,256]{1,0:T(8,128)(2,1)S(1)}, bf16[1024,256]{1,0:T(8,128)(2,1)S(1)}, u32[]{:S(2)}, u32[]{:S(2)}) collective-permute-start(bf16[1024,256]{1,0:T(8,128)(2,1)S(1)} %collective-permute-done.14.refs_4_), channel_id=1, source_target_pairs={{0,1},{1,0},{2,3},{3,2},{4,5},{5,4},{6,7},{7,6},{8,9},{9,8},{10,11... | collective-permute-start | bytes 1572872 | tf_op jit(solution)/shard_map/ppermute | solution.py:30
  110.5 24.4 %collective-permute-start.25 = (bf16[1024,256]{1,0:T(8,128)(2,1)S(1)}, bf16[1024,256]{1,0:T(8,128)(2,1)S(1)}, u32[]{:S(2)}, u32[]{:S(2)}) collective-permute-start(bf16[1024,256]{1,0:T(8,128)(2,1)S(1)} %collective-permute-done.15.refs_9_), channel_id=1, source_target_pairs={{0,6},{2,0},{4,2},{6,4},{1,7},{3,1},{5,3},{7,5},{8,14},{10,8},{12,... | collective-permute-start | bytes 1572872 | tf_op jit(solution)/shard_map/ppermute | solution.py:30
  124.8 11.8 %collective-permute-start.23 = (bf16[1024,256]{1,0:T(8,128)(2,1)S(1)}, bf16[1024,256]{1,0:T(8,128)(2,1)S(1)}, u32[]{:S(2)}, u32[]{:S(2)}) collective-permute-start(bf16[1024,256]{1,0:T(8,128)(2,1)S(1)} %collective-permute-done.15.refs_9_), channel_id=1, source_target_pairs={{0,1},{1,0},{2,3},{3,2},{4,5},{5,4},{6,7},{7,6},{8,9},{9,8},{10,11... | collective-permute-start | bytes 1572872 | tf_op jit(solution)/shard_map/ppermute | solution.py:30
  134.9 1.9 collective-permute-start.22
  134.9 2.6 %collective-permute-start.20 = (bf16[1024,256]{1,0:T(8,128)(2,1)S(1)}, bf16[1024,256]{1,0:T(8,128)(2,1)S(1)}, u32[]{:S(2)}, u32[]{:S(2)}) collective-permute-start(bf16[1024,256]{1,0:T(8,128)(2,1)S(1)} %collective-permute-done.18.refs_5_), channel_id=1, source_target_pairs={{0,1},{1,0},{2,3},{3,2},{4,5},{5,4},{6,7},{7,6},{8,9},{9,8},{10,11... | collective-permute-start | bytes 1572872 | tf_op jit(solution)/shard_map/ppermute | solution.py:30
  135.4 2.9 %collective-permute-start.26 = (bf16[1024,256]{1,0:T(8,128)(2,1)S(1)}, bf16[1024,256]{1,0:T(8,128)(2,1)S(1)}, u32[]{:S(2)}, u32[]{:S(2)}) collective-permute-start(bf16[1024,256]{1,0:T(8,128)(2,1)S(1)} %collective-permute-done.24.refs_12_), channel_id=1, source_target_pairs={{0,1},{1,0},{2,3},{3,2},{4,5},{5,4},{6,7},{7,6},{8,9},{9,8},{10,11... | collective-permute-start | bytes 1572872 | tf_op jit(solution)/shard_map/ppermute | solution.py:30
  135.5 3.5 %collective-permute-start.27 = (bf16[1024,256]{1,0:T(8,128)(2,1)S(1)}, bf16[1024,256]{1,0:T(8,128)(2,1)S(1)}, u32[]{:S(2)}, u32[]{:S(2)}) collective-permute-start(bf16[1024,256]{1,0:T(8,128)(2,1)S(1)} %collective-permute-done.25.refs_13_), channel_id=1, source_target_pairs={{0,1},{1,0},{2,3},{3,2},{4,5},{5,4},{6,7},{7,6},{8,9},{9,8},{10,11... | collective-permute-start | bytes 1572872 | tf_op jit(solution)/shard_map/ppermute | solution.py:30
  149.7 59.7 %copy-start.1 = (s32[1,512]{1,0:T(1,128)S(1)}, s32[1,512]{1,0:T(1,128)}, u32[]{:S(2)}) copy-start(s32[1,512]{1,0:T(1,128)} %param.15) | copy-start | bytes 6148
  (23 other events, 314.1 us)
Sparse Core Ops, SparseCore 0:
  10.8 113.6 all-gather.3

commit v4 on v3

--- a/solution.py
+++ b/solution.py
@@ -33,11 +33,10 @@
 def ring_pairs(left, right, axis):
     left_before = shifted(left, axis, 1)
     right_after = shifted(right, axis, -1)
-    right, left_before, right_after = lax.optimization_barrier((right, left_before, right_after))
+    right_before = shifted(right, axis, 1)
+    left_after = shifted(left, axis, -1)
     left_far = shifted(left_before, axis, 1)
     right_far = shifted(right_after, axis, -1)
-    right_before = shifted(right, axis, 1)
-    left_after = shifted(left, axis, -1)
     return [
         (left, right),
         (left_before, right_before),
@@ -239,67 +238,33 @@
     )(place, *contexts, out_cols, target_embed, final_gain.reshape(1, -1))
 
 
-def assemble_kernel(*refs):
-    *row_refs, degain_ref, rows_ref, scale_ref = refs
-    tile, width = rows_ref.shape
-    squares = jnp.zeros((tile, 128), jnp.float32)
-    k = 0
-    for ref in row_refs:
-        rows_ref[:, k : k + ref.shape[1]] = ref[...]
-        for i in range(0, ref.shape[1], 128):
-            x = ref[:, i : i + 128].astype(jnp.float32) * degain_ref[:, k + i : k + i + 128]
-            squares += x * x
-        k += ref.shape[1]
-    mean = jnp.sum(squares, axis=1, keepdims=True) / width
-    scale_ref[...] = jnp.broadcast_to(lax.rsqrt(mean + EPSILON) * LOG2E, scale_ref.shape)
-
-
-def assemble(row_blocks, degain):
-    rows, width, tile = row_blocks[0].shape[0], degain.shape[1], 256
-    by_tile = lambda columns: pl.BlockSpec((tile, columns), lambda i: (i, 0))
-    return pl.pallas_call(
-        assemble_kernel,
-        out_shape=[
-            jax.ShapeDtypeStruct((rows, width), jnp.bfloat16),
-            jax.ShapeDtypeStruct((rows, 128), jnp.float32),
-        ],
-        grid=(rows // tile,),
-        in_specs=[
-            *(by_tile(b.shape[1]) for b in row_blocks),
-            pl.BlockSpec(degain.shape, lambda i: (0, 0)),
-        ],
-        out_specs=[by_tile(width), by_tile(128)],
-        compiler_params=pltpu.CompilerParams(vmem_limit_bytes=VMEM_LIMIT),
-        cost_estimate=pl.CostEstimate(
-            flops=4 * rows * width, bytes_accessed=4 * rows * width, transcendentals=0
-        ),
-        name="assemble",
-    )(*row_blocks, degain)
-
-
-def vocab_kernel(
-    first_ref, rows_ref, scale_s, label_s, w_ref, out_ref,
-    rows_s, first_s, second_s, top_s, sum_s, pick_s, sem,
-):
+def vocab_kernel(first_ref, *refs, n_rows):
+    row_refs = refs[:n_rows]
+    degain_ref, label_s, w_ref, out_ref = refs[n_rows : n_rows + 4]
+    rows_s, first_s, second_s, top_s, sum_s, pick_s, scale_s = refs[n_rows + 4 :]
     step = pl.program_id(0)
+    n_steps = pl.num_programs(0)
     rows, width = rows_s.shape
     tile, columns = first_s.shape
     n_tiles = rows // tile
     at_tile = lambda t: slice(t * tile, (t + 1) * tile)
-    arrivals = [
-        pltpu.make_async_copy(rows_ref.at[at_tile(t)], rows_s.at[at_tile(t)], sem.at[t])
-        for t in range(n_tiles)
-    ]
+    lane = lax.broadcasted_iota(jnp.int32, (1, 128), 1)
 
     @pl.when(step == 0)
     def _():
-        for copy in arrivals:
-            copy.start()
+        squares = jnp.zeros((rows, 128), jnp.float32)
+        k = 0
+        for ref in row_refs:
+            rows_s[:, k : k + ref.shape[1]] = ref[...]
+            for i in range(0, ref.shape[1], 128):
+                x = ref[:, i : i + 128].astype(jnp.float32) * degain_ref[:, k + i : k + i + 128]
+                squares += x * x
+            k += ref.shape[1]
+        mean = jnp.sum(squares, axis=1, keepdims=True) / width
+        scale_s[...] = jnp.broadcast_to(lax.rsqrt(mean + EPSILON) * LOG2E, scale_s.shape)
         top_s[...] = jnp.full_like(top_s, MASKED)
         sum_s[...] = jnp.zeros_like(sum_s)
         pick_s[...] = jnp.zeros_like(pick_s)
-
-    lane = lax.broadcasted_iota(jnp.int32, (1, 128), 1)
 
     def take(at, product_ref, first_column):
         scale = scale_s[at, :]
@@ -321,18 +286,13 @@
     first_column = first_ref[0] + step * first_ref[1]
     products = (first_s, second_s)
     for t in range(n_tiles):
-
-        @pl.when(step == 0)
-        def _():
-            arrivals[t].wait()
-
         product = jnp.dot(rows_s[at_tile(t), :], w_ref[0], preferred_element_type=jnp.float32)
         if t:
             take(at_tile(t - 1), products[(t + 1) % 2], first_column)
         products[t % 2][...] = product
     take(at_tile(n_tiles - 1), products[(n_tiles + 1) % 2], first_column)
 
-    @pl.when(step == pl.num_programs(0) - 1)
+    @pl.when(step == n_steps - 1)
     def _():
         top = jnp.max(top_s[...], axis=1, keepdims=True)
         total = jnp.sum(sum_s[...] * jnp.exp2(top_s[...] - top), axis=1, keepdims=True)
@@ -342,29 +302,29 @@
         out_ref[...] = both.T[:8, :]
 
 
-def vocab_stats(first, rows, scale, row_labels, vocab_all):
-    n_rows, width = rows.shape
-    n_blocks, _, columns = vocab_all.shape
+def vocab_stats(first, row_blocks, degain, row_labels, vocab_all):
+    n_rows = row_blocks[0].shape[0]
+    n_blocks, width, columns = vocab_all.shape
     tile = 256
-    whole = lambda shape: pl.BlockSpec(shape, lambda j, f: (0, 0))
+    whole = lambda a: pl.BlockSpec(a.shape, lambda j, f: (0, 0), pipeline_mode=pl.Buffered(1))
+    kernel = lambda *refs: vocab_kernel(*refs, n_rows=len(row_blocks))
     return pl.pallas_call(
-        vocab_kernel,
+        kernel,
         out_shape=jax.ShapeDtypeStruct((8, n_rows), jnp.float32),
         grid_spec=pltpu.PrefetchScalarGridSpec(
             num_scalar_prefetch=1,
             grid=(n_blocks,),
             in_specs=[
-                pl.BlockSpec(memory_space=pl.ANY),
-                whole(scale.shape),
-                whole(row_labels.shape),
+                *(whole(b) for b in row_blocks),
+                whole(degain),
+                whole(row_labels),
                 pl.BlockSpec((1, width, columns), lambda j, f: (j, 0, 0)),
             ],
-            out_specs=whole((8, n_rows)),
+            out_specs=pl.BlockSpec((8, n_rows), lambda j, f: (0, 0)),
             scratch_shapes=[
                 pltpu.VMEM((n_rows, width), jnp.bfloat16),
                 *(pltpu.VMEM((tile, columns), jnp.float32) for _ in range(2)),
-                *(pltpu.VMEM((n_rows, 128), jnp.float32) for _ in range(3)),
-                pltpu.SemaphoreType.DMA((n_rows // tile,)),
+                *(pltpu.VMEM((n_rows, 128), jnp.float32) for _ in range(4)),
             ],
         ),
         compiler_params=pltpu.CompilerParams(vmem_limit_bytes=VMEM_LIMIT),
@@ -374,7 +334,7 @@
             transcendentals=n_rows * n_blocks * columns,
         ),
         name="vocab_stats",
-    )(first, rows, scale, row_labels, vocab_all)
+    )(first, *row_blocks, degain, row_labels, vocab_all)
 
 
 def piece_kernel(row_ref, vocab_ref, piece_ref, sem):
@@ -498,9 +458,8 @@
         [lax.dynamic_slice_in_dim(final_gain, p * part, part, 0) for p in places], axis=0
     ).reshape(1, -1)
     row_labels = jnp.tile(labels.reshape(-1, 1), (prompts_here, 128))
-    rows, scale = assemble(row_blocks, degain)
     first = jnp.stack([lax.axis_index(MP) * vocab_cols, n_model * vocab_cols]).astype(jnp.int32)
-    here = vocab_stats(first, rows, scale, row_labels, vocab_all)[:2]
+    here = vocab_stats(first, row_blocks, degain, row_labels, vocab_all)[:2]
 
     every = lax.all_gather(here, MP)
     top_val = jnp.max(every[:, 0], axis=0)

time: 217 us -> 192 us (0.88)
  waiting for transfers between devices: 66 us -> 48.2 us
  Pallas kernels: 70.4 us -> 61.7 us
  starting transfers between devices: 24.8 us -> 27.1 us
    ppermute x28, waiting for transfers between devices: 65.9 us -> 46.2 us  [shifted(): return lax.ppermute(value, axis, [(i, (i + shift) % n) for i in range(n)])]
    pallas_call x2 -> x1, Pallas kernels: 38.1 us -> 29.4 us  [vocab_stats(): pl.pallas_call(kernel, out_shape=jax.ShapeDtypeStruct((8, n_rows), jnp.fl...]
    ppermute x28, starting transfers between devices: 19.3 us -> 21.6 us  [shifted(): return lax.ppermute(value, axis, [(i, (i + shift) % n) for i in range(n)])]
    unnamed x61 -> x57, local copies, waits for them, and re-layouts: 6.98 us -> 7.02 us
  transfers between devices with their start and end apart: 30 -> 30, of which waited for: 12 -> 12; matrix products, arithmetic and copies ran while one was open for 3% -> 3% of each run, Pallas kernels for 18% -> 15%
where the time goes in v4:
time: 192 us; the launch traced here: 191 us
  Pallas kernels  61.7 us (32%)
  waiting for transfers between devices  48.2 us (25%)
  starting transfers between devices  27.1 us (14%)
  blocking collectives  25.8 us (13%)
  between operations  15.2 us (8%)
  local copies, waits for them, and re-layouts  9.43 us (5%)
  other arithmetic  3.9 us (2%)
    ppermute x28, waiting for transfers between devices, shifted(): return lax.ppermute(value, axis, [(i, (i + shift) % n) for i in range(n)])  46.2 us
    pallas_call x1, Pallas kernels, vocab_stats(): pl.pallas_call(kernel, out_shape=jax.ShapeDtypeStruct((8, n_rows), jnp.fl...  29.4 us
    ppermute x28, starting transfers between devices, shifted(): return lax.ppermute(value, axis, [(i, (i + shift) % n) for i in range(n)])  21.6 us
    pallas_call x1, Pallas kernels, attention(): pl.pallas_call(attention_kernel, out_shape=[jax.ShapeDtypeStruct((rows, i...  16.2 us
    all_gather x1, blocking collectives, shards(): every = lax.all_gather(here, MP)  13.2 us
    all_to_all x1, blocking collectives, of_everyone(): lax.all_to_all(copies, axis, split_axis=0, concat_axis=0, tiled=True)  12.6 us
    unnamed x57, local copies, waits for them, and re-layouts  7.02 us
    pallas_call x1, Pallas kernels, output_part(): pl.pallas_call(output_kernel, out_shape=[jax.ShapeDtypeStruct((rows, part...  6.8 us
  transfers between devices with their start and end apart: 30, of which 12 were waited for; matrix products, arithmetic and copies ran while one was open for 3% of the time, Pallas kernels for 15%

profile of v4, /device:TPU:0, one launch (start us, length us, event | category | flops | bytes accessed | tf_op | source)
XLA Modules:
  0.0 191.2 jit_solution(13941999606154393684)
XLA Ops:
  7.9 2.9 %vocab_piece.1 = bf16[1024,512]{1,0:T(8,128)(2,1)} custom-call(s32[2]{0:T(128)} %pad_add_fusion.1.row_ref, bf16[4096,512]{1,0:T(8,128)(2,1)} %vocab_ref.1), custom_call_target="tpu_custom_call" | custom-call | bytes 2097152 | tf_op jit(solution)/shard_map/vocab_piece/pallas_call | solution.py:357
  10.8 2.7 %split_columns.1 = bf16[8,256,512]{2,1,0:T(8,128)(2,1)} custom-call(bf16[256,4096]{1,0:T(8,128)(2,1)} %w_ref.3), custom_call_target="tpu_custom_call" | custom-call | bytes 4194304 | tf_op jit(solution)/shard_map/split_columns/pallas_call | solution.py:382
  13.5 5.4 %all-to-all-start = ((bf16[8,256,512]{2,1,0:T(8,128)(2,1)}), bf16[8,256,512]{2,1,0:T(8,128)(2,1)S(1)}, u32[]{:S(2)}, u32[]{:S(2)}) async-start(bf16[8,256,512]{2,1,0:T(8,128)(2,1)} %split_columns.1), calls=%async_computation | async-start | bytes 4194304 | tf_op jit(solution)/shard_map/all_to_all | solution.py:449
  18.9 3.6 %copy.20.prompt_ref = bf16[2,100,4096]{2,1,0:T(8,128)(2,1)} copy(bf16[2,100,4096]{2,0,1:T(2,128)(2,1)} %param.13) | data formatting | bytes 3276800 | tf_op args[0]
  22.5 16.2 %attention.1 = (bf16[1024,128]{1,0:T(8,128)(2,1)}, bf16[1024,128]{1,0:T(8,128)(2,1)}) custom-call(bf16[1,512,4096]{2,1,0:T(8,128)(2,1)} %refs_17_.1, bf16[2,100,4096]{2,1,0:T(8,128)(2,1)} %copy.20.prompt_ref, f32[1,4096]{1,0:T(1,128)} %bitcast.53, bf16[3,4096,256]{2,1,0:T(8,128)(2,1)} %w_ref.2, f32[512,64]{1,0:T(8,128)} %constant.102.clone.cos_t, ...), custom_call_target="tpu_custom_call" | custom-call | flops 8000000000 | bytes 12000000 | tf_op jit(solution)/shard_map/attention/pallas_call | solution.py:169
  38.7 3.2 %collective-permute-start.6 = (bf16[1024,128]{1,0:T(8,128)(2,1)}, bf16[1024,128]{1,0:T(8,128)(2,1)S(1)}, u32[]{:S(2)}, u32[]{:S(2)}) collective-permute-start(bf16[1024,128]{1,0:T(8,128)(2,1)} %get-tuple-element.6.refs_0_), channel_id=1, source_target_pairs={{0,6},{2,0},{4,2},{6,4},{1,7},{3,1},{5,3},{7,5},{8,14},{10,8},{12,... | collective-permute-start | bytes 786440 | tf_op jit(solution)/shard_map/ppermute | solution.py:30
  41.9 3.2 %collective-permute-start.7 = (bf16[1024,128]{1,0:T(8,128)(2,1)}, bf16[1024,128]{1,0:T(8,128)(2,1)S(1)}, u32[]{:S(2)}, u32[]{:S(2)}) collective-permute-start(bf16[1024,128]{1,0:T(8,128)(2,1)} %get-tuple-element.7.refs_1_), channel_id=1, source_target_pairs={{0,6},{2,0},{4,2},{6,4},{1,7},{3,1},{5,3},{7,5},{8,14},{10,8},{12,... | collective-permute-start | bytes 786440 | tf_op jit(solution)/shard_map/ppermute | solution.py:30
  45.2 5.5 %collective-permute-done.6.refs_8_ = bf16[1024,128]{1,0:T(8,128)(2,1)S(1)} collective-permute-done((bf16[1024,128]{1,0:T(8,128)(2,1)}, bf16[1024,128]{1,0:T(8,128)(2,1)S(1)}, u32[]{:S(2)}, u32[]{:S(2)}) %collective-permute-start.6) | collective-permute-done | bytes 262176 | tf_op jit(solution)/shard_map/ppermute | solution.py:30
  50.7 1.9 collective-permute-done.2.refs_4_
  52.8 3.0 %collective-permute-done.7.refs_9_ = bf16[1024,128]{1,0:T(8,128)(2,1)S(1)} collective-permute-done((bf16[1024,128]{1,0:T(8,128)(2,1)}, bf16[1024,128]{1,0:T(8,128)(2,1)S(1)}, u32[]{:S(2)}, u32[]{:S(2)}) %collective-permute-start.7) | collective-permute-done | bytes 262176 | tf_op jit(solution)/shard_map/ppermute | solution.py:30
  55.8 2.7 %collective-permute-start.11 = (bf16[1024,128]{1,0:T(8,128)(2,1)S(1)}, bf16[1024,128]{1,0:T(8,128)(2,1)}, u32[]{:S(2)}, u32[]{:S(2)}) collective-permute-start(bf16[1024,128]{1,0:T(8,128)(2,1)S(1)} %collective-permute-done.7.refs_9_), channel_id=1, source_target_pairs={{0,6},{2,0},{4,2},{6,4},{1,7},{3,1},{5,3},{7,5},{8,14},{10,8},{12,... | collective-permute-start | bytes 786440 | tf_op jit(solution)/shard_map/ppermute | solution.py:30
  59.1 4.0 %collective-permute-done.10.refs_12_ = bf16[1024,128]{1,0:T(8,128)(2,1)} collective-permute-done((bf16[1024,128]{1,0:T(8,128)(2,1)S(1)}, bf16[1024,128]{1,0:T(8,128)(2,1)}, u32[]{:S(2)}, u32[]{:S(2)}) %collective-permute-start.10) | collective-permute-done | bytes 262176 | tf_op jit(solution)/shard_map/ppermute | solution.py:30
  63.1 1.4 collective-permute-done.11.refs_13_
  66.2 1.3 copy-done.1
  67.5 3.6 %in_ring_order.1.refs_16_ = bf16[2048,512]{1,0:T(8,128)(2,1)} custom-call(s32[8]{0:T(128)} %stack.52.place_ref, bf16[8,256,512]{2,1,0:T(8,128)(2,1)} %copy-done.1), custom_call_target="tpu_custom_call" | custom-call | bytes 4194304 | tf_op jit(solution)/shard_map/in_ring_order/pallas_call | solution.py:410
  71.3 6.8 %output_part.1 = (bf16[1024,256]{1,0:T(8,128)(2,1)}, bf16[1024,256]{1,0:T(8,128)(2,1)}) custom-call(s32[1]{0:T(128)} %bitcast.2.places_ref, bf16[1024,128]{1,0:T(8,128)(2,1)} %get-tuple-element.6.refs_0_, bf16[1024,128]{1,0:T(8,128)(2,1)} %get-tuple-element.7.refs_1_, bf16[1024,128]{1,0:T(8,128)(2,1)} %copy-done.4, bf16[1024,128]{1,0:T(8,128)(2,1)} %copy-done.7, ...), custom_call_target="tpu_custom_call" | custom-call | flops 2000000000 | bytes 8000000 | tf_op jit(solution)/shard_map/output_part/pallas_call | solution.py:218
  78.1 3.6 %collective-permute-start.20 = (bf16[1024,256]{1,0:T(8,128)(2,1)}, bf16[1024,256]{1,0:T(8,128)(2,1)S(1)}, u32[]{:S(2)}, u32[]{:S(2)}) collective-permute-start(bf16[1024,256]{1,0:T(8,128)(2,1)} %get-tuple-element.8.refs_1_), channel_id=1, source_target_pairs={{0,6},{2,0},{4,2},{6,4},{1,7},{3,1},{5,3},{7,5},{8,14},{10,8},{12,... | collective-permute-start | bytes 1572872 | tf_op jit(solution)/shard_map/ppermute | solution.py:30
  81.8 3.1 %collective-permute-start.21 = (bf16[1024,256]{1,0:T(8,128)(2,1)}, bf16[1024,256]{1,0:T(8,128)(2,1)S(1)}, u32[]{:S(2)}, u32[]{:S(2)}) collective-permute-start(bf16[1024,256]{1,0:T(8,128)(2,1)} %get-tuple-element.9.refs_2_), channel_id=1, source_target_pairs={{0,6},{2,0},{4,2},{6,4},{1,7},{3,1},{5,3},{7,5},{8,14},{10,8},{12,... | collective-permute-start | bytes 1572872 | tf_op jit(solution)/shard_map/ppermute | solution.py:30
  85.0 9.2 %collective-permute-done.20.refs_9_ = bf16[1024,256]{1,0:T(8,128)(2,1)S(1)} collective-permute-done((bf16[1024,256]{1,0:T(8,128)(2,1)}, bf16[1024,256]{1,0:T(8,128)(2,1)S(1)}, u32[]{:S(2)}, u32[]{:S(2)}) %collective-permute-start.20) | collective-permute-done | bytes 524320 | tf_op jit(solution)/shard_map/ppermute | solution.py:30
  94.2 3.6 %collective-permute-done.16.refs_5_ = bf16[1024,256]{1,0:T(8,128)(2,1)S(1)} collective-permute-done((bf16[1024,256]{1,0:T(8,128)(2,1)}, bf16[1024,256]{1,0:T(8,128)(2,1)S(1)}, u32[]{:S(2)}, u32[]{:S(2)}) %collective-permute-start.16) | collective-permute-done | bytes 524320 | tf_op jit(solution)/shard_map/ppermute | solution.py:30
  97.9 7.0 %collective-permute-done.21.refs_10_ = bf16[1024,256]{1,0:T(8,128)(2,1)S(1)} collective-permute-done((bf16[1024,256]{1,0:T(8,128)(2,1)}, bf16[1024,256]{1,0:T(8,128)(2,1)S(1)}, u32[]{:S(2)}, u32[]{:S(2)}) %collective-permute-start.21) | collective-permute-done | bytes 524320 | tf_op jit(solution)/shard_map/ppermute | solution.py:30
  105.0 3.6 %collective-permute-start.25 = (bf16[1024,256]{1,0:T(8,128)(2,1)S(1)}, bf16[1024,256]{1,0:T(8,128)(2,1)S(1)}, u32[]{:S(2)}, u32[]{:S(2)}) collective-permute-start(bf16[1024,256]{1,0:T(8,128)(2,1)S(1)} %collective-permute-done.21.refs_10_), channel_id=1, source_target_pairs={{0,6},{2,0},{4,2},{6,4},{1,7},{3,1},{5,3},{7,5},{8,14},{10,8},{12,... | collective-permute-start | bytes 1572872 | tf_op jit(solution)/shard_map/ppermute | solution.py:30
  109.9 9.6 %collective-permute-done.24.refs_13_ = bf16[1024,256]{1,0:T(8,128)(2,1)S(1)} collective-permute-done((bf16[1024,256]{1,0:T(8,128)(2,1)S(1)}, bf16[1024,256]{1,0:T(8,128)(2,1)S(1)}, u32[]{:S(2)}, u32[]{:S(2)}) %collective-permute-start.24) | collective-permute-done | bytes 524320 | tf_op jit(solution)/shard_map/ppermute | solution.py:30
  120.7 0.7 collective-permute-done.26.refs_15_
  121.8 0.8 copy-done.22
  122.6 2.0 %all-gather.4.cloned.1.call-done = bf16[16384,512]{1,0:T(8,128)(2,1)} async-done(((bf16[1024,512]{1,0:T(8,128)(2,1)}), bf16[16384,512]{1,0:T(8,128)(2,1)}) %all-gather.4.cloned.1.call-update) | async-done | bytes 16777232 | tf_op jit(solution)/shard_map/all_gather | solution.py:446
  124.6 1.0 tile.15.refs_18_
  125.6 29.4 %vocab_stats.1 = f32[8,1024]{1,0:T(8,128)} custom-call(s32[2]{0:T(128)} %pad_add_fusion.refs_0_, bf16[1024,256]{1,0:T(8,128)(2,1)} %get-tuple-element.8.refs_1_, bf16[1024,256]{1,0:T(8,128)(2,1)} %get-tuple-element.9.refs_2_, bf16[1024,256]{1,0:T(8,128)(2,1)} %copy-done.12, bf16[1024,256]{1,0:T(8,128)(2,1)} %copy-done.15, bf16[1024,256]{1,0:T(8,128)(2,1)} %copy-done.11, ...), custom_call_target="tpu_custom_call" | custom-call | flops 17179869184 | bytes 25165824 | tf_op jit(solution)/shard_map/vocab_stats/pallas_call | solution.py:311
  155.1 0.8 slice_bitcast_fusion
  155.9 13.2 %all-gather.1 = f32[8,2,1024]{2,1,0:T(2,128)S(1)} all-gather(f32[1,2,1024]{2,1,0:T(2,128)S(1)} %slice_bitcast_fusion), channel_id=2, replica_groups=mesh['prompt'=4,'dp'=4,'mp_0'=4,'mp_1'=2] {'mp_0','mp_1'}, dimensions={0}, use_global_device_ids=true | all-gather | bytes 73728 | tf_op jit(solution)/shard_map/all_gather | solution.py:464
  170.0 12.6 %all_to_all.11 = f32[16,1,9]{2,1,0:T(1,128)S(1)} all-to-all(f32[16,1,9]{2,1,0:T(1,128)S(1)} %broadcast_in_dim.38), channel_id=1, replica_groups=mesh['prompt'=4,'dp'=4,'mp_0'=4,'mp_1'=2] {'prompt','dp'}, dimensions={0} | all-to-all | bytes 1152 | tf_op jit(solution)/shard_map/all_to_all | solution.py:24
  183.2 1.1 multiply_divide_fusion
  (113 shorter events, 7.2 us)
Async XLA Ops:
  7.2 57.4 %copy-start = (s32[1,512]{1,0:T(1,128)S(1)}, s32[1,512]{1,0:T(1,128)}, u32[]{:S(2)}) copy-start(s32[1,512]{1,0:T(1,128)} %param.15) | copy-start | bytes 6148
  7.2 117.4 %all-gather.4.cloned.1.call-start = ((), (), s32[]{:S(2)}) async-start(), calls=%async_computation.2 | async-start | bytes 17825792 | tf_op jit(solution)/shard_map/all_gather | solution.py:446
  13.5 52.7 %all-to-all-start = ((bf16[8,256,512]{2,1,0:T(8,128)(2,1)}), bf16[8,256,512]{2,1,0:T(8,128)(2,1)S(1)}, u32[]{:S(2)}, u32[]{:S(2)}) async-start(bf16[8,256,512]{2,1,0:T(8,128)(2,1)} %split_columns.1), calls=%async_computation | async-start | bytes 4194304 | tf_op jit(solution)/shard_map/all_to_all | solution.py:449
  22.5 43.6 %copy-start.9 = (f32[4096]{0:T(1024)S(1)}, f32[4096]{0:T(1024)}, u32[]{:S(2)}) copy-start(f32[4096]{0:T(1024)} %param.20) | copy-start | bytes 49156
  38.7 11.9 %collective-permute-start.6 = (bf16[1024,128]{1,0:T(8,128)(2,1)}, bf16[1024,128]{1,0:T(8,128)(2,1)S(1)}, u32[]{:S(2)}, u32[]{:S(2)}) collective-permute-start(bf16[1024,128]{1,0:T(8,128)(2,1)} %get-tuple-element.6.refs_0_), channel_id=1, source_target_pairs={{0,6},{2,0},{4,2},{6,4},{1,7},{3,1},{5,3},{7,5},{8,14},{10,8},{12,... | collective-permute-start | bytes 786440 | tf_op jit(solution)/shard_map/ppermute | solution.py:30
  41.9 10.6 %collective-permute-start.2 = (bf16[1024,128]{1,0:T(8,128)(2,1)}, bf16[1024,128]{1,0:T(8,128)(2,1)S(1)}, u32[]{:S(2)}, u32[]{:S(2)}) collective-permute-start(bf16[1024,128]{1,0:T(8,128)(2,1)} %get-tuple-element.6.refs_0_), channel_id=1, source_target_pairs={{0,2},{2,4},{4,6},{6,0},{1,3},{3,5},{5,7},{7,1},{8,10},{10,12},{12... | collective-permute-start | bytes 786440 | tf_op jit(solution)/shard_map/ppermute | solution.py:30
  41.9 10.6 %collective-permute-start = (bf16[1024,128]{1,0:T(8,128)(2,1)}, bf16[1024,128]{1,0:T(8,128)(2,1)S(1)}, u32[]{:S(2)}, u32[]{:S(2)}) collective-permute-start(bf16[1024,128]{1,0:T(8,128)(2,1)} %get-tuple-element.6.refs_0_), channel_id=1, source_target_pairs={{0,1},{1,0},{2,3},{3,2},{4,5},{5,4},{6,7},{7,6},{8,9},{9,8},{10,11... | collective-permute-start | bytes 786440 | tf_op jit(solution)/shard_map/ppermute | solution.py:30
  41.9 13.9 %collective-permute-start.7 = (bf16[1024,128]{1,0:T(8,128)(2,1)}, bf16[1024,128]{1,0:T(8,128)(2,1)S(1)}, u32[]{:S(2)}, u32[]{:S(2)}) collective-permute-start(bf16[1024,128]{1,0:T(8,128)(2,1)} %get-tuple-element.7.refs_1_), channel_id=1, source_target_pairs={{0,6},{2,0},{4,2},{6,4},{1,7},{3,1},{5,3},{7,5},{8,14},{10,8},{12,... | collective-permute-start | bytes 786440 | tf_op jit(solution)/shard_map/ppermute | solution.py:30
  45.2 13.3 %collective-permute-start.3 = (bf16[1024,128]{1,0:T(8,128)(2,1)}, bf16[1024,128]{1,0:T(8,128)(2,1)S(1)}, u32[]{:S(2)}, u32[]{:S(2)}) collective-permute-start(bf16[1024,128]{1,0:T(8,128)(2,1)} %get-tuple-element.7.refs_1_), channel_id=1, source_target_pairs={{0,2},{2,4},{4,6},{6,0},{1,3},{3,5},{5,7},{7,1},{8,10},{10,12},{12... | collective-permute-start | bytes 786440 | tf_op jit(solution)/shard_map/ppermute | solution.py:30
  50.7 7.8 %collective-permute-start.1 = (bf16[1024,128]{1,0:T(8,128)(2,1)}, bf16[1024,128]{1,0:T(8,128)(2,1)S(1)}, u32[]{:S(2)}, u32[]{:S(2)}) collective-permute-start(bf16[1024,128]{1,0:T(8,128)(2,1)} %get-tuple-element.7.refs_1_), channel_id=1, source_target_pairs={{0,1},{1,0},{2,3},{3,2},{4,5},{5,4},{6,7},{7,6},{8,9},{9,8},{10,11... | collective-permute-start | bytes 786440 | tf_op jit(solution)/shard_map/ppermute | solution.py:30
  52.5 6.5 %collective-permute-start.8 = (bf16[1024,128]{1,0:T(8,128)(2,1)S(1)}, bf16[1024,128]{1,0:T(8,128)(2,1)S(1)}, u32[]{:S(2)}, u32[]{:S(2)}) collective-permute-start(bf16[1024,128]{1,0:T(8,128)(2,1)S(1)} %collective-permute-done.6.refs_8_), channel_id=1, source_target_pairs={{0,1},{1,0},{2,3},{3,2},{4,5},{5,4},{6,7},{7,6},{8,9},{9,8},{10,11... | collective-permute-start | bytes 786440 | tf_op jit(solution)/shard_map/ppermute | solution.py:30
  52.6 10.6 %collective-permute-start.10 = (bf16[1024,128]{1,0:T(8,128)(2,1)S(1)}, bf16[1024,128]{1,0:T(8,128)(2,1)}, u32[]{:S(2)}, u32[]{:S(2)}) collective-permute-start(bf16[1024,128]{1,0:T(8,128)(2,1)S(1)} %collective-permute-done.2.refs_4_), channel_id=1, source_target_pairs={{0,2},{2,4},{4,6},{6,0},{1,3},{3,5},{5,7},{7,1},{8,10},{10,12},{12... | collective-permute-start | bytes 786440 | tf_op jit(solution)/shard_map/ppermute | solution.py:30
  55.8 8.8 %collective-permute-start.11 = (bf16[1024,128]{1,0:T(8,128)(2,1)S(1)}, bf16[1024,128]{1,0:T(8,128)(2,1)}, u32[]{:S(2)}, u32[]{:S(2)}) collective-permute-start(bf16[1024,128]{1,0:T(8,128)(2,1)S(1)} %collective-permute-done.7.refs_9_), channel_id=1, source_target_pairs={{0,6},{2,0},{4,2},{6,4},{1,7},{3,1},{5,3},{7,5},{8,14},{10,8},{12,... | collective-permute-start | bytes 786440 | tf_op jit(solution)/shard_map/ppermute | solution.py:30
  58.5 12.7 %collective-permute-start.4 = (bf16[1024,128]{1,0:T(8,128)(2,1)S(1)}, bf16[1024,128]{1,0:T(8,128)(2,1)}, u32[]{:S(2)}, u32[]{:S(2)}) collective-permute-start(bf16[1024,128]{1,0:T(8,128)(2,1)S(1)} %collective-permute-done.2.refs_4_), channel_id=1, source_target_pairs={{0,1},{1,0},{2,3},{3,2},{4,5},{5,4},{6,7},{7,6},{8,9},{9,8},{10,11... | collective-permute-start | bytes 786440 | tf_op jit(solution)/shard_map/ppermute | solution.py:30
  58.5 12.7 %collective-permute-start.9 = (bf16[1024,128]{1,0:T(8,128)(2,1)S(1)}, bf16[1024,128]{1,0:T(8,128)(2,1)}, u32[]{:S(2)}, u32[]{:S(2)}) collective-permute-start(bf16[1024,128]{1,0:T(8,128)(2,1)S(1)} %collective-permute-done.7.refs_9_), channel_id=1, source_target_pairs={{0,1},{1,0},{2,3},{3,2},{4,5},{5,4},{6,7},{7,6},{8,9},{9,8},{10,11... | collective-permute-start | bytes 786440 | tf_op jit(solution)/shard_map/ppermute | solution.py:30
  59.0 12.2 %collective-permute-start.5 = (bf16[1024,128]{1,0:T(8,128)(2,1)S(1)}, bf16[1024,128]{1,0:T(8,128)(2,1)}, u32[]{:S(2)}, u32[]{:S(2)}) collective-permute-start(bf16[1024,128]{1,0:T(8,128)(2,1)S(1)} %collective-permute-done.3.refs_5_), channel_id=1, source_target_pairs={{0,1},{1,0},{2,3},{3,2},{4,5},{5,4},{6,7},{7,6},{8,9},{9,8},{10,11... | collective-permute-start | bytes 786440 | tf_op jit(solution)/shard_map/ppermute | solution.py:30
  63.1 8.1 %collective-permute-start.12 = (bf16[1024,128]{1,0:T(8,128)(2,1)}, bf16[1024,128]{1,0:T(8,128)(2,1)}, u32[]{:S(2)}, u32[]{:S(2)}) collective-permute-start(bf16[1024,128]{1,0:T(8,128)(2,1)} %collective-permute-done.10.refs_12_), channel_id=1, source_target_pairs={{0,1},{1,0},{2,3},{3,2},{4,5},{5,4},{6,7},{7,6},{8,9},{9,8},{10,11... | collective-permute-start | bytes 786440 | tf_op jit(solution)/shard_map/ppermute | solution.py:30
  64.6 6.6 %collective-permute-start.13 = (bf16[1024,128]{1,0:T(8,128)(2,1)}, bf16[1024,128]{1,0:T(8,128)(2,1)}, u32[]{:S(2)}, u32[]{:S(2)}) collective-permute-start(bf16[1024,128]{1,0:T(8,128)(2,1)} %collective-permute-done.11.refs_13_), channel_id=1, source_target_pairs={{0,1},{1,0},{2,3},{3,2},{4,5},{5,4},{6,7},{7,6},{8,9},{9,8},{10,11... | collective-permute-start | bytes 786440 | tf_op jit(solution)/shard_map/ppermute | solution.py:30
  78.1 16.1 %collective-permute-start.20 = (bf16[1024,256]{1,0:T(8,128)(2,1)}, bf16[1024,256]{1,0:T(8,128)(2,1)S(1)}, u32[]{:S(2)}, u32[]{:S(2)}) collective-permute-start(bf16[1024,256]{1,0:T(8,128)(2,1)} %get-tuple-element.8.refs_1_), channel_id=1, source_target_pairs={{0,6},{2,0},{4,2},{6,4},{1,7},{3,1},{5,3},{7,5},{8,14},{10,8},{12,... | collective-permute-start | bytes 1572872 | tf_op jit(solution)/shard_map/ppermute | solution.py:30
  81.6 16.2 %collective-permute-start.16 = (bf16[1024,256]{1,0:T(8,128)(2,1)}, bf16[1024,256]{1,0:T(8,128)(2,1)S(1)}, u32[]{:S(2)}, u32[]{:S(2)}) collective-permute-start(bf16[1024,256]{1,0:T(8,128)(2,1)} %get-tuple-element.8.refs_1_), channel_id=1, source_target_pairs={{0,2},{2,4},{4,6},{6,0},{1,3},{3,5},{5,7},{7,1},{8,10},{10,12},{12... | collective-permute-start | bytes 1572872 | tf_op jit(solution)/shard_map/ppermute | solution.py:30
  81.6 16.2 %collective-permute-start.14 = (bf16[1024,256]{1,0:T(8,128)(2,1)}, bf16[1024,256]{1,0:T(8,128)(2,1)S(1)}, u32[]{:S(2)}, u32[]{:S(2)}) collective-permute-start(bf16[1024,256]{1,0:T(8,128)(2,1)} %get-tuple-element.8.refs_1_), channel_id=1, source_target_pairs={{0,1},{1,0},{2,3},{3,2},{4,5},{5,4},{6,7},{7,6},{8,9},{9,8},{10,11... | collective-permute-start | bytes 1572872 | tf_op jit(solution)/shard_map/ppermute | solution.py:30
  81.8 23.2 %collective-permute-start.21 = (bf16[1024,256]{1,0:T(8,128)(2,1)}, bf16[1024,256]{1,0:T(8,128)(2,1)S(1)}, u32[]{:S(2)}, u32[]{:S(2)}) collective-permute-start(bf16[1024,256]{1,0:T(8,128)(2,1)} %get-tuple-element.9.refs_2_), channel_id=1, source_target_pairs={{0,6},{2,0},{4,2},{6,4},{1,7},{3,1},{5,3},{7,5},{8,14},{10,8},{12,... | collective-permute-start | bytes 1572872 | tf_op jit(solution)/shard_map/ppermute | solution.py:30
  84.9 24.3 %collective-permute-start.17 = (bf16[1024,256]{1,0:T(8,128)(2,1)}, bf16[1024,256]{1,0:T(8,128)(2,1)S(1)}, u32[]{:S(2)}, u32[]{:S(2)}) collective-permute-start(bf16[1024,256]{1,0:T(8,128)(2,1)} %get-tuple-element.9.refs_2_), channel_id=1, source_target_pairs={{0,2},{2,4},{4,6},{6,0},{1,3},{3,5},{5,7},{7,1},{8,10},{10,12},{12... | collective-permute-start | bytes 1572872 | tf_op jit(solution)/shard_map/ppermute | solution.py:30
  94.2 15.1 %collective-permute-start.15 = (bf16[1024,256]{1,0:T(8,128)(2,1)}, bf16[1024,256]{1,0:T(8,128)(2,1)S(1)}, u32[]{:S(2)}, u32[]{:S(2)}) collective-permute-start(bf16[1024,256]{1,0:T(8,128)(2,1)} %get-tuple-element.9.refs_2_), channel_id=1, source_target_pairs={{0,1},{1,0},{2,3},{3,2},{4,5},{5,4},{6,7},{7,6},{8,9},{9,8},{10,11... | collective-permute-start | bytes 1572872 | tf_op jit(solution)/shard_map/ppermute | solution.py:30
  97.8 12.0 %collective-permute-start.22 = (bf16[1024,256]{1,0:T(8,128)(2,1)S(1)}, bf16[1024,256]{1,0:T(8,128)(2,1)S(1)}, u32[]{:S(2)}, u32[]{:S(2)}) collective-permute-start(bf16[1024,256]{1,0:T(8,128)(2,1)S(1)} %collective-permute-done.20.refs_9_), channel_id=1, source_target_pairs={{0,1},{1,0},{2,3},{3,2},{4,5},{5,4},{6,7},{7,6},{8,9},{9,8},{10,11... | collective-permute-start | bytes 1572872 | tf_op jit(solution)/shard_map/ppermute | solution.py:30
  97.8 21.7 %collective-permute-start.24 = (bf16[1024,256]{1,0:T(8,128)(2,1)S(1)}, bf16[1024,256]{1,0:T(8,128)(2,1)S(1)}, u32[]{:S(2)}, u32[]{:S(2)}) collective-permute-start(bf16[1024,256]{1,0:T(8,128)(2,1)S(1)} %collective-permute-done.16.refs_5_), channel_id=1, source_target_pairs={{0,2},{2,4},{4,6},{6,0},{1,3},{3,5},{5,7},{7,1},{8,10},{10,12},{12... | collective-permute-start | bytes 1572872 | tf_op jit(solution)/shard_map/ppermute | solution.py:30
  105.0 14.7 %collective-permute-start.25 = (bf16[1024,256]{1,0:T(8,128)(2,1)S(1)}, bf16[1024,256]{1,0:T(8,128)(2,1)S(1)}, u32[]{:S(2)}, u32[]{:S(2)}) collective-permute-start(bf16[1024,256]{1,0:T(8,128)(2,1)S(1)} %collective-permute-done.21.refs_10_), channel_id=1, source_target_pairs={{0,6},{2,0},{4,2},{6,4},{1,7},{3,1},{5,3},{7,5},{8,14},{10,8},{12,... | collective-permute-start | bytes 1572872 | tf_op jit(solution)/shard_map/ppermute | solution.py:30
  109.2 11.5 %collective-permute-start.18 = (bf16[1024,256]{1,0:T(8,128)(2,1)S(1)}, bf16[1024,256]{1,0:T(8,128)(2,1)S(1)}, u32[]{:S(2)}, u32[]{:S(2)}) collective-permute-start(bf16[1024,256]{1,0:T(8,128)(2,1)S(1)} %collective-permute-done.16.refs_5_), channel_id=1, source_target_pairs={{0,1},{1,0},{2,3},{3,2},{4,5},{5,4},{6,7},{7,6},{8,9},{9,8},{10,11... | collective-permute-start | bytes 1572872 | tf_op jit(solution)/shard_map/ppermute | solution.py:30
  109.3 11.4 %collective-permute-start.23 = (bf16[1024,256]{1,0:T(8,128)(2,1)S(1)}, bf16[1024,256]{1,0:T(8,128)(2,1)S(1)}, u32[]{:S(2)}, u32[]{:S(2)}) collective-permute-start(bf16[1024,256]{1,0:T(8,128)(2,1)S(1)} %collective-permute-done.21.refs_10_), channel_id=1, source_target_pairs={{0,1},{1,0},{2,3},{3,2},{4,5},{5,4},{6,7},{7,6},{8,9},{9,8},{10,11... | collective-permute-start | bytes 1572872 | tf_op jit(solution)/shard_map/ppermute | solution.py:30
  109.8 10.9 %collective-permute-start.19 = (bf16[1024,256]{1,0:T(8,128)(2,1)S(1)}, bf16[1024,256]{1,0:T(8,128)(2,1)S(1)}, u32[]{:S(2)}, u32[]{:S(2)}) collective-permute-start(bf16[1024,256]{1,0:T(8,128)(2,1)S(1)} %collective-permute-done.17.refs_6_), channel_id=1, source_target_pairs={{0,1},{1,0},{2,3},{3,2},{4,5},{5,4},{6,7},{7,6},{8,9},{9,8},{10,11... | collective-permute-start | bytes 1572872 | tf_op jit(solution)/shard_map/ppermute | solution.py:30
  119.5 1.9 collective-permute-start.26
  119.6 3.0 %collective-permute-start.27 = (bf16[1024,256]{1,0:T(8,128)(2,1)S(1)}, bf16[1024,256]{1,0:T(8,128)(2,1)}, u32[]{:S(2)}, u32[]{:S(2)}) collective-permute-start(bf16[1024,256]{1,0:T(8,128)(2,1)S(1)} %collective-permute-done.25.refs_14_), channel_id=1, source_target_pairs={{0,1},{1,0},{2,3},{3,2},{4,5},{5,4},{6,7},{7,6},{8,9},{9,8},{10,11... | collective-permute-start | bytes 1572872 | tf_op jit(solution)/shard_map/ppermute | solution.py:30
  (21 other events, 257.9 us)
Sparse Core Ops, SparseCore 0:
  10.9 113.6 all-gather.3

commit v5 on v3

--- a/solution.py
+++ b/solution.py
@@ -33,11 +33,10 @@
 def ring_pairs(left, right, axis):
     left_before = shifted(left, axis, 1)
     right_after = shifted(right, axis, -1)
-    right, left_before, right_after = lax.optimization_barrier((right, left_before, right_after))
+    right_before = shifted(right, axis, 1)
+    left_after = shifted(left, axis, -1)
     left_far = shifted(left_before, axis, 1)
     right_far = shifted(right_after, axis, -1)
-    right_before = shifted(right, axis, 1)
-    left_after = shifted(left, axis, -1)
     return [
         (left, right),
         (left_before, right_before),
@@ -163,7 +162,7 @@
     n_prompts, prompt_len, width = prompts.shape
     target_len = target_embed.shape[1]
     inner = w_qkv.shape[2]
-    chunk = 512
+    chunk = 1024
     tables = (*rope_tables(target_len, prompt_len), *rope_tables(prompt_len, 0))
     whole = lambda shape: pl.BlockSpec(shape, lambda k: (0,) * len(shape))
     rows = n_prompts * target_len
@@ -196,26 +195,22 @@
 
 
 def output_kernel(places_ref, *refs):
-    *ctx_refs, w_ref, embed_ref, gain_ref, left_ref, right_ref, ctx_s = refs
-    at = 0
-    for ref in ctx_refs:
-        ctx_s[:, at : at + ref.shape[1]] = ref[...]
-        at += ref.shape[1]
-
-    total = embed_ref[0].astype(jnp.float32) + jnp.dot(
-        ctx_s[...], w_ref[...], preferred_element_type=jnp.float32
-    )
+    *ctx_refs, w_ref, embed_ref, gain_ref, left_ref, right_ref = refs
+    total = embed_ref[0].astype(jnp.float32)
+    for group in range(w_ref.shape[0]):
+        both = jnp.concatenate([ref[...] for ref in ctx_refs[2 * group : 2 * group + 2]], axis=1)
+        total += jnp.dot(both, w_ref[places_ref[group]], preferred_element_type=jnp.float32)
     scaled = (total * gain_ref[...]).astype(jnp.bfloat16)
     half = scaled.shape[1] // 2
     left_ref[...] = scaled[:, :half]
     right_ref[...] = scaled[:, half:]
 
 
-def output_part(place, contexts, out_cols, target_embed, final_gain):
+def output_part(places, contexts, out_cols, target_embed, final_gain):
     rows = contexts[0].shape[0]
-    inner, part = out_cols.shape
+    part = out_cols.shape[2]
     target_len = target_embed.shape[1]
-    tile = target_len // 2
+    tile = target_len
     return pl.pallas_call(
         output_kernel,
         out_shape=[jax.ShapeDtypeStruct((rows, part // 2), jnp.bfloat16)] * 2,
@@ -224,19 +219,18 @@
             grid=(rows // tile,),
             in_specs=[
                 *(pl.BlockSpec((tile, c.shape[1]), lambda i, at: (i, 0)) for c in contexts),
-                pl.BlockSpec(out_cols.shape, lambda i, at: (0, 0)),
-                pl.BlockSpec((1, tile, part), lambda i, at: (0, i % 2, at[0])),
+                pl.BlockSpec(out_cols.shape, lambda i, at: (0, 0, 0)),
+                pl.BlockSpec((1, tile, part), lambda i, at: (0, 0, at[0])),
                 pl.BlockSpec((1, part), lambda i, at: (0, at[0])),
             ],
             out_specs=[pl.BlockSpec((tile, part // 2), lambda i, at: (i, 0))] * 2,
-            scratch_shapes=[pltpu.VMEM((tile, inner), jnp.bfloat16)],
         ),
         compiler_params=pltpu.CompilerParams(vmem_limit_bytes=VMEM_LIMIT),
         cost_estimate=pl.CostEstimate(
             flops=2 * 10**9, bytes_accessed=8 * 10**6, transcendentals=0
         ),
         name="output_part",
-    )(place, *contexts, out_cols, target_embed, final_gain.reshape(1, -1))
+    )(places, *contexts, out_cols, target_embed, final_gain.reshape(1, -1))
 
 
 def assemble_kernel(*refs):
@@ -278,28 +272,22 @@
 
 
 def vocab_kernel(
-    first_ref, rows_ref, scale_s, label_s, w_ref, out_ref,
-    rows_s, first_s, second_s, top_s, sum_s, pick_s, sem,
+    first_ref, rows_s, scale_s, label_ref, w_ref, out_ref,
+    first_s, second_s, top_s, sum_s, pick_s, label_s,
 ):
     step = pl.program_id(0)
-    rows, width = rows_s.shape
+    rows = rows_s.shape[0]
     tile, columns = first_s.shape
     n_tiles = rows // tile
     at_tile = lambda t: slice(t * tile, (t + 1) * tile)
-    arrivals = [
-        pltpu.make_async_copy(rows_ref.at[at_tile(t)], rows_s.at[at_tile(t)], sem.at[t])
-        for t in range(n_tiles)
-    ]
+    lane = lax.broadcasted_iota(jnp.int32, (1, 128), 1)
 
     @pl.when(step == 0)
     def _():
-        for copy in arrivals:
-            copy.start()
+        label_s[...] = jnp.broadcast_to(label_ref[...], label_s.shape)
         top_s[...] = jnp.full_like(top_s, MASKED)
         sum_s[...] = jnp.zeros_like(sum_s)
         pick_s[...] = jnp.zeros_like(pick_s)
-
-    lane = lax.broadcasted_iota(jnp.int32, (1, 128), 1)
 
     def take(at, product_ref, first_column):
         scale = scale_s[at, :]
@@ -321,11 +309,6 @@
     first_column = first_ref[0] + step * first_ref[1]
     products = (first_s, second_s)
     for t in range(n_tiles):
-
-        @pl.when(step == 0)
-        def _():
-            arrivals[t].wait()
-
         product = jnp.dot(rows_s[at_tile(t), :], w_ref[0], preferred_element_type=jnp.float32)
         if t:
             take(at_tile(t - 1), products[(t + 1) % 2], first_column)
@@ -339,32 +322,31 @@
         total = top * (1.0 / LOG2E) + jnp.log(total)
         pick = jnp.sum(pick_s[...], axis=1, keepdims=True) * (1.0 / LOG2E)
         both = jnp.where(lane == 0, total, jnp.where(lane == 1, pick, 0.0))
-        out_ref[...] = both.T[:8, :]
+        out_ref[...] = both.T[:2, :]
 
 
 def vocab_stats(first, rows, scale, row_labels, vocab_all):
-    n_rows, width = rows.shape
-    n_blocks, _, columns = vocab_all.shape
+    n_rows = rows.shape[0]
+    n_blocks, width, columns = vocab_all.shape
     tile = 256
-    whole = lambda shape: pl.BlockSpec(shape, lambda j, f: (0, 0))
+    whole = lambda a: pl.BlockSpec(a.shape, lambda j, f: (0, 0), pipeline_mode=pl.Buffered(1))
     return pl.pallas_call(
         vocab_kernel,
-        out_shape=jax.ShapeDtypeStruct((8, n_rows), jnp.float32),
+        out_shape=jax.ShapeDtypeStruct((2, n_rows), jnp.float32),
         grid_spec=pltpu.PrefetchScalarGridSpec(
             num_scalar_prefetch=1,
             grid=(n_blocks,),
             in_specs=[
-                pl.BlockSpec(memory_space=pl.ANY),
-                whole(scale.shape),
-                whole(row_labels.shape),
+                whole(rows),
+                whole(scale),
+                whole(row_labels),
                 pl.BlockSpec((1, width, columns), lambda j, f: (j, 0, 0)),
             ],
-            out_specs=whole((8, n_rows)),
+            out_specs=pl.BlockSpec((2, n_rows), lambda j, f: (0, 0)),
             scratch_shapes=[
-                pltpu.VMEM((n_rows, width), jnp.bfloat16),
                 *(pltpu.VMEM((tile, columns), jnp.float32) for _ in range(2)),
                 *(pltpu.VMEM((n_rows, 128), jnp.float32) for _ in range(3)),
-                pltpu.SemaphoreType.DMA((n_rows // tile,)),
+                pltpu.VMEM((n_rows, 128), jnp.int32),
             ],
         ),
         compiler_params=pltpu.CompilerParams(vmem_limit_bytes=VMEM_LIMIT),
@@ -430,39 +412,6 @@
     )(w)
 
 
-def order_kernel(place_ref, in_ref, out_ref, sem):
-    n, width, _ = in_ref.shape
-    started = [
-        pltpu.make_async_copy(
-            in_ref.at[place_ref[i]], out_ref.at[i * width : (i + 1) * width], sem.at[i]
-        )
-        for i in range(n)
-    ]
-    for copy in started:
-        copy.start()
-    for copy in started:
-        copy.wait()
-
-
-def in_ring_order(places, blocks):
-    n, width, part = blocks.shape
-    anywhere = pl.BlockSpec(memory_space=pl.ANY)
-    return pl.pallas_call(
-        order_kernel,
-        out_shape=jax.ShapeDtypeStruct((n * width, part), blocks.dtype),
-        grid_spec=pltpu.PrefetchScalarGridSpec(
-            num_scalar_prefetch=1,
-            grid=(),
-            in_specs=[anywhere],
-            out_specs=pl.BlockSpec(memory_space=pltpu.VMEM),
-            scratch_shapes=[pltpu.SemaphoreType.DMA((n,))],
-        ),
-        compiler_params=pltpu.CompilerParams(vmem_limit_bytes=VMEM_LIMIT),
-        cost_estimate=pl.CostEstimate(flops=0, bytes_accessed=4 << 20, transcendentals=0),
-        name="in_ring_order",
-    )(places, blocks)
-
-
 def shards(prompts, target_embed, labels, lengths, attn_gain, w_qkv, w_out, final_gain, w_vocab):
     n_prompt = lax.axis_size("prompt")
     n_dp = lax.axis_size("dp")
@@ -490,17 +439,16 @@
 
     halves = attention(target_embed, prompts, attn_gain, w_qkv)
     contexts = whole_row(*halves)
-    out_cols = in_ring_order(place_ids, out_cols)
-    halves = output_part(place_ids[:1], contexts, out_cols, target_embed, final_gain)
+    halves = output_part(place_ids, contexts, out_cols, target_embed, final_gain)
     row_blocks = whole_row(*halves)
 
     degain = 1.0 / jnp.concatenate(
         [lax.dynamic_slice_in_dim(final_gain, p * part, part, 0) for p in places], axis=0
     ).reshape(1, -1)
-    row_labels = jnp.tile(labels.reshape(-1, 1), (prompts_here, 128))
+    row_labels = jnp.tile(labels.reshape(-1, 1), (prompts_here, 1))
     rows, scale = assemble(row_blocks, degain)
     first = jnp.stack([lax.axis_index(MP) * vocab_cols, n_model * vocab_cols]).astype(jnp.int32)
-    here = vocab_stats(first, rows, scale, row_labels, vocab_all)[:2]
+    here = vocab_stats(first, rows, scale, row_labels, vocab_all)
 
     every = lax.all_gather(here, MP)
     top_val = jnp.max(every[:, 0], axis=0)

time: 217 us -> 197 us (0.908)
  waiting for transfers between devices: 66 us -> 55.9 us
  Pallas kernels: 70.4 us -> 61.6 us
    ppermute x28, waiting for transfers between devices: 65.9 us -> 55.9 us  [shifted(): return lax.ppermute(value, axis, [(i, (i + shift) % n) for i in range(n)])]
    pallas_call x2 -> x1, Pallas kernels: 33 us -> 26.2 us  [vocab_stats(): pl.pallas_call(vocab_kernel, out_shape=jax.ShapeDtypeStruct((2, n_rows),...]
    unnamed x61 -> x59, local copies, waits for them, and re-layouts: 6.98 us -> 7 us
  transfers between devices with their start and end apart: 30 -> 30, of which waited for: 12 -> 9; matrix products, arithmetic and copies ran while one was open for 3% -> 3% of each run, Pallas kernels for 18% -> 16%
where the time goes in v5:
time: 197 us
  Pallas kernels  61.6 us (31%)
  waiting for transfers between devices  55.9 us (28%)
  blocking collectives  27.1 us (14%)
  starting transfers between devices  24.9 us (13%)
  between operations  15.1 us (8%)
  local copies, waits for them, and re-layouts  8.34 us (4%)
  other arithmetic  4.03 us (2%)
    ppermute x28, waiting for transfers between devices, shifted(): return lax.ppermute(value, axis, [(i, (i + shift) % n) for i in range(n)])  55.9 us
    pallas_call x1, Pallas kernels, vocab_stats(): pl.pallas_call(vocab_kernel, out_shape=jax.ShapeDtypeStruct((2, n_rows),...  26.2 us
    ppermute x28, starting transfers between devices, shifted(): return lax.ppermute(value, axis, [(i, (i + shift) % n) for i in range(n)])  19.5 us
    pallas_call x1, Pallas kernels, attention(): pl.pallas_call(attention_kernel, out_shape=[jax.ShapeDtypeStruct((rows, i...  14.4 us
    all_to_all x1, blocking collectives, of_everyone(): lax.all_to_all(copies, axis, split_axis=0, concat_axis=0, tiled=True)  14.1 us
    all_gather x1, blocking collectives, shards(): every = lax.all_gather(here, MP)  12.9 us
    pallas_call x1, Pallas kernels, assemble(): pl.pallas_call(assemble_kernel, out_shape=[jax.ShapeDtypeStruct((rows, wi...  8.73 us
    unnamed x59, local copies, waits for them, and re-layouts  7 us
  transfers between devices with their start and end apart: 30, of which 9 were waited for; matrix products, arithmetic and copies ran while one was open for 3% of the time, Pallas kernels for 16%

profile of v5, /device:TPU:0, one launch (start us, length us, event | category | flops | bytes accessed | tf_op | source)
XLA Modules:
  0.0 197.0 jit_solution(6668965183409890066)
XLA Ops:
  7.3 0.6 pad_add_fusion.1.row_ref
  7.9 2.9 %vocab_piece.1 = bf16[1024,512]{1,0:T(8,128)(2,1)} custom-call(s32[2]{0:T(128)} %pad_add_fusion.1.row_ref, bf16[4096,512]{1,0:T(8,128)(2,1)} %vocab_ref.1), custom_call_target="tpu_custom_call" | custom-call | bytes 2097152 | tf_op jit(solution)/shard_map/vocab_piece/pallas_call | solution.py:379
  10.8 2.7 %split_columns.1 = bf16[8,256,512]{2,1,0:T(8,128)(2,1)} custom-call(bf16[256,4096]{1,0:T(8,128)(2,1)} %w_ref.3), custom_call_target="tpu_custom_call" | custom-call | bytes 4194304 | tf_op jit(solution)/shard_map/split_columns/pallas_call | solution.py:404
  13.5 5.4 %all-to-all-start = ((bf16[8,256,512]{2,1,0:T(8,128)(2,1)}), bf16[8,256,512]{2,1,0:T(8,128)(2,1)S(1)}, u32[]{:S(2)}, u32[]{:S(2)}) async-start(bf16[8,256,512]{2,1,0:T(8,128)(2,1)} %split_columns.1), calls=%async_computation | async-start | bytes 4194304 | tf_op jit(solution)/shard_map/all_to_all | solution.py:438
  18.9 3.6 %copy.25.prompt_ref = bf16[2,100,4096]{2,1,0:T(8,128)(2,1)} copy(bf16[2,100,4096]{2,0,1:T(2,128)(2,1)} %param.13) | data formatting | bytes 3276800 | tf_op args[0]
  22.4 14.4 %attention.1 = (bf16[1024,128]{1,0:T(8,128)(2,1)}, bf16[1024,128]{1,0:T(8,128)(2,1)}) custom-call(bf16[1,512,4096]{2,1,0:T(8,128)(2,1)} %refs_17_.1, bf16[2,100,4096]{2,1,0:T(8,128)(2,1)} %copy.25.prompt_ref, f32[1,4096]{1,0:T(1,128)} %bitcast.56, bf16[3,4096,256]{2,1,0:T(8,128)(2,1)} %w_ref.2, f32[512,64]{1,0:T(8,128)} %constant.102.clone.cos_t, ...), custom_call_target="tpu_custom_call" | custom-call | flops 8000000000 | bytes 12000000 | tf_op jit(solution)/shard_map/attention/pallas_call | solution.py:169
  36.9 2.0 %collective-permute-start.2 = (bf16[1024,128]{1,0:T(8,128)(2,1)}, bf16[1024,128]{1,0:T(8,128)(2,1)S(1)}, u32[]{:S(2)}, u32[]{:S(2)}) collective-permute-start(bf16[1024,128]{1,0:T(8,128)(2,1)} %get-tuple-element.8.refs_0_), channel_id=1, source_target_pairs={{0,2},{2,4},{4,6},{6,0},{1,3},{3,5},{5,7},{7,1},{8,10},{10,12},{12... | collective-permute-start | bytes 786440 | tf_op jit(solution)/shard_map/ppermute | solution.py:30
  38.9 1.3 collective-permute-start.7
  40.2 0.7 collective-permute-start.3
  40.9 2.5 %collective-permute-start.6 = (bf16[1024,128]{1,0:T(8,128)(2,1)}, bf16[1024,128]{1,0:T(8,128)(2,1)S(1)}, u32[]{:S(2)}, u32[]{:S(2)}) collective-permute-start(bf16[1024,128]{1,0:T(8,128)(2,1)} %get-tuple-element.8.refs_0_), channel_id=1, source_target_pairs={{0,6},{2,0},{4,2},{6,4},{1,7},{3,1},{5,3},{7,5},{8,14},{10,8},{12,... | collective-permute-start | bytes 786440 | tf_op jit(solution)/shard_map/ppermute | solution.py:30
  43.4 8.3 %collective-permute-done.2.refs_4_ = bf16[1024,128]{1,0:T(8,128)(2,1)S(1)} collective-permute-done((bf16[1024,128]{1,0:T(8,128)(2,1)}, bf16[1024,128]{1,0:T(8,128)(2,1)S(1)}, u32[]{:S(2)}, u32[]{:S(2)}) %collective-permute-start.2) | collective-permute-done | bytes 262176 | tf_op jit(solution)/shard_map/ppermute | solution.py:30
  52.3 5.0 %collective-permute-done.3.refs_5_ = bf16[1024,128]{1,0:T(8,128)(2,1)S(1)} collective-permute-done((bf16[1024,128]{1,0:T(8,128)(2,1)}, bf16[1024,128]{1,0:T(8,128)(2,1)S(1)}, u32[]{:S(2)}, u32[]{:S(2)}) %collective-permute-start.3) | collective-permute-done | bytes 262176 | tf_op jit(solution)/shard_map/ppermute | solution.py:30
  57.3 1.0 collective-permute-start.11
  59.0 4.0 %collective-permute-done.10.refs_12_ = bf16[1024,128]{1,0:T(8,128)(2,1)} collective-permute-done((bf16[1024,128]{1,0:T(8,128)(2,1)S(1)}, bf16[1024,128]{1,0:T(8,128)(2,1)}, u32[]{:S(2)}, u32[]{:S(2)}) %collective-permute-start.10) | collective-permute-done | bytes 262176 | tf_op jit(solution)/shard_map/ppermute | solution.py:30
  63.1 2.7 %collective-permute-done.11.refs_13_ = bf16[1024,128]{1,0:T(8,128)(2,1)} collective-permute-done((bf16[1024,128]{1,0:T(8,128)(2,1)S(1)}, bf16[1024,128]{1,0:T(8,128)(2,1)}, u32[]{:S(2)}, u32[]{:S(2)}) %collective-permute-start.11) | collective-permute-done | bytes 262176 | tf_op jit(solution)/shard_map/ppermute | solution.py:30
  66.5 1.0 copy.33
  69.0 1.3 copy-done.1
  70.3 6.6 %output_part.1 = (bf16[1024,256]{1,0:T(8,128)(2,1)}, bf16[1024,256]{1,0:T(8,128)(2,1)}) custom-call(s32[8]{0:T(128)} %stack.52.places_ref, bf16[1024,128]{1,0:T(8,128)(2,1)} %get-tuple-element.8.refs_0_, bf16[1024,128]{1,0:T(8,128)(2,1)} %get-tuple-element.9.refs_1_, bf16[1024,128]{1,0:T(8,128)(2,1)} %copy-done.20, bf16[1024,128]{1,0:T(8,128)(2,1)} %copy-done.21, ...), custom_call_target="tpu_custom_call" | custom-call | flops 2000000000 | bytes 8000000 | tf_op jit(solution)/shard_map/output_part/pallas_call | solution.py:214
  77.0 1.7 collective-permute-start.21
  79.1 3.2 %collective-permute-start.20 = (bf16[1024,256]{1,0:T(8,128)(2,1)}, bf16[1024,256]{1,0:T(8,128)(2,1)S(1)}, u32[]{:S(2)}, u32[]{:S(2)}) collective-permute-start(bf16[1024,256]{1,0:T(8,128)(2,1)} %get-tuple-element.10.refs_0_), channel_id=1, source_target_pairs={{0,6},{2,0},{4,2},{6,4},{1,7},{3,1},{5,3},{7,5},{8,14},{10,8},{12,... | collective-permute-start | bytes 1572872 | tf_op jit(solution)/shard_map/ppermute | solution.py:30
  82.4 22.9 %collective-permute-done.16.refs_4_ = bf16[1024,256]{1,0:T(8,128)(2,1)S(1)} collective-permute-done((bf16[1024,256]{1,0:T(8,128)(2,1)}, bf16[1024,256]{1,0:T(8,128)(2,1)S(1)}, u32[]{:S(2)}, u32[]{:S(2)}) %collective-permute-start.16) | collective-permute-done | bytes 524320 | tf_op jit(solution)/shard_map/ppermute | solution.py:30
  106.0 2.9 %collective-permute-start.25 = (bf16[1024,256]{1,0:T(8,128)(2,1)S(1)}, bf16[1024,256]{1,0:T(8,128)(2,1)S(1)}, u32[]{:S(2)}, u32[]{:S(2)}) collective-permute-start(bf16[1024,256]{1,0:T(8,128)(2,1)S(1)} %collective-permute-done.21.refs_9_), channel_id=1, source_target_pairs={{0,6},{2,0},{4,2},{6,4},{1,7},{3,1},{5,3},{7,5},{8,14},{10,8},{12,... | collective-permute-start | bytes 1572872 | tf_op jit(solution)/shard_map/ppermute | solution.py:30
  110.1 10.8 %collective-permute-done.24.refs_12_ = bf16[1024,256]{1,0:T(8,128)(2,1)S(1)} collective-permute-done((bf16[1024,256]{1,0:T(8,128)(2,1)S(1)}, bf16[1024,256]{1,0:T(8,128)(2,1)S(1)}, u32[]{:S(2)}, u32[]{:S(2)}) %collective-permute-start.24) | collective-permute-done | bytes 524320 | tf_op jit(solution)/shard_map/ppermute | solution.py:30
  121.5 0.7 broadcast_divide_fusion.refs_16_
  122.8 0.7 collective-permute-done.26.refs_14_
  123.6 0.7 collective-permute-done.27.refs_15_
  124.4 0.8 copy-done.15
  125.3 8.7 %assemble.1 = (bf16[1024,4096]{1,0:T(8,128)(2,1)}, f32[1024,128]{1,0:T(8,128)}) custom-call(bf16[1024,256]{1,0:T(8,128)(2,1)} %get-tuple-element.10.refs_0_, bf16[1024,256]{1,0:T(8,128)(2,1)} %get-tuple-element.11.refs_1_, bf16[1024,256]{1,0:T(8,128)(2,1)} %copy-done.6, bf16[1024,256]{1,0:T(8,128)(2,1)} %copy-done.7, bf16[1024,256]{1,0:T(8,128)(2,1)} %copy-done.4, ...), custom_call_target="tpu_custom_call" | custom-call | flops 16777216 | bytes 16777216 | tf_op jit(solution)/shard_map/assemble/pallas_call | solution.py:254
  134.0 26.2 %vocab_stats.1 = f32[2,1024]{1,0:T(2,128)} custom-call(s32[2]{0:T(128)} %pad_add_fusion.first_ref, bf16[1024,4096]{1,0:T(8,128)(2,1)} %get-tuple-element.12.rows_s, f32[1024,128]{1,0:T(8,128)} %get-tuple-element.13.scale_s, s32[1024,1]{1,0:T(8,128)} %bitcast.42, bf16[4,4096,512]{2,1,0:T(8,128)(2,1)} %bitcast.55), custom_call_target="tpu_custom_call" | custom-call | flops 17179869184 | bytes 25165824 | tf_op jit(solution)/shard_map/vocab_stats/pallas_call | solution.py:333
  160.3 12.9 %all-gather.1 = f32[8,2,1024]{2,1,0:T(2,128)S(1)} all-gather(f32[1,2,1024]{2,1,0:T(2,128)} %bitcast.46), channel_id=2, replica_groups=mesh['prompt'=4,'dp'=4,'mp_0'=4,'mp_1'=2] {'mp_0','mp_1'}, dimensions={0}, use_global_device_ids=true | all-gather | bytes 73728 | tf_op jit(solution)/shard_map/all_gather | solution.py:453
  174.1 14.1 %all_to_all.11 = f32[16,1,9]{2,1,0:T(1,128)S(1)} all-to-all(f32[16,1,9]{2,1,0:T(1,128)S(1)} %broadcast_in_dim.38), channel_id=1, replica_groups=mesh['prompt'=4,'dp'=4,'mp_0'=4,'mp_1'=2] {'prompt','dp'}, dimensions={0} | all-to-all | bytes 1152 | tf_op jit(solution)/shard_map/all_to_all | solution.py:24
  188.9 1.2 multiply_divide_fusion
  (114 shorter events, 7.9 us)
Async XLA Ops:
  7.2 59.4 %copy-start = (s32[1,512]{1,0:T(1,128)S(1)}, s32[1,512]{1,0:T(1,128)}, u32[]{:S(2)}) copy-start(s32[1,512]{1,0:T(1,128)} %param.15) | copy-start | bytes 6148
  7.2 126.8 %all-gather.4.cloned.1.call-start = ((), (), s32[]{:S(2)}) async-start(), calls=%async_computation.2 | async-start | bytes 17825792 | tf_op jit(solution)/shard_map/all_gather | solution.py:435
  13.5 55.5 %all-to-all-start = ((bf16[8,256,512]{2,1,0:T(8,128)(2,1)}), bf16[8,256,512]{2,1,0:T(8,128)(2,1)S(1)}, u32[]{:S(2)}, u32[]{:S(2)}) async-start(bf16[8,256,512]{2,1,0:T(8,128)(2,1)} %split_columns.1), calls=%async_computation | async-start | bytes 4194304 | tf_op jit(solution)/shard_map/all_to_all | solution.py:438
  22.4 46.4 %copy-start.23 = (f32[4096]{0:T(1024)S(1)}, f32[4096]{0:T(1024)}, u32[]{:S(2)}) copy-start(f32[4096]{0:T(1024)} %param.20) | copy-start | bytes 49156
  36.9 14.8 %collective-permute-start.2 = (bf16[1024,128]{1,0:T(8,128)(2,1)}, bf16[1024,128]{1,0:T(8,128)(2,1)S(1)}, u32[]{:S(2)}, u32[]{:S(2)}) collective-permute-start(bf16[1024,128]{1,0:T(8,128)(2,1)} %get-tuple-element.8.refs_0_), channel_id=1, source_target_pairs={{0,2},{2,4},{4,6},{6,0},{1,3},{3,5},{5,7},{7,1},{8,10},{10,12},{12... | collective-permute-start | bytes 786440 | tf_op jit(solution)/shard_map/ppermute | solution.py:30
  38.9 12.9 %collective-permute-start.7 = (bf16[1024,128]{1,0:T(8,128)(2,1)}, bf16[1024,128]{1,0:T(8,128)(2,1)S(1)}, u32[]{:S(2)}, u32[]{:S(2)}) collective-permute-start(bf16[1024,128]{1,0:T(8,128)(2,1)} %get-tuple-element.9.refs_1_), channel_id=1, source_target_pairs={{0,6},{2,0},{4,2},{6,4},{1,7},{3,1},{5,3},{7,5},{8,14},{10,8},{12,... | collective-permute-start | bytes 786440 | tf_op jit(solution)/shard_map/ppermute | solution.py:30
  40.2 17.2 %collective-permute-start.3 = (bf16[1024,128]{1,0:T(8,128)(2,1)}, bf16[1024,128]{1,0:T(8,128)(2,1)S(1)}, u32[]{:S(2)}, u32[]{:S(2)}) collective-permute-start(bf16[1024,128]{1,0:T(8,128)(2,1)} %get-tuple-element.9.refs_1_), channel_id=1, source_target_pairs={{0,2},{2,4},{4,6},{6,0},{1,3},{3,5},{5,7},{7,1},{8,10},{10,12},{12... | collective-permute-start | bytes 786440 | tf_op jit(solution)/shard_map/ppermute | solution.py:30
  40.9 17.5 %collective-permute-start.6 = (bf16[1024,128]{1,0:T(8,128)(2,1)}, bf16[1024,128]{1,0:T(8,128)(2,1)S(1)}, u32[]{:S(2)}, u32[]{:S(2)}) collective-permute-start(bf16[1024,128]{1,0:T(8,128)(2,1)} %get-tuple-element.8.refs_0_), channel_id=1, source_target_pairs={{0,6},{2,0},{4,2},{6,4},{1,7},{3,1},{5,3},{7,5},{8,14},{10,8},{12,... | collective-permute-start | bytes 786440 | tf_op jit(solution)/shard_map/ppermute | solution.py:30
  43.4 15.0 %collective-permute-start = (bf16[1024,128]{1,0:T(8,128)(2,1)}, bf16[1024,128]{1,0:T(8,128)(2,1)S(1)}, u32[]{:S(2)}, u32[]{:S(2)}) collective-permute-start(bf16[1024,128]{1,0:T(8,128)(2,1)} %get-tuple-element.8.refs_0_), channel_id=1, source_target_pairs={{0,1},{1,0},{2,3},{3,2},{4,5},{5,4},{6,7},{7,6},{8,9},{9,8},{10,11... | collective-permute-start | bytes 786440 | tf_op jit(solution)/shard_map/ppermute | solution.py:30
  51.7 7.2 %collective-permute-start.1 = (bf16[1024,128]{1,0:T(8,128)(2,1)}, bf16[1024,128]{1,0:T(8,128)(2,1)S(1)}, u32[]{:S(2)}, u32[]{:S(2)}) collective-permute-start(bf16[1024,128]{1,0:T(8,128)(2,1)} %get-tuple-element.9.refs_1_), channel_id=1, source_target_pairs={{0,1},{1,0},{2,3},{3,2},{4,5},{5,4},{6,7},{7,6},{8,9},{9,8},{10,11... | collective-permute-start | bytes 786440 | tf_op jit(solution)/shard_map/ppermute | solution.py:30
  51.8 11.3 %collective-permute-start.10 = (bf16[1024,128]{1,0:T(8,128)(2,1)S(1)}, bf16[1024,128]{1,0:T(8,128)(2,1)}, u32[]{:S(2)}, u32[]{:S(2)}) collective-permute-start(bf16[1024,128]{1,0:T(8,128)(2,1)S(1)} %collective-permute-done.2.refs_4_), channel_id=1, source_target_pairs={{0,2},{2,4},{4,6},{6,0},{1,3},{3,5},{5,7},{7,1},{8,10},{10,12},{12... | collective-permute-start | bytes 786440 | tf_op jit(solution)/shard_map/ppermute | solution.py:30
  57.3 8.4 %collective-permute-start.11 = (bf16[1024,128]{1,0:T(8,128)(2,1)S(1)}, bf16[1024,128]{1,0:T(8,128)(2,1)}, u32[]{:S(2)}, u32[]{:S(2)}) collective-permute-start(bf16[1024,128]{1,0:T(8,128)(2,1)S(1)} %collective-permute-done.7.refs_9_), channel_id=1, source_target_pairs={{0,6},{2,0},{4,2},{6,4},{1,7},{3,1},{5,3},{7,5},{8,14},{10,8},{12,... | collective-permute-start | bytes 786440 | tf_op jit(solution)/shard_map/ppermute | solution.py:30
  58.4 7.4 %collective-permute-start.4 = (bf16[1024,128]{1,0:T(8,128)(2,1)S(1)}, bf16[1024,128]{1,0:T(8,128)(2,1)S(1)}, u32[]{:S(2)}, u32[]{:S(2)}) collective-permute-start(bf16[1024,128]{1,0:T(8,128)(2,1)S(1)} %collective-permute-done.2.refs_4_), channel_id=1, source_target_pairs={{0,1},{1,0},{2,3},{3,2},{4,5},{5,4},{6,7},{7,6},{8,9},{9,8},{10,11... | collective-permute-start | bytes 786440 | tf_op jit(solution)/shard_map/ppermute | solution.py:30
  58.4 10.5 %collective-permute-start.9 = (bf16[1024,128]{1,0:T(8,128)(2,1)S(1)}, bf16[1024,128]{1,0:T(8,128)(2,1)}, u32[]{:S(2)}, u32[]{:S(2)}) collective-permute-start(bf16[1024,128]{1,0:T(8,128)(2,1)S(1)} %collective-permute-done.7.refs_9_), channel_id=1, source_target_pairs={{0,1},{1,0},{2,3},{3,2},{4,5},{5,4},{6,7},{7,6},{8,9},{9,8},{10,11... | collective-permute-start | bytes 786440 | tf_op jit(solution)/shard_map/ppermute | solution.py:30
  58.9 10.0 %collective-permute-start.5 = (bf16[1024,128]{1,0:T(8,128)(2,1)S(1)}, bf16[1024,128]{1,0:T(8,128)(2,1)}, u32[]{:S(2)}, u32[]{:S(2)}) collective-permute-start(bf16[1024,128]{1,0:T(8,128)(2,1)S(1)} %collective-permute-done.3.refs_5_), channel_id=1, source_target_pairs={{0,1},{1,0},{2,3},{3,2},{4,5},{5,4},{6,7},{7,6},{8,9},{9,8},{10,11... | collective-permute-start | bytes 786440 | tf_op jit(solution)/shard_map/ppermute | solution.py:30
  63.0 5.9 %collective-permute-start.8 = (bf16[1024,128]{1,0:T(8,128)(2,1)S(1)}, bf16[1024,128]{1,0:T(8,128)(2,1)}, u32[]{:S(2)}, u32[]{:S(2)}) collective-permute-start(bf16[1024,128]{1,0:T(8,128)(2,1)S(1)} %collective-permute-done.6.refs_8_), channel_id=1, source_target_pairs={{0,1},{1,0},{2,3},{3,2},{4,5},{5,4},{6,7},{7,6},{8,9},{9,8},{10,11... | collective-permute-start | bytes 786440 | tf_op jit(solution)/shard_map/ppermute | solution.py:30
  65.8 3.2 %collective-permute-start.12 = (bf16[1024,128]{1,0:T(8,128)(2,1)}, bf16[1024,128]{1,0:T(8,128)(2,1)}, u32[]{:S(2)}, u32[]{:S(2)}) collective-permute-start(bf16[1024,128]{1,0:T(8,128)(2,1)} %collective-permute-done.10.refs_12_), channel_id=1, source_target_pairs={{0,1},{1,0},{2,3},{3,2},{4,5},{5,4},{6,7},{7,6},{8,9},{9,8},{10,11... | collective-permute-start | bytes 786440 | tf_op jit(solution)/shard_map/ppermute | solution.py:30
  65.8 3.2 %collective-permute-start.13 = (bf16[1024,128]{1,0:T(8,128)(2,1)}, bf16[1024,128]{1,0:T(8,128)(2,1)}, u32[]{:S(2)}, u32[]{:S(2)}) collective-permute-start(bf16[1024,128]{1,0:T(8,128)(2,1)} %collective-permute-done.11.refs_13_), channel_id=1, source_target_pairs={{0,1},{1,0},{2,3},{3,2},{4,5},{5,4},{6,7},{7,6},{8,9},{9,8},{10,11... | collective-permute-start | bytes 786440 | tf_op jit(solution)/shard_map/ppermute | solution.py:30
  77.0 28.4 %collective-permute-start.21 = (bf16[1024,256]{1,0:T(8,128)(2,1)}, bf16[1024,256]{1,0:T(8,128)(2,1)S(1)}, u32[]{:S(2)}, u32[]{:S(2)}) collective-permute-start(bf16[1024,256]{1,0:T(8,128)(2,1)} %get-tuple-element.11.refs_1_), channel_id=1, source_target_pairs={{0,6},{2,0},{4,2},{6,4},{1,7},{3,1},{5,3},{7,5},{8,14},{10,8},{12,... | collective-permute-start | bytes 1572872 | tf_op jit(solution)/shard_map/ppermute | solution.py:30
  78.7 26.7 %collective-permute-start.17 = (bf16[1024,256]{1,0:T(8,128)(2,1)}, bf16[1024,256]{1,0:T(8,128)(2,1)S(1)}, u32[]{:S(2)}, u32[]{:S(2)}) collective-permute-start(bf16[1024,256]{1,0:T(8,128)(2,1)} %get-tuple-element.11.refs_1_), channel_id=1, source_target_pairs={{0,2},{2,4},{4,6},{6,0},{1,3},{3,5},{5,7},{7,1},{8,10},{10,12},{12... | collective-permute-start | bytes 1572872 | tf_op jit(solution)/shard_map/ppermute | solution.py:30
  79.1 26.3 %collective-permute-start.16 = (bf16[1024,256]{1,0:T(8,128)(2,1)}, bf16[1024,256]{1,0:T(8,128)(2,1)S(1)}, u32[]{:S(2)}, u32[]{:S(2)}) collective-permute-start(bf16[1024,256]{1,0:T(8,128)(2,1)} %get-tuple-element.10.refs_0_), channel_id=1, source_target_pairs={{0,2},{2,4},{4,6},{6,0},{1,3},{3,5},{5,7},{7,1},{8,10},{10,12},{12... | collective-permute-start | bytes 1572872 | tf_op jit(solution)/shard_map/ppermute | solution.py:30
  79.1 26.9 %collective-permute-start.20 = (bf16[1024,256]{1,0:T(8,128)(2,1)}, bf16[1024,256]{1,0:T(8,128)(2,1)S(1)}, u32[]{:S(2)}, u32[]{:S(2)}) collective-permute-start(bf16[1024,256]{1,0:T(8,128)(2,1)} %get-tuple-element.10.refs_0_), channel_id=1, source_target_pairs={{0,6},{2,0},{4,2},{6,4},{1,7},{3,1},{5,3},{7,5},{8,14},{10,8},{12,... | collective-permute-start | bytes 1572872 | tf_op jit(solution)/shard_map/ppermute | solution.py:30
  82.3 27.1 %collective-permute-start.14 = (bf16[1024,256]{1,0:T(8,128)(2,1)}, bf16[1024,256]{1,0:T(8,128)(2,1)S(1)}, u32[]{:S(2)}, u32[]{:S(2)}) collective-permute-start(bf16[1024,256]{1,0:T(8,128)(2,1)} %get-tuple-element.10.refs_0_), channel_id=1, source_target_pairs={{0,1},{1,0},{2,3},{3,2},{4,5},{5,4},{6,7},{7,6},{8,9},{9,8},{10,11... | collective-permute-start | bytes 1572872 | tf_op jit(solution)/shard_map/ppermute | solution.py:30
  105.3 4.3 %collective-permute-start.15 = (bf16[1024,256]{1,0:T(8,128)(2,1)}, bf16[1024,256]{1,0:T(8,128)(2,1)S(1)}, u32[]{:S(2)}, u32[]{:S(2)}) collective-permute-start(bf16[1024,256]{1,0:T(8,128)(2,1)} %get-tuple-element.11.refs_1_), channel_id=1, source_target_pairs={{0,1},{1,0},{2,3},{3,2},{4,5},{5,4},{6,7},{7,6},{8,9},{9,8},{10,11... | collective-permute-start | bytes 1572872 | tf_op jit(solution)/shard_map/ppermute | solution.py:30
  105.4 15.6 %collective-permute-start.24 = (bf16[1024,256]{1,0:T(8,128)(2,1)S(1)}, bf16[1024,256]{1,0:T(8,128)(2,1)S(1)}, u32[]{:S(2)}, u32[]{:S(2)}) collective-permute-start(bf16[1024,256]{1,0:T(8,128)(2,1)S(1)} %collective-permute-done.16.refs_4_), channel_id=1, source_target_pairs={{0,2},{2,4},{4,6},{6,0},{1,3},{3,5},{5,7},{7,1},{8,10},{10,12},{12... | collective-permute-start | bytes 1572872 | tf_op jit(solution)/shard_map/ppermute | solution.py:30
  105.5 16.0 %collective-permute-start.18 = (bf16[1024,256]{1,0:T(8,128)(2,1)S(1)}, bf16[1024,256]{1,0:T(8,128)(2,1)S(1)}, u32[]{:S(2)}, u32[]{:S(2)}) collective-permute-start(bf16[1024,256]{1,0:T(8,128)(2,1)S(1)} %collective-permute-done.16.refs_4_), channel_id=1, source_target_pairs={{0,1},{1,0},{2,3},{3,2},{4,5},{5,4},{6,7},{7,6},{8,9},{9,8},{10,11... | collective-permute-start | bytes 1572872 | tf_op jit(solution)/shard_map/ppermute | solution.py:30
  106.0 15.0 %collective-permute-start.25 = (bf16[1024,256]{1,0:T(8,128)(2,1)S(1)}, bf16[1024,256]{1,0:T(8,128)(2,1)S(1)}, u32[]{:S(2)}, u32[]{:S(2)}) collective-permute-start(bf16[1024,256]{1,0:T(8,128)(2,1)S(1)} %collective-permute-done.21.refs_9_), channel_id=1, source_target_pairs={{0,6},{2,0},{4,2},{6,4},{1,7},{3,1},{5,3},{7,5},{8,14},{10,8},{12,... | collective-permute-start | bytes 1572872 | tf_op jit(solution)/shard_map/ppermute | solution.py:30
  109.5 13.4 %collective-permute-start.23 = (bf16[1024,256]{1,0:T(8,128)(2,1)S(1)}, bf16[1024,256]{1,0:T(8,128)(2,1)S(1)}, u32[]{:S(2)}, u32[]{:S(2)}) collective-permute-start(bf16[1024,256]{1,0:T(8,128)(2,1)S(1)} %collective-permute-done.21.refs_9_), channel_id=1, source_target_pairs={{0,1},{1,0},{2,3},{3,2},{4,5},{5,4},{6,7},{7,6},{8,9},{9,8},{10,11... | collective-permute-start | bytes 1572872 | tf_op jit(solution)/shard_map/ppermute | solution.py:30
  109.6 12.6 %collective-permute-start.19 = (bf16[1024,256]{1,0:T(8,128)(2,1)S(1)}, bf16[1024,256]{1,0:T(8,128)(2,1)S(1)}, u32[]{:S(2)}, u32[]{:S(2)}) collective-permute-start(bf16[1024,256]{1,0:T(8,128)(2,1)S(1)} %collective-permute-done.17.refs_5_), channel_id=1, source_target_pairs={{0,1},{1,0},{2,3},{3,2},{4,5},{5,4},{6,7},{7,6},{8,9},{9,8},{10,11... | collective-permute-start | bytes 1572872 | tf_op jit(solution)/shard_map/ppermute | solution.py:30
  120.9 1.9 collective-permute-start.22
  120.9 2.6 %collective-permute-start.26 = (bf16[1024,256]{1,0:T(8,128)(2,1)S(1)}, bf16[1024,256]{1,0:T(8,128)(2,1)S(1)}, u32[]{:S(2)}, u32[]{:S(2)}) collective-permute-start(bf16[1024,256]{1,0:T(8,128)(2,1)S(1)} %collective-permute-done.24.refs_12_), channel_id=1, source_target_pairs={{0,1},{1,0},{2,3},{3,2},{4,5},{5,4},{6,7},{7,6},{8,9},{9,8},{10,11... | collective-permute-start | bytes 1572872 | tf_op jit(solution)/shard_map/ppermute | solution.py:30
  121.4 2.9 %collective-permute-start.27 = (bf16[1024,256]{1,0:T(8,128)(2,1)S(1)}, bf16[1024,256]{1,0:T(8,128)(2,1)S(1)}, u32[]{:S(2)}, u32[]{:S(2)}) collective-permute-start(bf16[1024,256]{1,0:T(8,128)(2,1)S(1)} %collective-permute-done.25.refs_13_), channel_id=1, source_target_pairs={{0,1},{1,0},{2,3},{3,2},{4,5},{5,4},{6,7},{7,6},{8,9},{9,8},{10,11... | collective-permute-start | bytes 1572872 | tf_op jit(solution)/shard_map/ppermute | solution.py:30
  (22 other events, 198.2 us)
Sparse Core Ops, SparseCore 0:
  10.9 113.6 all-gather.3

commit v6 on v5

--- a/solution.py
+++ b/solution.py
@@ -19,10 +19,9 @@
 LOG2E = math.log2(math.e)
 
 
-def of_everyone(value, axis):
+def of_each(value, axis):
     copies = jnp.broadcast_to(value, (lax.axis_size(axis), *value.shape))
-    everything = lax.all_to_all(copies, axis, split_axis=0, concat_axis=0, tiled=True)
-    return jnp.sum(everything, axis=0)
+    return lax.all_to_all(copies, axis, split_axis=0, concat_axis=0, tiled=True)
 
 
 def shifted(value, axis, shift):
@@ -233,50 +232,13 @@
     )(places, *contexts, out_cols, target_embed, final_gain.reshape(1, -1))
 
 
-def assemble_kernel(*refs):
-    *row_refs, degain_ref, rows_ref, scale_ref = refs
-    tile, width = rows_ref.shape
-    squares = jnp.zeros((tile, 128), jnp.float32)
-    k = 0
-    for ref in row_refs:
-        rows_ref[:, k : k + ref.shape[1]] = ref[...]
-        for i in range(0, ref.shape[1], 128):
-            x = ref[:, i : i + 128].astype(jnp.float32) * degain_ref[:, k + i : k + i + 128]
-            squares += x * x
-        k += ref.shape[1]
-    mean = jnp.sum(squares, axis=1, keepdims=True) / width
-    scale_ref[...] = jnp.broadcast_to(lax.rsqrt(mean + EPSILON) * LOG2E, scale_ref.shape)
-
-
-def assemble(row_blocks, degain):
-    rows, width, tile = row_blocks[0].shape[0], degain.shape[1], 256
-    by_tile = lambda columns: pl.BlockSpec((tile, columns), lambda i: (i, 0))
-    return pl.pallas_call(
-        assemble_kernel,
-        out_shape=[
-            jax.ShapeDtypeStruct((rows, width), jnp.bfloat16),
-            jax.ShapeDtypeStruct((rows, 128), jnp.float32),
-        ],
-        grid=(rows // tile,),
-        in_specs=[
-            *(by_tile(b.shape[1]) for b in row_blocks),
-            pl.BlockSpec(degain.shape, lambda i: (0, 0)),
-        ],
-        out_specs=[by_tile(width), by_tile(128)],
-        compiler_params=pltpu.CompilerParams(vmem_limit_bytes=VMEM_LIMIT),
-        cost_estimate=pl.CostEstimate(
-            flops=4 * rows * width, bytes_accessed=4 * rows * width, transcendentals=0
-        ),
-        name="assemble",
-    )(*row_blocks, degain)
-
-
-def vocab_kernel(
-    first_ref, rows_s, scale_s, label_ref, w_ref, out_ref,
-    first_s, second_s, top_s, sum_s, pick_s, label_s,
-):
+def vocab_kernel(first_ref, *refs, n_rows):
+    row_refs = refs[:n_rows]
+    degain_ref, label_ref, w_ref, out_ref = refs[n_rows : n_rows + 4]
+    rows_s, first_s, second_s, top_s, sum_s, pick_s, scale_s, label_s = refs[n_rows + 4 :]
     step = pl.program_id(0)
-    rows = rows_s.shape[0]
+    n_steps = pl.num_programs(0)
+    rows, width = rows_s.shape
     tile, columns = first_s.shape
     n_tiles = rows // tile
     at_tile = lambda t: slice(t * tile, (t + 1) * tile)
@@ -284,6 +246,16 @@
 
     @pl.when(step == 0)
     def _():
+        squares = jnp.zeros((rows, 128), jnp.float32)
+        k = 0
+        for ref in row_refs:
+            rows_s[:, k : k + ref.shape[1]] = ref[...]
+            for i in range(0, ref.shape[1], 128):
+                x = ref[:, i : i + 128].astype(jnp.float32) * degain_ref[:, k + i : k + i + 128]
+                squares += x * x
+            k += ref.shape[1]
+        mean = jnp.sum(squares, axis=1, keepdims=True) / width
+        scale_s[...] = jnp.broadcast_to(lax.rsqrt(mean + EPSILON) * LOG2E, scale_s.shape)
         label_s[...] = jnp.broadcast_to(label_ref[...], label_s.shape)
         top_s[...] = jnp.full_like(top_s, MASKED)
         sum_s[...] = jnp.zeros_like(sum_s)
@@ -315,7 +287,7 @@
         products[t % 2][...] = product
     take(at_tile(n_tiles - 1), products[(n_tiles + 1) % 2], first_column)
 
-    @pl.when(step == pl.num_programs(0) - 1)
+    @pl.when(step == n_steps - 1)
     def _():
         top = jnp.max(top_s[...], axis=1, keepdims=True)
         total = jnp.sum(sum_s[...] * jnp.exp2(top_s[...] - top), axis=1, keepdims=True)
@@ -325,27 +297,29 @@
         out_ref[...] = both.T[:2, :]
 
 
-def vocab_stats(first, rows, scale, row_labels, vocab_all):
-    n_rows = rows.shape[0]
+def vocab_stats(first, row_blocks, degain, row_labels, vocab_all):
+    n_rows = row_blocks[0].shape[0]
     n_blocks, width, columns = vocab_all.shape
     tile = 256
     whole = lambda a: pl.BlockSpec(a.shape, lambda j, f: (0, 0), pipeline_mode=pl.Buffered(1))
+    kernel = lambda *refs: vocab_kernel(*refs, n_rows=len(row_blocks))
     return pl.pallas_call(
-        vocab_kernel,
+        kernel,
         out_shape=jax.ShapeDtypeStruct((2, n_rows), jnp.float32),
         grid_spec=pltpu.PrefetchScalarGridSpec(
             num_scalar_prefetch=1,
             grid=(n_blocks,),
             in_specs=[
-                whole(rows),
-                whole(scale),
+                *(whole(b) for b in row_blocks),
+                whole(degain),
                 whole(row_labels),
                 pl.BlockSpec((1, width, columns), lambda j, f: (j, 0, 0)),
             ],
             out_specs=pl.BlockSpec((2, n_rows), lambda j, f: (0, 0)),
             scratch_shapes=[
+                pltpu.VMEM((n_rows, width), jnp.bfloat16),
                 *(pltpu.VMEM((tile, columns), jnp.float32) for _ in range(2)),
-                *(pltpu.VMEM((n_rows, 128), jnp.float32) for _ in range(3)),
+                *(pltpu.VMEM((n_rows, 128), jnp.float32) for _ in range(4)),
                 pltpu.VMEM((n_rows, 128), jnp.int32),
             ],
         ),
@@ -356,7 +330,7 @@
             transcendentals=n_rows * n_blocks * columns,
         ),
         name="vocab_stats",
-    )(first, rows, scale, row_labels, vocab_all)
+    )(first, *row_blocks, degain, row_labels, vocab_all)
 
 
 def piece_kernel(row_ref, vocab_ref, piece_ref, sem):
@@ -446,11 +420,10 @@
         [lax.dynamic_slice_in_dim(final_gain, p * part, part, 0) for p in places], axis=0
     ).reshape(1, -1)
     row_labels = jnp.tile(labels.reshape(-1, 1), (prompts_here, 1))
-    rows, scale = assemble(row_blocks, degain)
     first = jnp.stack([lax.axis_index(MP) * vocab_cols, n_model * vocab_cols]).astype(jnp.int32)
-    here = vocab_stats(first, rows, scale, row_labels, vocab_all)
-
-    every = lax.all_gather(here, MP)
+    here = vocab_stats(first, row_blocks, degain, row_labels, vocab_all)
+
+    every = of_each(here, MP)
     top_val = jnp.max(every[:, 0], axis=0)
     log_total = top_val + jnp.log(jnp.sum(jnp.exp(every[:, 0] - top_val), axis=0))
     losses = (log_total - jnp.sum(every[:, 1], axis=0)).reshape(prompts_here, 1, target_len)
@@ -468,7 +441,8 @@
         axis=1,
     )
     valid_here = jnp.sum(lengths).astype(jnp.float32).reshape(1)
-    totals = of_everyone(jnp.concatenate([placed, valid_here]), ("prompt", "dp"))
+    totals = of_each(jnp.concatenate([placed, valid_here]), ("prompt", "dp"))
+    totals = jnp.sum(totals, axis=0)
     prompt_loss = totals[:all_prompts] * float(n_prompt) / totals[all_prompts]
     return (token_loss, prompt_loss)
 

time: 197 us -> 188 us (0.954)
  blocking collectives: 27.1 us -> 12.6 us
  starting transfers between devices: 24.9 us -> 32.2 us
  Pallas kernels: 61.6 us -> 56.3 us
    all_gather x1 -> x0, blocking collectives: 12.9 us -> none  [shards(): every = lax.all_gather(here, MP)]
    ppermute x28, waiting for transfers between devices: 55.9 us -> 46.6 us  [shifted(): return lax.ppermute(value, axis, [(i, (i + shift) % n) for i in range(n)])]
    all_to_all x0 -> x1, waiting for transfers between devices: none -> 5.62 us  [of_each(): return lax.all_to_all(copies, axis, split_axis=0, concat_axis=0, tiled=True)]
    all_gather x1, waiting for transfers between devices: 0.02 us -> 5.48 us  [shards(): vocab_all = lax.all_gather(piece, ('dp', 'prompt'), axis=0, tiled=True)]
    pallas_call x2 -> x1, Pallas kernels: 35 us -> 29.6 us  [vocab_stats(): pl.pallas_call(kernel, out_shape=jax.ShapeDtypeStruct((2, n_rows), jnp.fl...]
    all_to_all x0 -> x1, starting transfers between devices: none -> 4.39 us  [of_each(): return lax.all_to_all(copies, axis, split_axis=0, concat_axis=0, tiled=True)]
    ppermute x28, starting transfers between devices: 19.5 us -> 22.4 us  [shifted(): return lax.ppermute(value, axis, [(i, (i + shift) % n) for i in range(n)])]
    unnamed x59 -> x53, local copies, waits for them, and re-layouts: 7 us -> 7.26 us
  transfers between devices with their start and end apart: 30 -> 31, of which waited for: 9 -> 14; matrix products, arithmetic and copies ran while one was open for 3% -> 4% of each run, Pallas kernels for 16% -> 13%
where the time goes in v6:
time: 188 us
  waiting for transfers between devices  57.7 us (31%)
  Pallas kernels  56.3 us (30%)
  starting transfers between devices  32.2 us (17%)
  between operations  15 us (8%)
  blocking collectives  12.6 us (7%)
  local copies, waits for them, and re-layouts  9.96 us (5%)
  other arithmetic  3.9 us (2%)
    ppermute x28, waiting for transfers between devices, shifted(): return lax.ppermute(value, axis, [(i, (i + shift) % n) for i in range(n)])  46.6 us
    pallas_call x1, Pallas kernels, vocab_stats(): pl.pallas_call(kernel, out_shape=jax.ShapeDtypeStruct((2, n_rows), jnp.fl...  29.6 us
    ppermute x28, starting transfers between devices, shifted(): return lax.ppermute(value, axis, [(i, (i + shift) % n) for i in range(n)])  22.4 us
    pallas_call x1, Pallas kernels, attention(): pl.pallas_call(attention_kernel, out_shape=[jax.ShapeDtypeStruct((rows, i...  14.5 us
    all_to_all x1, blocking collectives, of_each(): return lax.all_to_all(copies, axis, split_axis=0, concat_axis=0, tiled=True)  12.6 us
    unnamed x53, local copies, waits for them, and re-layouts  7.26 us
    pallas_call x1, Pallas kernels, output_part(): pl.pallas_call(output_kernel, out_shape=[jax.ShapeDtypeStruct((rows, part...  6.8 us
    all_to_all x1, waiting for transfers between devices, of_each(): return lax.all_to_all(copies, axis, split_axis=0, concat_axis=0, tiled=True)  5.62 us
  transfers between devices with their start and end apart: 31, of which 14 were waited for; matrix products, arithmetic and copies ran while one was open for 4% of the time, Pallas kernels for 13%

profile of v6, /device:TPU:0, one launch (start us, length us, event | category | flops | bytes accessed | tf_op | source)
XLA Modules:
  0.0 187.7 jit_solution(11186531569947743920)
XLA Ops:
  7.9 2.9 %vocab_piece.1 = bf16[1024,512]{1,0:T(8,128)(2,1)} custom-call(s32[2]{0:T(128)} %pad_add_fusion.1.row_ref, bf16[4096,512]{1,0:T(8,128)(2,1)} %vocab_ref.1), custom_call_target="tpu_custom_call" | custom-call | bytes 2097152 | tf_op jit(solution)/shard_map/vocab_piece/pallas_call | solution.py:353
  10.8 2.6 %split_columns.1 = bf16[8,256,512]{2,1,0:T(8,128)(2,1)} custom-call(bf16[256,4096]{1,0:T(8,128)(2,1)} %w_ref.3), custom_call_target="tpu_custom_call" | custom-call | bytes 4194304 | tf_op jit(solution)/shard_map/split_columns/pallas_call | solution.py:378
  13.4 5.4 %all-to-all-start = ((bf16[8,256,512]{2,1,0:T(8,128)(2,1)}), bf16[8,256,512]{2,1,0:T(8,128)(2,1)S(1)}, u32[]{:S(2)}, u32[]{:S(2)}) async-start(bf16[8,256,512]{2,1,0:T(8,128)(2,1)} %split_columns.1), calls=%async_computation | async-start | bytes 4194304 | tf_op jit(solution)/shard_map/all_to_all | solution.py:412
  18.8 3.6 %copy.25.prompt_ref = bf16[2,100,4096]{2,1,0:T(8,128)(2,1)} copy(bf16[2,100,4096]{2,0,1:T(2,128)(2,1)} %param.13) | data formatting | bytes 3276800 | tf_op args[0]
  22.4 14.5 %attention.1 = (bf16[1024,128]{1,0:T(8,128)(2,1)}, bf16[1024,128]{1,0:T(8,128)(2,1)}) custom-call(bf16[1,512,4096]{2,1,0:T(8,128)(2,1)} %refs_17_.1, bf16[2,100,4096]{2,1,0:T(8,128)(2,1)} %copy.25.prompt_ref, f32[1,4096]{1,0:T(1,128)} %bitcast.54, bf16[3,4096,256]{2,1,0:T(8,128)(2,1)} %w_ref.2, f32[512,64]{1,0:T(8,128)} %constant.102.clone.cos_t, ...), custom_call_target="tpu_custom_call" | custom-call | flops 8000000000 | bytes 12000000 | tf_op jit(solution)/shard_map/attention/pallas_call | solution.py:168
  36.8 3.2 %collective-permute-start.6 = (bf16[1024,128]{1,0:T(8,128)(2,1)}, bf16[1024,128]{1,0:T(8,128)(2,1)S(1)}, u32[]{:S(2)}, u32[]{:S(2)}) collective-permute-start(bf16[1024,128]{1,0:T(8,128)(2,1)} %get-tuple-element.6.refs_0_), channel_id=1, source_target_pairs={{0,6},{2,0},{4,2},{6,4},{1,7},{3,1},{5,3},{7,5},{8,14},{10,8},{12,... | collective-permute-start | bytes 786440 | tf_op jit(solution)/shard_map/ppermute | solution.py:29
  40.1 3.2 %collective-permute-start.7 = (bf16[1024,128]{1,0:T(8,128)(2,1)}, bf16[1024,128]{1,0:T(8,128)(2,1)S(1)}, u32[]{:S(2)}, u32[]{:S(2)}) collective-permute-start(bf16[1024,128]{1,0:T(8,128)(2,1)} %get-tuple-element.7.refs_1_), channel_id=1, source_target_pairs={{0,6},{2,0},{4,2},{6,4},{1,7},{3,1},{5,3},{7,5},{8,14},{10,8},{12,... | collective-permute-start | bytes 786440 | tf_op jit(solution)/shard_map/ppermute | solution.py:29
  43.3 7.3 %collective-permute-done.6.refs_8_ = bf16[1024,128]{1,0:T(8,128)(2,1)S(1)} collective-permute-done((bf16[1024,128]{1,0:T(8,128)(2,1)}, bf16[1024,128]{1,0:T(8,128)(2,1)S(1)}, u32[]{:S(2)}, u32[]{:S(2)}) %collective-permute-start.6) | collective-permute-done | bytes 262176 | tf_op jit(solution)/shard_map/ppermute | solution.py:29
  50.6 1.1 collective-permute-done.2.refs_4_
  51.7 1.0 collective-permute-start.10
  52.8 3.0 %collective-permute-done.7.refs_9_ = bf16[1024,128]{1,0:T(8,128)(2,1)S(1)} collective-permute-done((bf16[1024,128]{1,0:T(8,128)(2,1)}, bf16[1024,128]{1,0:T(8,128)(2,1)S(1)}, u32[]{:S(2)}, u32[]{:S(2)}) %collective-permute-start.7) | collective-permute-done | bytes 262176 | tf_op jit(solution)/shard_map/ppermute | solution.py:29
  55.8 2.6 %collective-permute-start.11 = (bf16[1024,128]{1,0:T(8,128)(2,1)S(1)}, bf16[1024,128]{1,0:T(8,128)(2,1)}, u32[]{:S(2)}, u32[]{:S(2)}) collective-permute-start(bf16[1024,128]{1,0:T(8,128)(2,1)S(1)} %collective-permute-done.7.refs_9_), channel_id=1, source_target_pairs={{0,6},{2,0},{4,2},{6,4},{1,7},{3,1},{5,3},{7,5},{8,14},{10,8},{12,... | collective-permute-start | bytes 786440 | tf_op jit(solution)/shard_map/ppermute | solution.py:29
  59.8 3.2 %collective-permute-done.10.refs_12_ = bf16[1024,128]{1,0:T(8,128)(2,1)} collective-permute-done((bf16[1024,128]{1,0:T(8,128)(2,1)S(1)}, bf16[1024,128]{1,0:T(8,128)(2,1)}, u32[]{:S(2)}, u32[]{:S(2)}) %collective-permute-start.10) | collective-permute-done | bytes 262176 | tf_op jit(solution)/shard_map/ppermute | solution.py:29
  63.0 1.5 collective-permute-done.11.refs_13_
  64.5 1.0 copy.37
  66.5 1.3 copy-done.1
  67.7 6.8 %output_part.1 = (bf16[1024,256]{1,0:T(8,128)(2,1)}, bf16[1024,256]{1,0:T(8,128)(2,1)}) custom-call(s32[8]{0:T(128)} %stack.52.places_ref, bf16[1024,128]{1,0:T(8,128)(2,1)} %get-tuple-element.6.refs_0_, bf16[1024,128]{1,0:T(8,128)(2,1)} %get-tuple-element.7.refs_1_, bf16[1024,128]{1,0:T(8,128)(2,1)} %copy-done.4, ...), custom_call_target="tpu_custom_call" | custom-call | flops 2000000000 | bytes 8000000 | tf_op jit(solution)/shard_map/output_part/pallas_call | solution.py:213
  74.5 3.5 %collective-permute-start.20 = (bf16[1024,256]{1,0:T(8,128)(2,1)}, bf16[1024,256]{1,0:T(8,128)(2,1)S(1)}, u32[]{:S(2)}, u32[]{:S(2)}) collective-permute-start(bf16[1024,256]{1,0:T(8,128)(2,1)} %get-tuple-element.8.refs_1_), channel_id=1, source_target_pairs={{0,6},{2,0},{4,2},{6,4},{1,7},{3,1},{5,3},{7,5},{8,14},{10,8},{12,... | collective-permute-start | bytes 1572872 | tf_op jit(solution)/shard_map/ppermute | solution.py:29
  78.2 3.1 %collective-permute-start.21 = (bf16[1024,256]{1,0:T(8,128)(2,1)}, bf16[1024,256]{1,0:T(8,128)(2,1)S(1)}, u32[]{:S(2)}, u32[]{:S(2)}) collective-permute-start(bf16[1024,256]{1,0:T(8,128)(2,1)} %get-tuple-element.9.refs_2_), channel_id=1, source_target_pairs={{0,6},{2,0},{4,2},{6,4},{1,7},{3,1},{5,3},{7,5},{8,14},{10,8},{12,... | collective-permute-start | bytes 1572872 | tf_op jit(solution)/shard_map/ppermute | solution.py:29
  81.4 9.2 %collective-permute-done.20.refs_9_ = bf16[1024,256]{1,0:T(8,128)(2,1)S(1)} collective-permute-done((bf16[1024,256]{1,0:T(8,128)(2,1)}, bf16[1024,256]{1,0:T(8,128)(2,1)S(1)}, u32[]{:S(2)}, u32[]{:S(2)}) %collective-permute-start.20) | collective-permute-done | bytes 524320 | tf_op jit(solution)/shard_map/ppermute | solution.py:29
  90.6 3.6 %collective-permute-done.16.refs_5_ = bf16[1024,256]{1,0:T(8,128)(2,1)S(1)} collective-permute-done((bf16[1024,256]{1,0:T(8,128)(2,1)}, bf16[1024,256]{1,0:T(8,128)(2,1)S(1)}, u32[]{:S(2)}, u32[]{:S(2)}) %collective-permute-start.16) | collective-permute-done | bytes 524320 | tf_op jit(solution)/shard_map/ppermute | solution.py:29
  94.3 7.0 %collective-permute-done.21.refs_10_ = bf16[1024,256]{1,0:T(8,128)(2,1)S(1)} collective-permute-done((bf16[1024,256]{1,0:T(8,128)(2,1)}, bf16[1024,256]{1,0:T(8,128)(2,1)S(1)}, u32[]{:S(2)}, u32[]{:S(2)}) %collective-permute-start.21) | collective-permute-done | bytes 524320 | tf_op jit(solution)/shard_map/ppermute | solution.py:29
  101.4 3.6 %collective-permute-start.25 = (bf16[1024,256]{1,0:T(8,128)(2,1)S(1)}, bf16[1024,256]{1,0:T(8,128)(2,1)S(1)}, u32[]{:S(2)}, u32[]{:S(2)}) collective-permute-start(bf16[1024,256]{1,0:T(8,128)(2,1)S(1)} %collective-permute-done.21.refs_10_), channel_id=1, source_target_pairs={{0,6},{2,0},{4,2},{6,4},{1,7},{3,1},{5,3},{7,5},{8,14},{10,8},{12,... | collective-permute-start | bytes 1572872 | tf_op jit(solution)/shard_map/ppermute | solution.py:29
  106.3 9.6 %collective-permute-done.24.refs_13_ = bf16[1024,256]{1,0:T(8,128)(2,1)S(1)} collective-permute-done((bf16[1024,256]{1,0:T(8,128)(2,1)S(1)}, bf16[1024,256]{1,0:T(8,128)(2,1)S(1)}, u32[]{:S(2)}, u32[]{:S(2)}) %collective-permute-start.24) | collective-permute-done | bytes 524320 | tf_op jit(solution)/shard_map/ppermute | solution.py:29
  118.3 0.8 copy-done.20
  119.1 5.5 %all-gather.2.cloned.1.call-done = bf16[16384,512]{1,0:T(8,128)(2,1)} async-done(((bf16[1024,512]{1,0:T(8,128)(2,1)}), bf16[16384,512]{1,0:T(8,128)(2,1)}) %all-gather.2.cloned.1.call-update) | async-done | bytes 16777232 | tf_op jit(solution)/shard_map/all_gather | solution.py:409
  124.6 29.6 %vocab_stats.1 = f32[2,1024]{1,0:T(2,128)} custom-call(s32[2]{0:T(128)} %pad_add_fusion.refs_0_, bf16[1024,256]{1,0:T(8,128)(2,1)} %get-tuple-element.8.refs_1_, bf16[1024,256]{1,0:T(8,128)(2,1)} %get-tuple-element.9.refs_2_, bf16[1024,256]{1,0:T(8,128)(2,1)} %copy-done.10, bf16[1024,256]{1,0:T(8,128)(2,1)} %copy-done.13, bf16[1024,256]{1,0:T(8,128)(2,1)} %copy-done.9, ...), custom_call_target="tpu_custom_call" | custom-call | flops 17179869184 | bytes 25165824 | tf_op jit(solution)/shard_map/vocab_stats/pallas_call | solution.py:306
  154.2 1.3 broadcast_in_dim.38
  155.5 4.4 %all-to-all-start.1 = ((f32[8,2,1024]{2,1,0:T(2,128)}), f32[8,2,1024]{2,1,0:T(2,128)S(1)}, u32[]{:S(2)}, u32[]{:S(2)}) async-start(f32[8,2,1024]{2,1,0:T(2,128)} %broadcast_in_dim.38), calls=%async_computation.1 | async-start | bytes 131072 | tf_op jit(solution)/shard_map/all_to_all | solution.py:24
  159.9 5.6 %all-to-all-done.1 = f32[8,2,1024]{2,1,0:T(2,128)S(1)} async-done(((f32[8,2,1024]{2,1,0:T(2,128)}), f32[8,2,1024]{2,1,0:T(2,128)S(1)}, u32[]{:S(2)}, u32[]{:S(2)}) %all-to-all-start.1) | async-done | bytes 65568 | tf_op jit(solution)/shard_map/all_to_all | solution.py:24
  166.5 12.6 %all_to_all.16 = f32[16,1,9]{2,1,0:T(1,128)S(1)} all-to-all(f32[16,1,9]{2,1,0:T(1,128)S(1)} %broadcast_in_dim.42), channel_id=1, replica_groups=mesh['prompt'=4,'dp'=4,'mp_0'=4,'mp_1'=2] {'prompt','dp'}, dimensions={0} | all-to-all | bytes 1152 | tf_op jit(solution)/shard_map/all_to_all | solution.py:24
  179.7 1.1 multiply_divide_fusion
  (109 shorter events, 7.8 us)
Async XLA Ops:
  7.2 57.4 %copy-start = (s32[1,512]{1,0:T(1,128)S(1)}, s32[1,512]{1,0:T(1,128)}, u32[]{:S(2)}) copy-start(s32[1,512]{1,0:T(1,128)} %param.15) | copy-start | bytes 6148
  7.2 117.4 %all-gather.2.cloned.1.call-start = ((), (), s32[]{:S(2)}) async-start(), calls=%async_computation.3 | async-start | bytes 17825792 | tf_op jit(solution)/shard_map/all_gather | solution.py:409
  13.4 53.0 %all-to-all-start = ((bf16[8,256,512]{2,1,0:T(8,128)(2,1)}), bf16[8,256,512]{2,1,0:T(8,128)(2,1)S(1)}, u32[]{:S(2)}, u32[]{:S(2)}) async-start(bf16[8,256,512]{2,1,0:T(8,128)(2,1)} %split_columns.1), calls=%async_computation | async-start | bytes 4194304 | tf_op jit(solution)/shard_map/all_to_all | solution.py:412
  36.8 13.8 %collective-permute-start.6 = (bf16[1024,128]{1,0:T(8,128)(2,1)}, bf16[1024,128]{1,0:T(8,128)(2,1)S(1)}, u32[]{:S(2)}, u32[]{:S(2)}) collective-permute-start(bf16[1024,128]{1,0:T(8,128)(2,1)} %get-tuple-element.6.refs_0_), channel_id=1, source_target_pairs={{0,6},{2,0},{4,2},{6,4},{1,7},{3,1},{5,3},{7,5},{8,14},{10,8},{12,... | collective-permute-start | bytes 786440 | tf_op jit(solution)/shard_map/ppermute | solution.py:29
  40.1 11.6 %collective-permute-start.2 = (bf16[1024,128]{1,0:T(8,128)(2,1)}, bf16[1024,128]{1,0:T(8,128)(2,1)S(1)}, u32[]{:S(2)}, u32[]{:S(2)}) collective-permute-start(bf16[1024,128]{1,0:T(8,128)(2,1)} %get-tuple-element.6.refs_0_), channel_id=1, source_target_pairs={{0,2},{2,4},{4,6},{6,0},{1,3},{3,5},{5,7},{7,1},{8,10},{10,12},{12... | collective-permute-start | bytes 786440 | tf_op jit(solution)/shard_map/ppermute | solution.py:29
  40.1 11.6 %collective-permute-start = (bf16[1024,128]{1,0:T(8,128)(2,1)}, bf16[1024,128]{1,0:T(8,128)(2,1)S(1)}, u32[]{:S(2)}, u32[]{:S(2)}) collective-permute-start(bf16[1024,128]{1,0:T(8,128)(2,1)} %get-tuple-element.6.refs_0_), channel_id=1, source_target_pairs={{0,1},{1,0},{2,3},{3,2},{4,5},{5,4},{6,7},{7,6},{8,9},{9,8},{10,11... | collective-permute-start | bytes 786440 | tf_op jit(solution)/shard_map/ppermute | solution.py:29
  40.1 15.7 %collective-permute-start.7 = (bf16[1024,128]{1,0:T(8,128)(2,1)}, bf16[1024,128]{1,0:T(8,128)(2,1)S(1)}, u32[]{:S(2)}, u32[]{:S(2)}) collective-permute-start(bf16[1024,128]{1,0:T(8,128)(2,1)} %get-tuple-element.7.refs_1_), channel_id=1, source_target_pairs={{0,6},{2,0},{4,2},{6,4},{1,7},{3,1},{5,3},{7,5},{8,14},{10,8},{12,... | collective-permute-start | bytes 786440 | tf_op jit(solution)/shard_map/ppermute | solution.py:29
  43.3 15.8 %collective-permute-start.3 = (bf16[1024,128]{1,0:T(8,128)(2,1)}, bf16[1024,128]{1,0:T(8,128)(2,1)S(1)}, u32[]{:S(2)}, u32[]{:S(2)}) collective-permute-start(bf16[1024,128]{1,0:T(8,128)(2,1)} %get-tuple-element.7.refs_1_), channel_id=1, source_target_pairs={{0,2},{2,4},{4,6},{6,0},{1,3},{3,5},{5,7},{7,1},{8,10},{10,12},{12... | collective-permute-start | bytes 786440 | tf_op jit(solution)/shard_map/ppermute | solution.py:29
  50.6 8.5 %collective-permute-start.1 = (bf16[1024,128]{1,0:T(8,128)(2,1)}, bf16[1024,128]{1,0:T(8,128)(2,1)}, u32[]{:S(2)}, u32[]{:S(2)}) collective-permute-start(bf16[1024,128]{1,0:T(8,128)(2,1)} %get-tuple-element.7.refs_1_), channel_id=1, source_target_pairs={{0,1},{1,0},{2,3},{3,2},{4,5},{5,4},{6,7},{7,6},{8,9},{9,8},{10,11... | collective-permute-start | bytes 786440 | tf_op jit(solution)/shard_map/ppermute | solution.py:29
  51.7 8.0 %collective-permute-start.8 = (bf16[1024,128]{1,0:T(8,128)(2,1)S(1)}, bf16[1024,128]{1,0:T(8,128)(2,1)}, u32[]{:S(2)}, u32[]{:S(2)}) collective-permute-start(bf16[1024,128]{1,0:T(8,128)(2,1)S(1)} %collective-permute-done.6.refs_8_), channel_id=1, source_target_pairs={{0,1},{1,0},{2,3},{3,2},{4,5},{5,4},{6,7},{7,6},{8,9},{9,8},{10,11... | collective-permute-start | bytes 786440 | tf_op jit(solution)/shard_map/ppermute | solution.py:29
  51.7 11.2 %collective-permute-start.10 = (bf16[1024,128]{1,0:T(8,128)(2,1)S(1)}, bf16[1024,128]{1,0:T(8,128)(2,1)}, u32[]{:S(2)}, u32[]{:S(2)}) collective-permute-start(bf16[1024,128]{1,0:T(8,128)(2,1)S(1)} %collective-permute-done.2.refs_4_), channel_id=1, source_target_pairs={{0,2},{2,4},{4,6},{6,0},{1,3},{3,5},{5,7},{7,1},{8,10},{10,12},{12... | collective-permute-start | bytes 786440 | tf_op jit(solution)/shard_map/ppermute | solution.py:29
  55.8 8.7 %collective-permute-start.11 = (bf16[1024,128]{1,0:T(8,128)(2,1)S(1)}, bf16[1024,128]{1,0:T(8,128)(2,1)}, u32[]{:S(2)}, u32[]{:S(2)}) collective-permute-start(bf16[1024,128]{1,0:T(8,128)(2,1)S(1)} %collective-permute-done.7.refs_9_), channel_id=1, source_target_pairs={{0,6},{2,0},{4,2},{6,4},{1,7},{3,1},{5,3},{7,5},{8,14},{10,8},{12,... | collective-permute-start | bytes 786440 | tf_op jit(solution)/shard_map/ppermute | solution.py:29
  59.1 7.2 %collective-permute-start.4 = (bf16[1024,128]{1,0:T(8,128)(2,1)S(1)}, bf16[1024,128]{1,0:T(8,128)(2,1)}, u32[]{:S(2)}, u32[]{:S(2)}) collective-permute-start(bf16[1024,128]{1,0:T(8,128)(2,1)S(1)} %collective-permute-done.2.refs_4_), channel_id=1, source_target_pairs={{0,1},{1,0},{2,3},{3,2},{4,5},{5,4},{6,7},{7,6},{8,9},{9,8},{10,11... | collective-permute-start | bytes 786440 | tf_op jit(solution)/shard_map/ppermute | solution.py:29
  59.2 7.1 %collective-permute-start.9 = (bf16[1024,128]{1,0:T(8,128)(2,1)S(1)}, bf16[1024,128]{1,0:T(8,128)(2,1)}, u32[]{:S(2)}, u32[]{:S(2)}) collective-permute-start(bf16[1024,128]{1,0:T(8,128)(2,1)S(1)} %collective-permute-done.7.refs_9_), channel_id=1, source_target_pairs={{0,1},{1,0},{2,3},{3,2},{4,5},{5,4},{6,7},{7,6},{8,9},{9,8},{10,11... | collective-permute-start | bytes 786440 | tf_op jit(solution)/shard_map/ppermute | solution.py:29
  59.7 6.6 %collective-permute-start.5 = (bf16[1024,128]{1,0:T(8,128)(2,1)S(1)}, bf16[1024,128]{1,0:T(8,128)(2,1)}, u32[]{:S(2)}, u32[]{:S(2)}) collective-permute-start(bf16[1024,128]{1,0:T(8,128)(2,1)S(1)} %collective-permute-done.3.refs_5_), channel_id=1, source_target_pairs={{0,1},{1,0},{2,3},{3,2},{4,5},{5,4},{6,7},{7,6},{8,9},{9,8},{10,11... | collective-permute-start | bytes 786440 | tf_op jit(solution)/shard_map/ppermute | solution.py:29
  63.0 3.4 %collective-permute-start.12 = (bf16[1024,128]{1,0:T(8,128)(2,1)}, bf16[1024,128]{1,0:T(8,128)(2,1)}, u32[]{:S(2)}, u32[]{:S(2)}) collective-permute-start(bf16[1024,128]{1,0:T(8,128)(2,1)} %collective-permute-done.10.refs_12_), channel_id=1, source_target_pairs={{0,1},{1,0},{2,3},{3,2},{4,5},{5,4},{6,7},{7,6},{8,9},{9,8},{10,11... | collective-permute-start | bytes 786440 | tf_op jit(solution)/shard_map/ppermute | solution.py:29
  64.5 1.9 %collective-permute-start.13 = (bf16[1024,128]{1,0:T(8,128)(2,1)}, bf16[1024,128]{1,0:T(8,128)(2,1)}, u32[]{:S(2)}, u32[]{:S(2)}) collective-permute-start(bf16[1024,128]{1,0:T(8,128)(2,1)} %collective-permute-done.11.refs_13_), channel_id=1, source_target_pairs={{0,1},{1,0},{2,3},{3,2},{4,5},{5,4},{6,7},{7,6},{8,9},{9,8},{10,11... | collective-permute-start | bytes 786440 | tf_op jit(solution)/shard_map/ppermute | solution.py:29
  74.5 16.1 %collective-permute-start.20 = (bf16[1024,256]{1,0:T(8,128)(2,1)}, bf16[1024,256]{1,0:T(8,128)(2,1)S(1)}, u32[]{:S(2)}, u32[]{:S(2)}) collective-permute-start(bf16[1024,256]{1,0:T(8,128)(2,1)} %get-tuple-element.8.refs_1_), channel_id=1, source_target_pairs={{0,6},{2,0},{4,2},{6,4},{1,7},{3,1},{5,3},{7,5},{8,14},{10,8},{12,... | collective-permute-start | bytes 1572872 | tf_op jit(solution)/shard_map/ppermute | solution.py:29
  78.1 16.2 %collective-permute-start.16 = (bf16[1024,256]{1,0:T(8,128)(2,1)}, bf16[1024,256]{1,0:T(8,128)(2,1)S(1)}, u32[]{:S(2)}, u32[]{:S(2)}) collective-permute-start(bf16[1024,256]{1,0:T(8,128)(2,1)} %get-tuple-element.8.refs_1_), channel_id=1, source_target_pairs={{0,2},{2,4},{4,6},{6,0},{1,3},{3,5},{5,7},{7,1},{8,10},{10,12},{12... | collective-permute-start | bytes 1572872 | tf_op jit(solution)/shard_map/ppermute | solution.py:29
  78.1 16.2 %collective-permute-start.14 = (bf16[1024,256]{1,0:T(8,128)(2,1)}, bf16[1024,256]{1,0:T(8,128)(2,1)S(1)}, u32[]{:S(2)}, u32[]{:S(2)}) collective-permute-start(bf16[1024,256]{1,0:T(8,128)(2,1)} %get-tuple-element.8.refs_1_), channel_id=1, source_target_pairs={{0,1},{1,0},{2,3},{3,2},{4,5},{5,4},{6,7},{7,6},{8,9},{9,8},{10,11... | collective-permute-start | bytes 1572872 | tf_op jit(solution)/shard_map/ppermute | solution.py:29
  78.2 23.2 %collective-permute-start.21 = (bf16[1024,256]{1,0:T(8,128)(2,1)}, bf16[1024,256]{1,0:T(8,128)(2,1)S(1)}, u32[]{:S(2)}, u32[]{:S(2)}) collective-permute-start(bf16[1024,256]{1,0:T(8,128)(2,1)} %get-tuple-element.9.refs_2_), channel_id=1, source_target_pairs={{0,6},{2,0},{4,2},{6,4},{1,7},{3,1},{5,3},{7,5},{8,14},{10,8},{12,... | collective-permute-start | bytes 1572872 | tf_op jit(solution)/shard_map/ppermute | solution.py:29
  81.3 24.3 %collective-permute-start.17 = (bf16[1024,256]{1,0:T(8,128)(2,1)}, bf16[1024,256]{1,0:T(8,128)(2,1)S(1)}, u32[]{:S(2)}, u32[]{:S(2)}) collective-permute-start(bf16[1024,256]{1,0:T(8,128)(2,1)} %get-tuple-element.9.refs_2_), channel_id=1, source_target_pairs={{0,2},{2,4},{4,6},{6,0},{1,3},{3,5},{5,7},{7,1},{8,10},{10,12},{12... | collective-permute-start | bytes 1572872 | tf_op jit(solution)/shard_map/ppermute | solution.py:29
  90.6 15.1 %collective-permute-start.15 = (bf16[1024,256]{1,0:T(8,128)(2,1)}, bf16[1024,256]{1,0:T(8,128)(2,1)S(1)}, u32[]{:S(2)}, u32[]{:S(2)}) collective-permute-start(bf16[1024,256]{1,0:T(8,128)(2,1)} %get-tuple-element.9.refs_2_), channel_id=1, source_target_pairs={{0,1},{1,0},{2,3},{3,2},{4,5},{5,4},{6,7},{7,6},{8,9},{9,8},{10,11... | collective-permute-start | bytes 1572872 | tf_op jit(solution)/shard_map/ppermute | solution.py:29
  94.2 12.0 %collective-permute-start.22 = (bf16[1024,256]{1,0:T(8,128)(2,1)S(1)}, bf16[1024,256]{1,0:T(8,128)(2,1)S(1)}, u32[]{:S(2)}, u32[]{:S(2)}) collective-permute-start(bf16[1024,256]{1,0:T(8,128)(2,1)S(1)} %collective-permute-done.20.refs_9_), channel_id=1, source_target_pairs={{0,1},{1,0},{2,3},{3,2},{4,5},{5,4},{6,7},{7,6},{8,9},{9,8},{10,11... | collective-permute-start | bytes 1572872 | tf_op jit(solution)/shard_map/ppermute | solution.py:29
  94.3 21.7 %collective-permute-start.24 = (bf16[1024,256]{1,0:T(8,128)(2,1)S(1)}, bf16[1024,256]{1,0:T(8,128)(2,1)S(1)}, u32[]{:S(2)}, u32[]{:S(2)}) collective-permute-start(bf16[1024,256]{1,0:T(8,128)(2,1)S(1)} %collective-permute-done.16.refs_5_), channel_id=1, source_target_pairs={{0,2},{2,4},{4,6},{6,0},{1,3},{3,5},{5,7},{7,1},{8,10},{10,12},{12... | collective-permute-start | bytes 1572872 | tf_op jit(solution)/shard_map/ppermute | solution.py:29
  101.4 14.7 %collective-permute-start.25 = (bf16[1024,256]{1,0:T(8,128)(2,1)S(1)}, bf16[1024,256]{1,0:T(8,128)(2,1)S(1)}, u32[]{:S(2)}, u32[]{:S(2)}) collective-permute-start(bf16[1024,256]{1,0:T(8,128)(2,1)S(1)} %collective-permute-done.21.refs_10_), channel_id=1, source_target_pairs={{0,6},{2,0},{4,2},{6,4},{1,7},{3,1},{5,3},{7,5},{8,14},{10,8},{12,... | collective-permute-start | bytes 1572872 | tf_op jit(solution)/shard_map/ppermute | solution.py:29
  105.6 11.5 %collective-permute-start.18 = (bf16[1024,256]{1,0:T(8,128)(2,1)S(1)}, bf16[1024,256]{1,0:T(8,128)(2,1)S(1)}, u32[]{:S(2)}, u32[]{:S(2)}) collective-permute-start(bf16[1024,256]{1,0:T(8,128)(2,1)S(1)} %collective-permute-done.16.refs_5_), channel_id=1, source_target_pairs={{0,1},{1,0},{2,3},{3,2},{4,5},{5,4},{6,7},{7,6},{8,9},{9,8},{10,11... | collective-permute-start | bytes 1572872 | tf_op jit(solution)/shard_map/ppermute | solution.py:29
  105.7 11.4 %collective-permute-start.23 = (bf16[1024,256]{1,0:T(8,128)(2,1)S(1)}, bf16[1024,256]{1,0:T(8,128)(2,1)S(1)}, u32[]{:S(2)}, u32[]{:S(2)}) collective-permute-start(bf16[1024,256]{1,0:T(8,128)(2,1)S(1)} %collective-permute-done.21.refs_10_), channel_id=1, source_target_pairs={{0,1},{1,0},{2,3},{3,2},{4,5},{5,4},{6,7},{7,6},{8,9},{9,8},{10,11... | collective-permute-start | bytes 1572872 | tf_op jit(solution)/shard_map/ppermute | solution.py:29
  106.2 10.9 %collective-permute-start.19 = (bf16[1024,256]{1,0:T(8,128)(2,1)S(1)}, bf16[1024,256]{1,0:T(8,128)(2,1)S(1)}, u32[]{:S(2)}, u32[]{:S(2)}) collective-permute-start(bf16[1024,256]{1,0:T(8,128)(2,1)S(1)} %collective-permute-done.17.refs_6_), channel_id=1, source_target_pairs={{0,1},{1,0},{2,3},{3,2},{4,5},{5,4},{6,7},{7,6},{8,9},{9,8},{10,11... | collective-permute-start | bytes 1572872 | tf_op jit(solution)/shard_map/ppermute | solution.py:29
  115.9 1.9 %collective-permute-start.26 = (bf16[1024,256]{1,0:T(8,128)(2,1)S(1)}, bf16[1024,256]{1,0:T(8,128)(2,1)S(1)}, u32[]{:S(2)}, u32[]{:S(2)}) collective-permute-start(bf16[1024,256]{1,0:T(8,128)(2,1)S(1)} %collective-permute-done.24.refs_13_), channel_id=1, source_target_pairs={{0,1},{1,0},{2,3},{3,2},{4,5},{5,4},{6,7},{7,6},{8,9},{9,8},{10,11... | collective-permute-start | bytes 1572872 | tf_op jit(solution)/shard_map/ppermute | solution.py:29
  116.1 3.0 %collective-permute-start.27 = (bf16[1024,256]{1,0:T(8,128)(2,1)S(1)}, bf16[1024,256]{1,0:T(8,128)(2,1)}, u32[]{:S(2)}, u32[]{:S(2)}) collective-permute-start(bf16[1024,256]{1,0:T(8,128)(2,1)S(1)} %collective-permute-done.25.refs_14_), channel_id=1, source_target_pairs={{0,1},{1,0},{2,3},{3,2},{4,5},{5,4},{6,7},{7,6},{8,9},{9,8},{10,11... | collective-permute-start | bytes 1572872 | tf_op jit(solution)/shard_map/ppermute | solution.py:29
  155.5 10.0 %all-to-all-start.1 = ((f32[8,2,1024]{2,1,0:T(2,128)}), f32[8,2,1024]{2,1,0:T(2,128)S(1)}, u32[]{:S(2)}, u32[]{:S(2)}) async-start(f32[8,2,1024]{2,1,0:T(2,128)} %broadcast_in_dim.38), calls=%async_computation.1 | async-start | bytes 131072 | tf_op jit(solution)/shard_map/all_to_all | solution.py:24
  (20 other events, 275.9 us)
Sparse Core Ops, SparseCore 0:
  10.9 113.6 all-gather.1

commit v7 on v6

--- a/solution.py
+++ b/solution.py
@@ -209,7 +209,7 @@
     rows = contexts[0].shape[0]
     part = out_cols.shape[2]
     target_len = target_embed.shape[1]
-    tile = target_len
+    tile = target_len // 2
     return pl.pallas_call(
         output_kernel,
         out_shape=[jax.ShapeDtypeStruct((rows, part // 2), jnp.bfloat16)] * 2,
@@ -219,7 +219,7 @@
             in_specs=[
                 *(pl.BlockSpec((tile, c.shape[1]), lambda i, at: (i, 0)) for c in contexts),
                 pl.BlockSpec(out_cols.shape, lambda i, at: (0, 0, 0)),
-                pl.BlockSpec((1, tile, part), lambda i, at: (0, 0, at[0])),
+                pl.BlockSpec((1, tile, part), lambda i, at: (0, i % 2, at[0])),
                 pl.BlockSpec((1, part), lambda i, at: (0, at[0])),
             ],
             out_specs=[pl.BlockSpec((tile, part // 2), lambda i, at: (i, 0))] * 2,
@@ -234,11 +234,11 @@
 
 def vocab_kernel(first_ref, *refs, n_rows):
     row_refs = refs[:n_rows]
-    degain_ref, label_ref, w_ref, out_ref = refs[n_rows : n_rows + 4]
+    scale_ref, label_ref, w_ref, out_ref = refs[n_rows : n_rows + 4]
     rows_s, first_s, second_s, top_s, sum_s, pick_s, scale_s, label_s = refs[n_rows + 4 :]
     step = pl.program_id(0)
     n_steps = pl.num_programs(0)
-    rows, width = rows_s.shape
+    rows = rows_s.shape[0]
     tile, columns = first_s.shape
     n_tiles = rows // tile
     at_tile = lambda t: slice(t * tile, (t + 1) * tile)
@@ -246,16 +246,11 @@
 
     @pl.when(step == 0)
     def _():
-        squares = jnp.zeros((rows, 128), jnp.float32)
-        k = 0
-        for ref in row_refs:
-            rows_s[:, k : k + ref.shape[1]] = ref[...]
-            for i in range(0, ref.shape[1], 128):
-                x = ref[:, i : i + 128].astype(jnp.float32) * degain_ref[:, k + i : k + i + 128]
-                squares += x * x
-            k += ref.shape[1]
-        mean = jnp.sum(squares, axis=1, keepdims=True) / width
-        scale_s[...] = jnp.broadcast_to(lax.rsqrt(mean + EPSILON) * LOG2E, scale_s.shape)
+        for k, ref in enumerate(row_refs):
+            wide = ref.shape[1]
+            at = (first_ref[2 + k // 2] * 2 + k % 2) * wide
+            rows_s[:, pl.ds(pl.multiple_of(at, wide), wide)] = ref[...]
+        scale_s[...] = jnp.broadcast_to(scale_ref[...], scale_s.shape)
         label_s[...] = jnp.broadcast_to(label_ref[...], label_s.shape)
         top_s[...] = jnp.full_like(top_s, MASKED)
         sum_s[...] = jnp.zeros_like(sum_s)
@@ -297,7 +292,7 @@
         out_ref[...] = both.T[:2, :]
 
 
-def vocab_stats(first, row_blocks, degain, row_labels, vocab_all):
+def vocab_stats(first, row_blocks, scale, row_labels, vocab_all):
     n_rows = row_blocks[0].shape[0]
     n_blocks, width, columns = vocab_all.shape
     tile = 256
@@ -311,7 +306,7 @@
             grid=(n_blocks,),
             in_specs=[
                 *(whole(b) for b in row_blocks),
-                whole(degain),
+                whole(scale),
                 whole(row_labels),
                 pl.BlockSpec((1, width, columns), lambda j, f: (j, 0, 0)),
             ],
@@ -330,40 +325,7 @@
             transcendentals=n_rows * n_blocks * columns,
         ),
         name="vocab_stats",
-    )(first, *row_blocks, degain, row_labels, vocab_all)
-
-
-def piece_kernel(row_ref, vocab_ref, piece_ref, sem):
-    part = piece_ref.shape[0] // 2
-    started = [
-        pltpu.make_async_copy(
-            vocab_ref.at[pl.ds(pl.multiple_of(row_ref[i] * part, part), part)],
-            piece_ref.at[i * part : (i + 1) * part],
-            sem.at[i],
-        )
-        for i in range(2)
-    ]
-    for copy in started:
-        copy.start()
-    for copy in started:
-        copy.wait()
-
-
-def vocab_piece(places, w_vocab, part):
-    return pl.pallas_call(
-        piece_kernel,
-        out_shape=jax.ShapeDtypeStruct((2 * part, w_vocab.shape[1]), jnp.bfloat16),
-        grid_spec=pltpu.PrefetchScalarGridSpec(
-            num_scalar_prefetch=1,
-            grid=(),
-            in_specs=[pl.BlockSpec(memory_space=pl.ANY)],
-            out_specs=pl.BlockSpec(memory_space=pltpu.VMEM),
-            scratch_shapes=[pltpu.SemaphoreType.DMA((2,))],
-        ),
-        compiler_params=pltpu.CompilerParams(vmem_limit_bytes=VMEM_LIMIT),
-        cost_estimate=pl.CostEstimate(flops=0, bytes_accessed=2 << 20, transcendentals=0),
-        name="vocab_piece",
-    )(places, w_vocab)
+    )(first, *row_blocks, scale, row_labels, vocab_all)
 
 
 def split_kernel(w_ref, out_ref):
@@ -401,11 +363,8 @@
     places = [((z_index + r) % 4) * 2 + (core + k) % 2 for r in RING for k in range(2)]
 
     place_ids = jnp.stack(places).astype(jnp.int32)
-    x_index = lax.axis_index("prompt")
-    turn = jnp.where(x_index == 0, 0, jnp.where(x_index == 1, 3, x_index - 1))
-    my_pair = ((z_index + turn) % 4) * 2
-    pair = jnp.stack([my_pair + core, my_pair + 1 - core]).astype(jnp.int32)
-    piece = vocab_piece(pair, w_vocab, part)
+    share = model_width // n_prompt
+    piece = lax.dynamic_slice_in_dim(w_vocab, lax.axis_index("prompt") * share, share, 0)
     vocab_all = lax.all_gather(piece, ("dp", "prompt"), axis=0, tiled=True)
     vocab_all = vocab_all.reshape(n_dp, model_width, vocab_cols)
     by_part = split_columns(w_out, n_model)
@@ -416,12 +375,17 @@
     halves = output_part(place_ids, contexts, out_cols, target_embed, final_gain)
     row_blocks = whole_row(*halves)
 
-    degain = 1.0 / jnp.concatenate(
-        [lax.dynamic_slice_in_dim(final_gain, p * part, part, 0) for p in places], axis=0
-    ).reshape(1, -1)
+    squares = 0.0
+    for k, block in enumerate(row_blocks):
+        wide = block.shape[1]
+        gain = lax.dynamic_slice_in_dim(final_gain, (places[k // 2] * 2 + k % 2) * wide, wide, 0)
+        unscaled = block.astype(jnp.float32) / gain
+        squares = squares + jnp.sum(unscaled * unscaled, axis=1, keepdims=True)
+    scale = lax.rsqrt(squares / model_width + EPSILON) * LOG2E
     row_labels = jnp.tile(labels.reshape(-1, 1), (prompts_here, 1))
-    first = jnp.stack([lax.axis_index(MP) * vocab_cols, n_model * vocab_cols]).astype(jnp.int32)
-    here = vocab_stats(first, row_blocks, degain, row_labels, vocab_all)
+    first = [lax.axis_index(MP) * vocab_cols, n_model * vocab_cols, *places]
+    first = jnp.stack(first).astype(jnp.int32)
+    here = vocab_stats(first, row_blocks, scale, row_labels, vocab_all)
 
     every = of_each(here, MP)
     top_val = jnp.max(every[:, 0], axis=0)

time: 188 us -> 187 us (level)
  Pallas kernels: 56.3 us -> 52.3 us
  starting transfers between devices: 32.2 us -> 28.4 us
  other arithmetic: 3.9 us -> 7.55 us
  local copies, waits for them, and re-layouts: 9.96 us -> 12.5 us
    all_gather x1, waiting for transfers between devices: 5.48 us -> 0.18 us  [shards(): vocab_all = lax.all_gather(piece, ('dp', 'prompt'), axis=0, tiled=True)]
    reduce_sum x0 -> x15, other arithmetic: none -> 4.53 us  [shards(): squares = squares + jnp.sum(unscaled * unscaled, axis=1, keepdims=True)]
    ppermute x28, waiting for transfers between devices: 46.6 us -> 50.7 us  [shifted(): return lax.ppermute(value, axis, [(i, (i + shift) % n) for i in range(n)])]
    ppermute x28, starting transfers between devices: 22.4 us -> 18.5 us  [shifted(): return lax.ppermute(value, axis, [(i, (i + shift) % n) for i in range(n)])]
    pallas_call x1 -> x0, Pallas kernels: 2.87 us -> none  [vocab_piece(): pl.pallas_call(piece_kernel, out_shape=jax.ShapeDtypeStruct((2 * part, w_...]
    dynamic_slice x1 -> x2, local copies, waits for them, and re-layouts: 0.1 us -> 2.43 us  [the longest x1 2.29 us: shards(): lax.dynamic_slice_in_dim(w_vocab, lax.axis_index('prompt') * share, share...]
    pallas_call x1, Pallas kernels: 29.6 us -> 27.6 us  [vocab_stats(): pl.pallas_call(kernel, out_shape=jax.ShapeDtypeStruct((2, n_rows), jnp.fl...]
    unnamed x53 -> x52, local copies, waits for them, and re-layouts: 7.26 us -> 6.55 us
  transfers between devices with their start and end apart: 31 -> 31, of which waited for: 14 -> 15; matrix products, arithmetic and copies ran while one was open for 4% -> 6% of each run, Pallas kernels for 13% -> 13%
where the time goes in v7:
time: 187 us; the launch traced here: 186 us
  waiting for transfers between devices  56.5 us (30%)
  Pallas kernels  52.3 us (28%)
  starting transfers between devices  28.4 us (15%)
  between operations  15.2 us (8%)
  blocking collectives  13.6 us (7%)
  local copies, waits for them, and re-layouts  12.5 us (7%)
  other arithmetic  7.55 us (4%)
    ppermute x28, waiting for transfers between devices, shifted(): return lax.ppermute(value, axis, [(i, (i + shift) % n) for i in range(n)])  50.7 us
    pallas_call x1, Pallas kernels, vocab_stats(): pl.pallas_call(kernel, out_shape=jax.ShapeDtypeStruct((2, n_rows), jnp.fl...  27.6 us
    ppermute x28, starting transfers between devices, shifted(): return lax.ppermute(value, axis, [(i, (i + shift) % n) for i in range(n)])  18.5 us
    pallas_call x1, Pallas kernels, attention(): pl.pallas_call(attention_kernel, out_shape=[jax.ShapeDtypeStruct((rows, i...  14.4 us
    all_to_all x1, blocking collectives, of_each(): return lax.all_to_all(copies, axis, split_axis=0, concat_axis=0, tiled=True)  13.6 us
    pallas_call x1, Pallas kernels, output_part(): pl.pallas_call(output_kernel, out_shape=[jax.ShapeDtypeStruct((rows, part...  7.57 us
    unnamed x52, local copies, waits for them, and re-layouts  6.55 us
    all_to_all x1, waiting for transfers between devices, of_each(): return lax.all_to_all(copies, axis, split_axis=0, concat_axis=0, tiled=True)  5.62 us
  transfers between devices with their start and end apart: 31, of which 15 were waited for; matrix products, arithmetic and copies ran while one was open for 6% of the time, Pallas kernels for 13%

profile of v7, /device:TPU:0, one launch (start us, length us, event | category | flops | bytes accessed | tf_op | source)
XLA Modules:
  0.0 186.2 jit_solution(6761169693926530078)
XLA Ops:
  7.2 2.3 %constant_dynamic-slice_fusion = bf16[1024,512]{1,0:T(8,128)(2,1)} fusion(bf16[4096,512]{1,0:T(8,128)(2,1)} %param.21, s32[]{:T(128)S(6)} %select_n.136), kind=kLoop, calls=%fused_computation.31 | loop fusion | bytes 2097156 | tf_op jit(solution)/shard_map/dynamic_slice | solution.py:367
  9.5 2.7 %split_columns.1 = bf16[8,256,512]{2,1,0:T(8,128)(2,1)} custom-call(bf16[256,4096]{1,0:T(8,128)(2,1)} %w_ref.3), custom_call_target="tpu_custom_call" | custom-call | bytes 4194304 | tf_op jit(solution)/shard_map/split_columns/pallas_call | solution.py:340
  12.3 5.4 %all-to-all-start = ((bf16[8,256,512]{2,1,0:T(8,128)(2,1)}), bf16[8,256,512]{2,1,0:T(8,128)(2,1)S(1)}, u32[]{:S(2)}, u32[]{:S(2)}) async-start(bf16[8,256,512]{2,1,0:T(8,128)(2,1)} %split_columns.1), calls=%async_computation | async-start | bytes 4194304 | tf_op jit(solution)/shard_map/all_to_all | solution.py:371
  17.7 3.6 %copy.34.prompt_ref = bf16[2,100,4096]{2,1,0:T(8,128)(2,1)} copy(bf16[2,100,4096]{2,0,1:T(2,128)(2,1)} %param.13) | data formatting | bytes 3276800 | tf_op args[0]
  21.2 14.4 %attention.1 = (bf16[1024,128]{1,0:T(8,128)(2,1)}, bf16[1024,128]{1,0:T(8,128)(2,1)}) custom-call(bf16[1,512,4096]{2,1,0:T(8,128)(2,1)} %refs_17_.1, bf16[2,100,4096]{2,1,0:T(8,128)(2,1)} %copy.34.prompt_ref, f32[1,4096]{1,0:T(1,128)} %bitcast.38, bf16[3,4096,256]{2,1,0:T(8,128)(2,1)} %w_ref.2, f32[512,64]{1,0:T(8,128)} %constant.113.clone.cos_t, ...), custom_call_target="tpu_custom_call" | custom-call | flops 8000000000 | bytes 12000000 | tf_op jit(solution)/shard_map/attention/pallas_call | solution.py:168
  35.7 3.2 %collective-permute-start.6 = (bf16[1024,128]{1,0:T(8,128)(2,1)}, bf16[1024,128]{1,0:T(8,128)(2,1)S(1)}, u32[]{:S(2)}, u32[]{:S(2)}) collective-permute-start(bf16[1024,128]{1,0:T(8,128)(2,1)} %get-tuple-element.6.refs_0_), channel_id=1, source_target_pairs={{0,6},{2,0},{4,2},{6,4},{1,7},{3,1},{5,3},{7,5},{8,14},{10,8},{12,... | collective-permute-start | bytes 786440 | tf_op jit(solution)/shard_map/ppermute | solution.py:29
  38.9 3.2 %collective-permute-start.7 = (bf16[1024,128]{1,0:T(8,128)(2,1)}, bf16[1024,128]{1,0:T(8,128)(2,1)S(1)}, u32[]{:S(2)}, u32[]{:S(2)}) collective-permute-start(bf16[1024,128]{1,0:T(8,128)(2,1)} %get-tuple-element.7.refs_1_), channel_id=1, source_target_pairs={{0,6},{2,0},{4,2},{6,4},{1,7},{3,1},{5,3},{7,5},{8,14},{10,8},{12,... | collective-permute-start | bytes 786440 | tf_op jit(solution)/shard_map/ppermute | solution.py:29
  42.2 7.3 %collective-permute-done.6.refs_8_ = bf16[1024,128]{1,0:T(8,128)(2,1)S(1)} collective-permute-done((bf16[1024,128]{1,0:T(8,128)(2,1)}, bf16[1024,128]{1,0:T(8,128)(2,1)S(1)}, u32[]{:S(2)}, u32[]{:S(2)}) %collective-permute-start.6) | collective-permute-done | bytes 262176 | tf_op jit(solution)/shard_map/ppermute | solution.py:29
  49.5 1.1 collective-permute-done.2.refs_4_
  50.6 1.0 collective-permute-start.10
  51.6 3.0 %collective-permute-done.7.refs_9_ = bf16[1024,128]{1,0:T(8,128)(2,1)S(1)} collective-permute-done((bf16[1024,128]{1,0:T(8,128)(2,1)}, bf16[1024,128]{1,0:T(8,128)(2,1)S(1)}, u32[]{:S(2)}, u32[]{:S(2)}) %collective-permute-start.7) | collective-permute-done | bytes 262176 | tf_op jit(solution)/shard_map/ppermute | solution.py:29
  54.6 2.6 %collective-permute-start.11 = (bf16[1024,128]{1,0:T(8,128)(2,1)S(1)}, bf16[1024,128]{1,0:T(8,128)(2,1)}, u32[]{:S(2)}, u32[]{:S(2)}) collective-permute-start(bf16[1024,128]{1,0:T(8,128)(2,1)S(1)} %collective-permute-done.7.refs_9_), channel_id=1, source_target_pairs={{0,6},{2,0},{4,2},{6,4},{1,7},{3,1},{5,3},{7,5},{8,14},{10,8},{12,... | collective-permute-start | bytes 786440 | tf_op jit(solution)/shard_map/ppermute | solution.py:29
  57.9 3.9 %collective-permute-done.10.refs_12_ = bf16[1024,128]{1,0:T(8,128)(2,1)} collective-permute-done((bf16[1024,128]{1,0:T(8,128)(2,1)S(1)}, bf16[1024,128]{1,0:T(8,128)(2,1)}, u32[]{:S(2)}, u32[]{:S(2)}) %collective-permute-start.10) | collective-permute-done | bytes 262176 | tf_op jit(solution)/shard_map/ppermute | solution.py:29
  61.8 1.5 collective-permute-done.11.refs_13_
  64.2 1.1 copy.48
  66.6 1.3 copy-done.1
  68.0 7.6 %output_part.1 = (bf16[1024,256]{1,0:T(8,128)(2,1)}, bf16[1024,256]{1,0:T(8,128)(2,1)}) custom-call(s32[8]{0:T(128)} %stack.51.places_ref, bf16[1024,128]{1,0:T(8,128)(2,1)} %get-tuple-element.6.refs_0_, bf16[1024,128]{1,0:T(8,128)(2,1)} %get-tuple-element.7.refs_1_, bf16[1024,128]{1,0:T(8,128)(2,1)} %copy-done.18, bf16[1024,128]{1,0:T(8,128)(2,1)} %copy-done.21, ...), custom_call_target="tpu_custom_call" | custom-call | flops 2000000000 | bytes 8000000 | tf_op jit(solution)/shard_map/output_part/pallas_call | solution.py:213
  75.5 3.5 %collective-permute-start.20 = (bf16[1024,256]{1,0:T(8,128)(2,1)}, bf16[1024,256]{1,0:T(8,128)(2,1)S(1)}, u32[]{:S(2)}, u32[]{:S(2)}) collective-permute-start(bf16[1024,256]{1,0:T(8,128)(2,1)} %get-tuple-element.8.refs_1_), channel_id=1, source_target_pairs={{0,6},{2,0},{4,2},{6,4},{1,7},{3,1},{5,3},{7,5},{8,14},{10,8},{12,... | collective-permute-start | bytes 1572872 | tf_op jit(solution)/shard_map/ppermute | solution.py:29
  79.6 3.1 %collective-permute-start.21 = (bf16[1024,256]{1,0:T(8,128)(2,1)}, bf16[1024,256]{1,0:T(8,128)(2,1)S(1)}, u32[]{:S(2)}, u32[]{:S(2)}) collective-permute-start(bf16[1024,256]{1,0:T(8,128)(2,1)} %get-tuple-element.9.refs_2_), channel_id=1, source_target_pairs={{0,6},{2,0},{4,2},{6,4},{1,7},{3,1},{5,3},{7,5},{8,14},{10,8},{12,... | collective-permute-start | bytes 1572872 | tf_op jit(solution)/shard_map/ppermute | solution.py:29
  82.7 1.6 multiply_reduce_fusion.14
  84.2 7.4 %collective-permute-done.20.refs_9_ = bf16[1024,256]{1,0:T(8,128)(2,1)S(1)} collective-permute-done((bf16[1024,256]{1,0:T(8,128)(2,1)}, bf16[1024,256]{1,0:T(8,128)(2,1)S(1)}, u32[]{:S(2)}, u32[]{:S(2)}) %collective-permute-start.20) | collective-permute-done | bytes 524320 | tf_op jit(solution)/shard_map/ppermute | solution.py:29
  91.9 3.8 %collective-permute-done.16.refs_5_ = bf16[1024,256]{1,0:T(8,128)(2,1)S(1)} collective-permute-done((bf16[1024,256]{1,0:T(8,128)(2,1)}, bf16[1024,256]{1,0:T(8,128)(2,1)S(1)}, u32[]{:S(2)}, u32[]{:S(2)}) %collective-permute-start.16) | collective-permute-done | bytes 524320 | tf_op jit(solution)/shard_map/ppermute | solution.py:29
  96.2 6.1 %collective-permute-done.21.refs_10_ = bf16[1024,256]{1,0:T(8,128)(2,1)S(1)} collective-permute-done((bf16[1024,256]{1,0:T(8,128)(2,1)}, bf16[1024,256]{1,0:T(8,128)(2,1)S(1)}, u32[]{:S(2)}, u32[]{:S(2)}) %collective-permute-start.21) | collective-permute-done | bytes 524320 | tf_op jit(solution)/shard_map/ppermute | solution.py:29
  102.5 4.4 %collective-permute-done.17.refs_6_ = bf16[1024,256]{1,0:T(8,128)(2,1)S(1)} collective-permute-done((bf16[1024,256]{1,0:T(8,128)(2,1)}, bf16[1024,256]{1,0:T(8,128)(2,1)S(1)}, u32[]{:S(2)}, u32[]{:S(2)}) %collective-permute-start.17) | collective-permute-done | bytes 524320 | tf_op jit(solution)/shard_map/ppermute | solution.py:29
  107.4 9.8 %collective-permute-done.24.refs_13_ = bf16[1024,256]{1,0:T(8,128)(2,1)S(1)} collective-permute-done((bf16[1024,256]{1,0:T(8,128)(2,1)S(1)}, bf16[1024,256]{1,0:T(8,128)(2,1)S(1)}, u32[]{:S(2)}, u32[]{:S(2)}) %collective-permute-start.24) | collective-permute-done | bytes 524320 | tf_op jit(solution)/shard_map/ppermute | solution.py:29
  117.4 1.7 collective-permute-done.25.refs_14_
  123.9 27.6 %vocab_stats.1 = f32[2,1024]{1,0:T(2,128)} custom-call(s32[10]{0:T(128)} %stack.50.refs_0_, bf16[1024,256]{1,0:T(8,128)(2,1)} %get-tuple-element.8.refs_1_, bf16[1024,256]{1,0:T(8,128)(2,1)} %get-tuple-element.9.refs_2_, bf16[1024,256]{1,0:T(8,128)(2,1)} %copy-done.4, bf16[1024,256]{1,0:T(8,128)(2,1)} %copy-done.7, bf16[1024,256]{1,0:T(8,128)(2,1)} %copy-done.3, ...), custom_call_target="tpu_custom_call" | custom-call | flops 17179869184 | bytes 25165824 | tf_op jit(solution)/shard_map/vocab_stats/pallas_call | solution.py:301
  151.5 1.3 broadcast_in_dim.21
  152.8 4.5 %all-to-all-start.1 = ((f32[8,2,1024]{2,1,0:T(2,128)}), f32[8,2,1024]{2,1,0:T(2,128)S(1)}, u32[]{:S(2)}, u32[]{:S(2)}) async-start(f32[8,2,1024]{2,1,0:T(2,128)} %broadcast_in_dim.21), calls=%async_computation.1 | async-start | bytes 131072 | tf_op jit(solution)/shard_map/all_to_all | solution.py:24
  157.3 5.6 %all-to-all-done.1 = f32[8,2,1024]{2,1,0:T(2,128)S(1)} async-done(((f32[8,2,1024]{2,1,0:T(2,128)}), f32[8,2,1024]{2,1,0:T(2,128)S(1)}, u32[]{:S(2)}, u32[]{:S(2)}) %all-to-all-start.1) | async-done | bytes 65568 | tf_op jit(solution)/shard_map/all_to_all | solution.py:24
  163.8 13.6 %all_to_all.16 = f32[16,1,9]{2,1,0:T(1,128)S(1)} all-to-all(f32[16,1,9]{2,1,0:T(1,128)S(1)} %broadcast_in_dim.25), channel_id=1, replica_groups=mesh['prompt'=4,'dp'=4,'mp_0'=4,'mp_1'=2] {'prompt','dp'}, dimensions={0} | all-to-all | bytes 1152 | tf_op jit(solution)/shard_map/all_to_all | solution.py:24
  178.1 1.2 multiply_divide_fusion
  (123 shorter events, 10.4 us)
Async XLA Ops:
  7.2 57.0 %copy-start = (s32[1,512]{1,0:T(1,128)S(1)}, s32[1,512]{1,0:T(1,128)}, u32[]{:S(2)}) copy-start(s32[1,512]{1,0:T(1,128)} %param.15) | copy-start | bytes 6148
  7.2 116.7 %all-gather.2.cloned.1.call-start = ((), (), s32[]{:S(2)}) async-start(), calls=%async_computation.3 | async-start | bytes 17825792 | tf_op jit(solution)/shard_map/all_gather | solution.py:368
  12.3 54.3 %all-to-all-start = ((bf16[8,256,512]{2,1,0:T(8,128)(2,1)}), bf16[8,256,512]{2,1,0:T(8,128)(2,1)S(1)}, u32[]{:S(2)}, u32[]{:S(2)}) async-start(bf16[8,256,512]{2,1,0:T(8,128)(2,1)} %split_columns.1), calls=%async_computation | async-start | bytes 4194304 | tf_op jit(solution)/shard_map/all_to_all | solution.py:371
  35.7 13.8 %collective-permute-start.6 = (bf16[1024,128]{1,0:T(8,128)(2,1)}, bf16[1024,128]{1,0:T(8,128)(2,1)S(1)}, u32[]{:S(2)}, u32[]{:S(2)}) collective-permute-start(bf16[1024,128]{1,0:T(8,128)(2,1)} %get-tuple-element.6.refs_0_), channel_id=1, source_target_pairs={{0,6},{2,0},{4,2},{6,4},{1,7},{3,1},{5,3},{7,5},{8,14},{10,8},{12,... | collective-permute-start | bytes 786440 | tf_op jit(solution)/shard_map/ppermute | solution.py:29
  38.9 11.6 %collective-permute-start.2 = (bf16[1024,128]{1,0:T(8,128)(2,1)}, bf16[1024,128]{1,0:T(8,128)(2,1)S(1)}, u32[]{:S(2)}, u32[]{:S(2)}) collective-permute-start(bf16[1024,128]{1,0:T(8,128)(2,1)} %get-tuple-element.6.refs_0_), channel_id=1, source_target_pairs={{0,2},{2,4},{4,6},{6,0},{1,3},{3,5},{5,7},{7,1},{8,10},{10,12},{12... | collective-permute-start | bytes 786440 | tf_op jit(solution)/shard_map/ppermute | solution.py:29
  38.9 11.6 %collective-permute-start = (bf16[1024,128]{1,0:T(8,128)(2,1)}, bf16[1024,128]{1,0:T(8,128)(2,1)S(1)}, u32[]{:S(2)}, u32[]{:S(2)}) collective-permute-start(bf16[1024,128]{1,0:T(8,128)(2,1)} %get-tuple-element.6.refs_0_), channel_id=1, source_target_pairs={{0,1},{1,0},{2,3},{3,2},{4,5},{5,4},{6,7},{7,6},{8,9},{9,8},{10,11... | collective-permute-start | bytes 786440 | tf_op jit(solution)/shard_map/ppermute | solution.py:29
  38.9 15.7 %collective-permute-start.7 = (bf16[1024,128]{1,0:T(8,128)(2,1)}, bf16[1024,128]{1,0:T(8,128)(2,1)S(1)}, u32[]{:S(2)}, u32[]{:S(2)}) collective-permute-start(bf16[1024,128]{1,0:T(8,128)(2,1)} %get-tuple-element.7.refs_1_), channel_id=1, source_target_pairs={{0,6},{2,0},{4,2},{6,4},{1,7},{3,1},{5,3},{7,5},{8,14},{10,8},{12,... | collective-permute-start | bytes 786440 | tf_op jit(solution)/shard_map/ppermute | solution.py:29
  42.2 15.1 %collective-permute-start.3 = (bf16[1024,128]{1,0:T(8,128)(2,1)}, bf16[1024,128]{1,0:T(8,128)(2,1)S(1)}, u32[]{:S(2)}, u32[]{:S(2)}) collective-permute-start(bf16[1024,128]{1,0:T(8,128)(2,1)} %get-tuple-element.7.refs_1_), channel_id=1, source_target_pairs={{0,2},{2,4},{4,6},{6,0},{1,3},{3,5},{5,7},{7,1},{8,10},{10,12},{12... | collective-permute-start | bytes 786440 | tf_op jit(solution)/shard_map/ppermute | solution.py:29
  49.5 7.8 %collective-permute-start.1 = (bf16[1024,128]{1,0:T(8,128)(2,1)}, bf16[1024,128]{1,0:T(8,128)(2,1)S(1)}, u32[]{:S(2)}, u32[]{:S(2)}) collective-permute-start(bf16[1024,128]{1,0:T(8,128)(2,1)} %get-tuple-element.7.refs_1_), channel_id=1, source_target_pairs={{0,1},{1,0},{2,3},{3,2},{4,5},{5,4},{6,7},{7,6},{8,9},{9,8},{10,11... | collective-permute-start | bytes 786440 | tf_op jit(solution)/shard_map/ppermute | solution.py:29
  50.6 7.2 %collective-permute-start.8 = (bf16[1024,128]{1,0:T(8,128)(2,1)S(1)}, bf16[1024,128]{1,0:T(8,128)(2,1)S(1)}, u32[]{:S(2)}, u32[]{:S(2)}) collective-permute-start(bf16[1024,128]{1,0:T(8,128)(2,1)S(1)} %collective-permute-done.6.refs_8_), channel_id=1, source_target_pairs={{0,1},{1,0},{2,3},{3,2},{4,5},{5,4},{6,7},{7,6},{8,9},{9,8},{10,11... | collective-permute-start | bytes 786440 | tf_op jit(solution)/shard_map/ppermute | solution.py:29
  50.6 11.2 %collective-permute-start.10 = (bf16[1024,128]{1,0:T(8,128)(2,1)S(1)}, bf16[1024,128]{1,0:T(8,128)(2,1)}, u32[]{:S(2)}, u32[]{:S(2)}) collective-permute-start(bf16[1024,128]{1,0:T(8,128)(2,1)S(1)} %collective-permute-done.2.refs_4_), channel_id=1, source_target_pairs={{0,2},{2,4},{4,6},{6,0},{1,3},{3,5},{5,7},{7,1},{8,10},{10,12},{12... | collective-permute-start | bytes 786440 | tf_op jit(solution)/shard_map/ppermute | solution.py:29
  54.6 8.7 %collective-permute-start.11 = (bf16[1024,128]{1,0:T(8,128)(2,1)S(1)}, bf16[1024,128]{1,0:T(8,128)(2,1)}, u32[]{:S(2)}, u32[]{:S(2)}) collective-permute-start(bf16[1024,128]{1,0:T(8,128)(2,1)S(1)} %collective-permute-done.7.refs_9_), channel_id=1, source_target_pairs={{0,6},{2,0},{4,2},{6,4},{1,7},{3,1},{5,3},{7,5},{8,14},{10,8},{12,... | collective-permute-start | bytes 786440 | tf_op jit(solution)/shard_map/ppermute | solution.py:29
  57.3 9.2 %collective-permute-start.4 = (bf16[1024,128]{1,0:T(8,128)(2,1)S(1)}, bf16[1024,128]{1,0:T(8,128)(2,1)}, u32[]{:S(2)}, u32[]{:S(2)}) collective-permute-start(bf16[1024,128]{1,0:T(8,128)(2,1)S(1)} %collective-permute-done.2.refs_4_), channel_id=1, source_target_pairs={{0,1},{1,0},{2,3},{3,2},{4,5},{5,4},{6,7},{7,6},{8,9},{9,8},{10,11... | collective-permute-start | bytes 786440 | tf_op jit(solution)/shard_map/ppermute | solution.py:29
  57.3 9.2 %collective-permute-start.9 = (bf16[1024,128]{1,0:T(8,128)(2,1)S(1)}, bf16[1024,128]{1,0:T(8,128)(2,1)}, u32[]{:S(2)}, u32[]{:S(2)}) collective-permute-start(bf16[1024,128]{1,0:T(8,128)(2,1)S(1)} %collective-permute-done.7.refs_9_), channel_id=1, source_target_pairs={{0,1},{1,0},{2,3},{3,2},{4,5},{5,4},{6,7},{7,6},{8,9},{9,8},{10,11... | collective-permute-start | bytes 786440 | tf_op jit(solution)/shard_map/ppermute | solution.py:29
  57.8 8.7 %collective-permute-start.5 = (bf16[1024,128]{1,0:T(8,128)(2,1)S(1)}, bf16[1024,128]{1,0:T(8,128)(2,1)}, u32[]{:S(2)}, u32[]{:S(2)}) collective-permute-start(bf16[1024,128]{1,0:T(8,128)(2,1)S(1)} %collective-permute-done.3.refs_5_), channel_id=1, source_target_pairs={{0,1},{1,0},{2,3},{3,2},{4,5},{5,4},{6,7},{7,6},{8,9},{9,8},{10,11... | collective-permute-start | bytes 786440 | tf_op jit(solution)/shard_map/ppermute | solution.py:29
  61.8 4.7 %collective-permute-start.12 = (bf16[1024,128]{1,0:T(8,128)(2,1)}, bf16[1024,128]{1,0:T(8,128)(2,1)}, u32[]{:S(2)}, u32[]{:S(2)}) collective-permute-start(bf16[1024,128]{1,0:T(8,128)(2,1)} %collective-permute-done.10.refs_12_), channel_id=1, source_target_pairs={{0,1},{1,0},{2,3},{3,2},{4,5},{5,4},{6,7},{7,6},{8,9},{9,8},{10,11... | collective-permute-start | bytes 786440 | tf_op jit(solution)/shard_map/ppermute | solution.py:29
  63.4 3.1 %collective-permute-start.13 = (bf16[1024,128]{1,0:T(8,128)(2,1)}, bf16[1024,128]{1,0:T(8,128)(2,1)}, u32[]{:S(2)}, u32[]{:S(2)}) collective-permute-start(bf16[1024,128]{1,0:T(8,128)(2,1)} %collective-permute-done.11.refs_13_), channel_id=1, source_target_pairs={{0,1},{1,0},{2,3},{3,2},{4,5},{5,4},{6,7},{7,6},{8,9},{9,8},{10,11... | collective-permute-start | bytes 786440 | tf_op jit(solution)/shard_map/ppermute | solution.py:29
  75.5 16.1 %collective-permute-start.20 = (bf16[1024,256]{1,0:T(8,128)(2,1)}, bf16[1024,256]{1,0:T(8,128)(2,1)S(1)}, u32[]{:S(2)}, u32[]{:S(2)}) collective-permute-start(bf16[1024,256]{1,0:T(8,128)(2,1)} %get-tuple-element.8.refs_1_), channel_id=1, source_target_pairs={{0,6},{2,0},{4,2},{6,4},{1,7},{3,1},{5,3},{7,5},{8,14},{10,8},{12,... | collective-permute-start | bytes 1572872 | tf_op jit(solution)/shard_map/ppermute | solution.py:29
  79.2 16.4 %collective-permute-start.16 = (bf16[1024,256]{1,0:T(8,128)(2,1)}, bf16[1024,256]{1,0:T(8,128)(2,1)S(1)}, u32[]{:S(2)}, u32[]{:S(2)}) collective-permute-start(bf16[1024,256]{1,0:T(8,128)(2,1)} %get-tuple-element.8.refs_1_), channel_id=1, source_target_pairs={{0,2},{2,4},{4,6},{6,0},{1,3},{3,5},{5,7},{7,1},{8,10},{10,12},{12... | collective-permute-start | bytes 1572872 | tf_op jit(solution)/shard_map/ppermute | solution.py:29
  79.5 16.4 %collective-permute-start.14 = (bf16[1024,256]{1,0:T(8,128)(2,1)}, bf16[1024,256]{1,0:T(8,128)(2,1)S(1)}, u32[]{:S(2)}, u32[]{:S(2)}) collective-permute-start(bf16[1024,256]{1,0:T(8,128)(2,1)} %get-tuple-element.8.refs_1_), channel_id=1, source_target_pairs={{0,1},{1,0},{2,3},{3,2},{4,5},{5,4},{6,7},{7,6},{8,9},{9,8},{10,11... | collective-permute-start | bytes 1572872 | tf_op jit(solution)/shard_map/ppermute | solution.py:29
  79.6 22.7 %collective-permute-start.21 = (bf16[1024,256]{1,0:T(8,128)(2,1)}, bf16[1024,256]{1,0:T(8,128)(2,1)S(1)}, u32[]{:S(2)}, u32[]{:S(2)}) collective-permute-start(bf16[1024,256]{1,0:T(8,128)(2,1)} %get-tuple-element.9.refs_2_), channel_id=1, source_target_pairs={{0,6},{2,0},{4,2},{6,4},{1,7},{3,1},{5,3},{7,5},{8,14},{10,8},{12,... | collective-permute-start | bytes 1572872 | tf_op jit(solution)/shard_map/ppermute | solution.py:29
  82.7 24.2 %collective-permute-start.17 = (bf16[1024,256]{1,0:T(8,128)(2,1)}, bf16[1024,256]{1,0:T(8,128)(2,1)S(1)}, u32[]{:S(2)}, u32[]{:S(2)}) collective-permute-start(bf16[1024,256]{1,0:T(8,128)(2,1)} %get-tuple-element.9.refs_2_), channel_id=1, source_target_pairs={{0,2},{2,4},{4,6},{6,0},{1,3},{3,5},{5,7},{7,1},{8,10},{10,12},{12... | collective-permute-start | bytes 1572872 | tf_op jit(solution)/shard_map/ppermute | solution.py:29
  91.7 15.5 %collective-permute-start.15 = (bf16[1024,256]{1,0:T(8,128)(2,1)}, bf16[1024,256]{1,0:T(8,128)(2,1)S(1)}, u32[]{:S(2)}, u32[]{:S(2)}) collective-permute-start(bf16[1024,256]{1,0:T(8,128)(2,1)} %get-tuple-element.9.refs_2_), channel_id=1, source_target_pairs={{0,1},{1,0},{2,3},{3,2},{4,5},{5,4},{6,7},{7,6},{8,9},{9,8},{10,11... | collective-permute-start | bytes 1572872 | tf_op jit(solution)/shard_map/ppermute | solution.py:29
  95.6 23.7 %collective-permute-start.22 = (bf16[1024,256]{1,0:T(8,128)(2,1)S(1)}, bf16[1024,256]{1,0:T(8,128)(2,1)S(1)}, u32[]{:S(2)}, u32[]{:S(2)}) collective-permute-start(bf16[1024,256]{1,0:T(8,128)(2,1)S(1)} %collective-permute-done.20.refs_9_), channel_id=1, source_target_pairs={{0,1},{1,0},{2,3},{3,2},{4,5},{5,4},{6,7},{7,6},{8,9},{9,8},{10,11... | collective-permute-start | bytes 1572872 | tf_op jit(solution)/shard_map/ppermute | solution.py:29
  95.9 21.3 %collective-permute-start.24 = (bf16[1024,256]{1,0:T(8,128)(2,1)S(1)}, bf16[1024,256]{1,0:T(8,128)(2,1)S(1)}, u32[]{:S(2)}, u32[]{:S(2)}) collective-permute-start(bf16[1024,256]{1,0:T(8,128)(2,1)S(1)} %collective-permute-done.16.refs_5_), channel_id=1, source_target_pairs={{0,2},{2,4},{4,6},{6,0},{1,3},{3,5},{5,7},{7,1},{8,10},{10,12},{12... | collective-permute-start | bytes 1572872 | tf_op jit(solution)/shard_map/ppermute | solution.py:29
  102.3 17.9 %collective-permute-start.18 = (bf16[1024,256]{1,0:T(8,128)(2,1)S(1)}, bf16[1024,256]{1,0:T(8,128)(2,1)S(1)}, u32[]{:S(2)}, u32[]{:S(2)}) collective-permute-start(bf16[1024,256]{1,0:T(8,128)(2,1)S(1)} %collective-permute-done.16.refs_5_), channel_id=1, source_target_pairs={{0,1},{1,0},{2,3},{3,2},{4,5},{5,4},{6,7},{7,6},{8,9},{9,8},{10,11... | collective-permute-start | bytes 1572872 | tf_op jit(solution)/shard_map/ppermute | solution.py:29
  106.9 12.2 %collective-permute-start.25 = (bf16[1024,256]{1,0:T(8,128)(2,1)S(1)}, bf16[1024,256]{1,0:T(8,128)(2,1)S(1)}, u32[]{:S(2)}, u32[]{:S(2)}) collective-permute-start(bf16[1024,256]{1,0:T(8,128)(2,1)S(1)} %collective-permute-done.21.refs_10_), channel_id=1, source_target_pairs={{0,6},{2,0},{4,2},{6,4},{1,7},{3,1},{5,3},{7,5},{8,14},{10,8},{12,... | collective-permute-start | bytes 1572872 | tf_op jit(solution)/shard_map/ppermute | solution.py:29
  107.1 13.3 %collective-permute-start.23 = (bf16[1024,256]{1,0:T(8,128)(2,1)S(1)}, bf16[1024,256]{1,0:T(8,128)(2,1)S(1)}, u32[]{:S(2)}, u32[]{:S(2)}) collective-permute-start(bf16[1024,256]{1,0:T(8,128)(2,1)S(1)} %collective-permute-done.21.refs_10_), channel_id=1, source_target_pairs={{0,1},{1,0},{2,3},{3,2},{4,5},{5,4},{6,7},{7,6},{8,9},{9,8},{10,11... | collective-permute-start | bytes 1572872 | tf_op jit(solution)/shard_map/ppermute | solution.py:29
  117.2 3.4 %collective-permute-start.19 = (bf16[1024,256]{1,0:T(8,128)(2,1)S(1)}, bf16[1024,256]{1,0:T(8,128)(2,1)S(1)}, u32[]{:S(2)}, u32[]{:S(2)}) collective-permute-start(bf16[1024,256]{1,0:T(8,128)(2,1)S(1)} %collective-permute-done.17.refs_6_), channel_id=1, source_target_pairs={{0,1},{1,0},{2,3},{3,2},{4,5},{5,4},{6,7},{7,6},{8,9},{9,8},{10,11... | collective-permute-start | bytes 1572872 | tf_op jit(solution)/shard_map/ppermute | solution.py:29
  119.1 1.9 %collective-permute-start.26 = (bf16[1024,256]{1,0:T(8,128)(2,1)S(1)}, bf16[1024,256]{1,0:T(8,128)(2,1)S(1)}, u32[]{:S(2)}, u32[]{:S(2)}) collective-permute-start(bf16[1024,256]{1,0:T(8,128)(2,1)S(1)} %collective-permute-done.24.refs_13_), channel_id=1, source_target_pairs={{0,1},{1,0},{2,3},{3,2},{4,5},{5,4},{6,7},{7,6},{8,9},{9,8},{10,11... | collective-permute-start | bytes 1572872 | tf_op jit(solution)/shard_map/ppermute | solution.py:29
  119.3 2.4 %collective-permute-start.27 = (bf16[1024,256]{1,0:T(8,128)(2,1)S(1)}, bf16[1024,256]{1,0:T(8,128)(2,1)S(1)}, u32[]{:S(2)}, u32[]{:S(2)}) collective-permute-start(bf16[1024,256]{1,0:T(8,128)(2,1)S(1)} %collective-permute-done.25.refs_14_), channel_id=1, source_target_pairs={{0,1},{1,0},{2,3},{3,2},{4,5},{5,4},{6,7},{7,6},{8,9},{9,8},{10,11... | collective-permute-start | bytes 1572872 | tf_op jit(solution)/shard_map/ppermute | solution.py:29
  152.8 10.1 %all-to-all-start.1 = ((f32[8,2,1024]{2,1,0:T(2,128)}), f32[8,2,1024]{2,1,0:T(2,128)S(1)}, u32[]{:S(2)}, u32[]{:S(2)}) async-start(f32[8,2,1024]{2,1,0:T(2,128)} %broadcast_in_dim.21), calls=%async_computation.1 | async-start | bytes 131072 | tf_op jit(solution)/shard_map/all_to_all | solution.py:24
  (23 other events, 253.4 us)
Sparse Core Ops, SparseCore 0:
  10.2 113.6 all-gather.1

commit v8 on v7

--- a/solution.py
+++ b/solution.py
@@ -289,10 +289,10 @@
         total = top * (1.0 / LOG2E) + jnp.log(total)
         pick = jnp.sum(pick_s[...], axis=1, keepdims=True) * (1.0 / LOG2E)
         both = jnp.where(lane == 0, total, jnp.where(lane == 1, pick, 0.0))
-        out_ref[...] = both.T[:2, :]
-
-
-def vocab_stats(first, row_blocks, scale, row_labels, vocab_all):
+        out_ref[...] = jnp.broadcast_to(both.T[None, :2, :], out_ref.shape)
+
+
+def vocab_stats(first, row_blocks, scale, row_labels, vocab_all, n_copies):
     n_rows = row_blocks[0].shape[0]
     n_blocks, width, columns = vocab_all.shape
     tile = 256
@@ -300,7 +300,7 @@
     kernel = lambda *refs: vocab_kernel(*refs, n_rows=len(row_blocks))
     return pl.pallas_call(
         kernel,
-        out_shape=jax.ShapeDtypeStruct((2, n_rows), jnp.float32),
+        out_shape=jax.ShapeDtypeStruct((n_copies, 2, n_rows), jnp.float32),
         grid_spec=pltpu.PrefetchScalarGridSpec(
             num_scalar_prefetch=1,
             grid=(n_blocks,),
@@ -310,7 +310,7 @@
                 whole(row_labels),
                 pl.BlockSpec((1, width, columns), lambda j, f: (j, 0, 0)),
             ],
-            out_specs=pl.BlockSpec((2, n_rows), lambda j, f: (0, 0)),
+            out_specs=pl.BlockSpec((n_copies, 2, n_rows), lambda j, f: (0, 0, 0)),
             scratch_shapes=[
                 pltpu.VMEM((n_rows, width), jnp.bfloat16),
                 *(pltpu.VMEM((tile, columns), jnp.float32) for _ in range(2)),
@@ -385,9 +385,9 @@
     row_labels = jnp.tile(labels.reshape(-1, 1), (prompts_here, 1))
     first = [lax.axis_index(MP) * vocab_cols, n_model * vocab_cols, *places]
     first = jnp.stack(first).astype(jnp.int32)
-    here = vocab_stats(first, row_blocks, scale, row_labels, vocab_all)
-
-    every = of_each(here, MP)
+    here = vocab_stats(first, row_blocks, scale, row_labels, vocab_all, n_model)
+
+    every = lax.all_to_all(here, MP, split_axis=0, concat_axis=0, tiled=True)
     top_val = jnp.max(every[:, 0], axis=0)
     log_total = top_val + jnp.log(jnp.sum(jnp.exp(every[:, 0] - top_val), axis=0))
     losses = (log_total - jnp.sum(every[:, 1], axis=0)).reshape(prompts_here, 1, target_len)

time: 187 us -> 185 us (0.989)
  no operation moved by 1% of the time
where the time goes in v8:
time: 185 us
  waiting for transfers between devices  56.5 us (31%)
  Pallas kernels  52.4 us (28%)
  starting transfers between devices  28.4 us (15%)
  between operations  15.2 us (8%)
  blocking collectives  13.6 us (7%)
  local copies, waits for them, and re-layouts  11.1 us (6%)
  other arithmetic  7.55 us (4%)
    ppermute x28, waiting for transfers between devices, shifted(): return lax.ppermute(value, axis, [(i, (i + shift) % n) for i in range(n)])  50.7 us
    pallas_call x1, Pallas kernels, vocab_stats(): pl.pallas_call(kernel, out_shape=jax.ShapeDtypeStruct((n_copies, 2, n_row...  27.6 us
    ppermute x28, starting transfers between devices, shifted(): return lax.ppermute(value, axis, [(i, (i + shift) % n) for i in range(n)])  18.5 us
    pallas_call x1, Pallas kernels, attention(): pl.pallas_call(attention_kernel, out_shape=[jax.ShapeDtypeStruct((rows, i...  14.4 us
    all_to_all x1, blocking collectives, of_each(): return lax.all_to_all(copies, axis, split_axis=0, concat_axis=0, tiled=True)  13.6 us
    pallas_call x1, Pallas kernels, output_part(): pl.pallas_call(output_kernel, out_shape=[jax.ShapeDtypeStruct((rows, part...  7.57 us
    unnamed x52, local copies, waits for them, and re-layouts  6.55 us
    all_to_all x1, waiting for transfers between devices, shards(): every = lax.all_to_all(here, MP, split_axis=0, concat_axis=0, tiled=True)  5.62 us
  transfers between devices with their start and end apart: 31, of which 15 were waited for; matrix products, arithmetic and copies ran while one was open for 6% of the time, Pallas kernels for 13%

profile of v8, /device:TPU:0, one launch (start us, length us, event | category | flops | bytes accessed | tf_op | source)
XLA Modules:
  0.0 184.9 jit_solution(15397241562871913782)
XLA Ops:
  7.2 2.3 %constant_dynamic-slice_fusion = bf16[1024,512]{1,0:T(8,128)(2,1)} fusion(bf16[4096,512]{1,0:T(8,128)(2,1)} %param.21, s32[]{:T(128)S(6)} %select_n.136), kind=kLoop, calls=%fused_computation.31 | loop fusion | bytes 2097156 | tf_op jit(solution)/shard_map/dynamic_slice | solution.py:367
  9.5 2.7 %split_columns.1 = bf16[8,256,512]{2,1,0:T(8,128)(2,1)} custom-call(bf16[256,4096]{1,0:T(8,128)(2,1)} %w_ref.3), custom_call_target="tpu_custom_call" | custom-call | bytes 4194304 | tf_op jit(solution)/shard_map/split_columns/pallas_call | solution.py:340
  12.3 5.4 %all-to-all-start = ((bf16[8,256,512]{2,1,0:T(8,128)(2,1)}), bf16[8,256,512]{2,1,0:T(8,128)(2,1)S(1)}, u32[]{:S(2)}, u32[]{:S(2)}) async-start(bf16[8,256,512]{2,1,0:T(8,128)(2,1)} %split_columns.1), calls=%async_computation | async-start | bytes 4194304 | tf_op jit(solution)/shard_map/all_to_all | solution.py:371
  17.7 3.6 %copy.30.prompt_ref = bf16[2,100,4096]{2,1,0:T(8,128)(2,1)} copy(bf16[2,100,4096]{2,0,1:T(2,128)(2,1)} %param.13) | data formatting | bytes 3276800 | tf_op args[0]
  21.2 14.4 %attention.1 = (bf16[1024,128]{1,0:T(8,128)(2,1)}, bf16[1024,128]{1,0:T(8,128)(2,1)}) custom-call(bf16[1,512,4096]{2,1,0:T(8,128)(2,1)} %refs_17_.1, bf16[2,100,4096]{2,1,0:T(8,128)(2,1)} %copy.30.prompt_ref, f32[1,4096]{1,0:T(1,128)} %bitcast.38, bf16[3,4096,256]{2,1,0:T(8,128)(2,1)} %w_ref.2, f32[512,64]{1,0:T(8,128)} %constant.113.clone.cos_t, ...), custom_call_target="tpu_custom_call" | custom-call | flops 8000000000 | bytes 12000000 | tf_op jit(solution)/shard_map/attention/pallas_call | solution.py:168
  35.7 3.2 %collective-permute-start.6 = (bf16[1024,128]{1,0:T(8,128)(2,1)}, bf16[1024,128]{1,0:T(8,128)(2,1)S(1)}, u32[]{:S(2)}, u32[]{:S(2)}) collective-permute-start(bf16[1024,128]{1,0:T(8,128)(2,1)} %get-tuple-element.6.refs_0_), channel_id=1, source_target_pairs={{0,6},{2,0},{4,2},{6,4},{1,7},{3,1},{5,3},{7,5},{8,14},{10,8},{12,... | collective-permute-start | bytes 786440 | tf_op jit(solution)/shard_map/ppermute | solution.py:29
  38.9 3.2 %collective-permute-start.7 = (bf16[1024,128]{1,0:T(8,128)(2,1)}, bf16[1024,128]{1,0:T(8,128)(2,1)S(1)}, u32[]{:S(2)}, u32[]{:S(2)}) collective-permute-start(bf16[1024,128]{1,0:T(8,128)(2,1)} %get-tuple-element.7.refs_1_), channel_id=1, source_target_pairs={{0,6},{2,0},{4,2},{6,4},{1,7},{3,1},{5,3},{7,5},{8,14},{10,8},{12,... | collective-permute-start | bytes 786440 | tf_op jit(solution)/shard_map/ppermute | solution.py:29
  42.2 7.3 %collective-permute-done.6.refs_8_ = bf16[1024,128]{1,0:T(8,128)(2,1)S(1)} collective-permute-done((bf16[1024,128]{1,0:T(8,128)(2,1)}, bf16[1024,128]{1,0:T(8,128)(2,1)S(1)}, u32[]{:S(2)}, u32[]{:S(2)}) %collective-permute-start.6) | collective-permute-done | bytes 262176 | tf_op jit(solution)/shard_map/ppermute | solution.py:29
  49.5 1.1 collective-permute-done.2.refs_4_
  50.6 1.0 collective-permute-start.10
  51.6 3.0 %collective-permute-done.7.refs_9_ = bf16[1024,128]{1,0:T(8,128)(2,1)S(1)} collective-permute-done((bf16[1024,128]{1,0:T(8,128)(2,1)}, bf16[1024,128]{1,0:T(8,128)(2,1)S(1)}, u32[]{:S(2)}, u32[]{:S(2)}) %collective-permute-start.7) | collective-permute-done | bytes 262176 | tf_op jit(solution)/shard_map/ppermute | solution.py:29
  54.6 2.6 %collective-permute-start.11 = (bf16[1024,128]{1,0:T(8,128)(2,1)S(1)}, bf16[1024,128]{1,0:T(8,128)(2,1)}, u32[]{:S(2)}, u32[]{:S(2)}) collective-permute-start(bf16[1024,128]{1,0:T(8,128)(2,1)S(1)} %collective-permute-done.7.refs_9_), channel_id=1, source_target_pairs={{0,6},{2,0},{4,2},{6,4},{1,7},{3,1},{5,3},{7,5},{8,14},{10,8},{12,... | collective-permute-start | bytes 786440 | tf_op jit(solution)/shard_map/ppermute | solution.py:29
  57.9 3.9 %collective-permute-done.10.refs_12_ = bf16[1024,128]{1,0:T(8,128)(2,1)} collective-permute-done((bf16[1024,128]{1,0:T(8,128)(2,1)S(1)}, bf16[1024,128]{1,0:T(8,128)(2,1)}, u32[]{:S(2)}, u32[]{:S(2)}) %collective-permute-start.10) | collective-permute-done | bytes 262176 | tf_op jit(solution)/shard_map/ppermute | solution.py:29
  61.8 1.5 collective-permute-done.11.refs_13_
  64.2 1.1 copy.40
  66.6 1.3 copy-done.1
  68.0 7.6 %output_part.1 = (bf16[1024,256]{1,0:T(8,128)(2,1)}, bf16[1024,256]{1,0:T(8,128)(2,1)}) custom-call(s32[8]{0:T(128)} %stack.51.places_ref, bf16[1024,128]{1,0:T(8,128)(2,1)} %get-tuple-element.6.refs_0_, bf16[1024,128]{1,0:T(8,128)(2,1)} %get-tuple-element.7.refs_1_, bf16[1024,128]{1,0:T(8,128)(2,1)} %copy-done.18, bf16[1024,128]{1,0:T(8,128)(2,1)} %copy-done.21, ...), custom_call_target="tpu_custom_call" | custom-call | flops 2000000000 | bytes 8000000 | tf_op jit(solution)/shard_map/output_part/pallas_call | solution.py:213
  75.5 3.5 %collective-permute-start.20 = (bf16[1024,256]{1,0:T(8,128)(2,1)}, bf16[1024,256]{1,0:T(8,128)(2,1)S(1)}, u32[]{:S(2)}, u32[]{:S(2)}) collective-permute-start(bf16[1024,256]{1,0:T(8,128)(2,1)} %get-tuple-element.8.refs_1_), channel_id=1, source_target_pairs={{0,6},{2,0},{4,2},{6,4},{1,7},{3,1},{5,3},{7,5},{8,14},{10,8},{12,... | collective-permute-start | bytes 1572872 | tf_op jit(solution)/shard_map/ppermute | solution.py:29
  79.6 3.1 %collective-permute-start.21 = (bf16[1024,256]{1,0:T(8,128)(2,1)}, bf16[1024,256]{1,0:T(8,128)(2,1)S(1)}, u32[]{:S(2)}, u32[]{:S(2)}) collective-permute-start(bf16[1024,256]{1,0:T(8,128)(2,1)} %get-tuple-element.9.refs_2_), channel_id=1, source_target_pairs={{0,6},{2,0},{4,2},{6,4},{1,7},{3,1},{5,3},{7,5},{8,14},{10,8},{12,... | collective-permute-start | bytes 1572872 | tf_op jit(solution)/shard_map/ppermute | solution.py:29
  82.7 1.6 multiply_reduce_fusion.14
  84.2 7.4 %collective-permute-done.20.refs_9_ = bf16[1024,256]{1,0:T(8,128)(2,1)S(1)} collective-permute-done((bf16[1024,256]{1,0:T(8,128)(2,1)}, bf16[1024,256]{1,0:T(8,128)(2,1)S(1)}, u32[]{:S(2)}, u32[]{:S(2)}) %collective-permute-start.20) | collective-permute-done | bytes 524320 | tf_op jit(solution)/shard_map/ppermute | solution.py:29
  91.9 3.8 %collective-permute-done.16.refs_5_ = bf16[1024,256]{1,0:T(8,128)(2,1)S(1)} collective-permute-done((bf16[1024,256]{1,0:T(8,128)(2,1)}, bf16[1024,256]{1,0:T(8,128)(2,1)S(1)}, u32[]{:S(2)}, u32[]{:S(2)}) %collective-permute-start.16) | collective-permute-done | bytes 524320 | tf_op jit(solution)/shard_map/ppermute | solution.py:29
  96.2 6.1 %collective-permute-done.21.refs_10_ = bf16[1024,256]{1,0:T(8,128)(2,1)S(1)} collective-permute-done((bf16[1024,256]{1,0:T(8,128)(2,1)}, bf16[1024,256]{1,0:T(8,128)(2,1)S(1)}, u32[]{:S(2)}, u32[]{:S(2)}) %collective-permute-start.21) | collective-permute-done | bytes 524320 | tf_op jit(solution)/shard_map/ppermute | solution.py:29
  102.5 4.4 %collective-permute-done.17.refs_6_ = bf16[1024,256]{1,0:T(8,128)(2,1)S(1)} collective-permute-done((bf16[1024,256]{1,0:T(8,128)(2,1)}, bf16[1024,256]{1,0:T(8,128)(2,1)S(1)}, u32[]{:S(2)}, u32[]{:S(2)}) %collective-permute-start.17) | collective-permute-done | bytes 524320 | tf_op jit(solution)/shard_map/ppermute | solution.py:29
  107.4 9.8 %collective-permute-done.24.refs_13_ = bf16[1024,256]{1,0:T(8,128)(2,1)S(1)} collective-permute-done((bf16[1024,256]{1,0:T(8,128)(2,1)S(1)}, bf16[1024,256]{1,0:T(8,128)(2,1)S(1)}, u32[]{:S(2)}, u32[]{:S(2)}) %collective-permute-start.24) | collective-permute-done | bytes 524320 | tf_op jit(solution)/shard_map/ppermute | solution.py:29
  117.4 1.7 collective-permute-done.25.refs_14_
  122.8 0.9 rsqrt_multiply_fusion.refs_17_
  123.9 27.6 %vocab_stats.1 = f32[8,2,1024]{2,1,0:T(2,128)} custom-call(s32[10]{0:T(128)} %stack.50.refs_0_, bf16[1024,256]{1,0:T(8,128)(2,1)} %get-tuple-element.8.refs_1_, bf16[1024,256]{1,0:T(8,128)(2,1)} %get-tuple-element.9.refs_2_, bf16[1024,256]{1,0:T(8,128)(2,1)} %copy-done.4, bf16[1024,256]{1,0:T(8,128)(2,1)} %copy-done.7, bf16[1024,256]{1,0:T(8,128)(2,1)} %copy-done.3, ...), custom_call_target="tpu_custom_call" | custom-call | flops 17179869184 | bytes 25165824 | tf_op jit(solution)/shard_map/vocab_stats/pallas_call | solution.py:301
  151.5 4.5 %all-to-all-start.1 = ((f32[8,2,1024]{2,1,0:T(2,128)}), f32[8,2,1024]{2,1,0:T(2,128)S(1)}, u32[]{:S(2)}, u32[]{:S(2)}) async-start(f32[8,2,1024]{2,1,0:T(2,128)} %vocab_stats.1), calls=%async_computation.1 | async-start | bytes 131072 | tf_op jit(solution)/shard_map/all_to_all | solution.py:390
  156.0 5.6 %all-to-all-done.1 = f32[8,2,1024]{2,1,0:T(2,128)S(1)} async-done(((f32[8,2,1024]{2,1,0:T(2,128)}), f32[8,2,1024]{2,1,0:T(2,128)S(1)}, u32[]{:S(2)}, u32[]{:S(2)}) %all-to-all-start.1) | async-done | bytes 65568 | tf_op jit(solution)/shard_map/all_to_all | solution.py:390
  162.5 13.6 %all_to_all.16 = f32[16,1,9]{2,1,0:T(1,128)S(1)} all-to-all(f32[16,1,9]{2,1,0:T(1,128)S(1)} %broadcast_in_dim.22), channel_id=1, replica_groups=mesh['prompt'=4,'dp'=4,'mp_0'=4,'mp_1'=2] {'prompt','dp'}, dimensions={0} | all-to-all | bytes 1152 | tf_op jit(solution)/shard_map/all_to_all | solution.py:24
  176.8 1.2 multiply_divide_fusion
  (122 shorter events, 9.5 us)
Async XLA Ops:
  7.2 57.0 %copy-start = (s32[1,512]{1,0:T(1,128)S(1)}, s32[1,512]{1,0:T(1,128)}, u32[]{:S(2)}) copy-start(s32[1,512]{1,0:T(1,128)} %param.15) | copy-start | bytes 6148
  7.2 116.7 %all-gather.2.cloned.1.call-start = ((), (), s32[]{:S(2)}) async-start(), calls=%async_computation.3 | async-start | bytes 17825792 | tf_op jit(solution)/shard_map/all_gather | solution.py:368
  12.3 54.3 %all-to-all-start = ((bf16[8,256,512]{2,1,0:T(8,128)(2,1)}), bf16[8,256,512]{2,1,0:T(8,128)(2,1)S(1)}, u32[]{:S(2)}, u32[]{:S(2)}) async-start(bf16[8,256,512]{2,1,0:T(8,128)(2,1)} %split_columns.1), calls=%async_computation | async-start | bytes 4194304 | tf_op jit(solution)/shard_map/all_to_all | solution.py:371
  35.7 13.8 %collective-permute-start.6 = (bf16[1024,128]{1,0:T(8,128)(2,1)}, bf16[1024,128]{1,0:T(8,128)(2,1)S(1)}, u32[]{:S(2)}, u32[]{:S(2)}) collective-permute-start(bf16[1024,128]{1,0:T(8,128)(2,1)} %get-tuple-element.6.refs_0_), channel_id=1, source_target_pairs={{0,6},{2,0},{4,2},{6,4},{1,7},{3,1},{5,3},{7,5},{8,14},{10,8},{12,... | collective-permute-start | bytes 786440 | tf_op jit(solution)/shard_map/ppermute | solution.py:29
  38.9 11.6 %collective-permute-start.2 = (bf16[1024,128]{1,0:T(8,128)(2,1)}, bf16[1024,128]{1,0:T(8,128)(2,1)S(1)}, u32[]{:S(2)}, u32[]{:S(2)}) collective-permute-start(bf16[1024,128]{1,0:T(8,128)(2,1)} %get-tuple-element.6.refs_0_), channel_id=1, source_target_pairs={{0,2},{2,4},{4,6},{6,0},{1,3},{3,5},{5,7},{7,1},{8,10},{10,12},{12... | collective-permute-start | bytes 786440 | tf_op jit(solution)/shard_map/ppermute | solution.py:29
  38.9 11.6 %collective-permute-start = (bf16[1024,128]{1,0:T(8,128)(2,1)}, bf16[1024,128]{1,0:T(8,128)(2,1)S(1)}, u32[]{:S(2)}, u32[]{:S(2)}) collective-permute-start(bf16[1024,128]{1,0:T(8,128)(2,1)} %get-tuple-element.6.refs_0_), channel_id=1, source_target_pairs={{0,1},{1,0},{2,3},{3,2},{4,5},{5,4},{6,7},{7,6},{8,9},{9,8},{10,11... | collective-permute-start | bytes 786440 | tf_op jit(solution)/shard_map/ppermute | solution.py:29
  38.9 15.7 %collective-permute-start.7 = (bf16[1024,128]{1,0:T(8,128)(2,1)}, bf16[1024,128]{1,0:T(8,128)(2,1)S(1)}, u32[]{:S(2)}, u32[]{:S(2)}) collective-permute-start(bf16[1024,128]{1,0:T(8,128)(2,1)} %get-tuple-element.7.refs_1_), channel_id=1, source_target_pairs={{0,6},{2,0},{4,2},{6,4},{1,7},{3,1},{5,3},{7,5},{8,14},{10,8},{12,... | collective-permute-start | bytes 786440 | tf_op jit(solution)/shard_map/ppermute | solution.py:29
  42.2 15.1 %collective-permute-start.3 = (bf16[1024,128]{1,0:T(8,128)(2,1)}, bf16[1024,128]{1,0:T(8,128)(2,1)S(1)}, u32[]{:S(2)}, u32[]{:S(2)}) collective-permute-start(bf16[1024,128]{1,0:T(8,128)(2,1)} %get-tuple-element.7.refs_1_), channel_id=1, source_target_pairs={{0,2},{2,4},{4,6},{6,0},{1,3},{3,5},{5,7},{7,1},{8,10},{10,12},{12... | collective-permute-start | bytes 786440 | tf_op jit(solution)/shard_map/ppermute | solution.py:29
  49.5 7.8 %collective-permute-start.1 = (bf16[1024,128]{1,0:T(8,128)(2,1)}, bf16[1024,128]{1,0:T(8,128)(2,1)S(1)}, u32[]{:S(2)}, u32[]{:S(2)}) collective-permute-start(bf16[1024,128]{1,0:T(8,128)(2,1)} %get-tuple-element.7.refs_1_), channel_id=1, source_target_pairs={{0,1},{1,0},{2,3},{3,2},{4,5},{5,4},{6,7},{7,6},{8,9},{9,8},{10,11... | collective-permute-start | bytes 786440 | tf_op jit(solution)/shard_map/ppermute | solution.py:29
  50.6 7.2 %collective-permute-start.8 = (bf16[1024,128]{1,0:T(8,128)(2,1)S(1)}, bf16[1024,128]{1,0:T(8,128)(2,1)S(1)}, u32[]{:S(2)}, u32[]{:S(2)}) collective-permute-start(bf16[1024,128]{1,0:T(8,128)(2,1)S(1)} %collective-permute-done.6.refs_8_), channel_id=1, source_target_pairs={{0,1},{1,0},{2,3},{3,2},{4,5},{5,4},{6,7},{7,6},{8,9},{9,8},{10,11... | collective-permute-start | bytes 786440 | tf_op jit(solution)/shard_map/ppermute | solution.py:29
  50.6 11.2 %collective-permute-start.10 = (bf16[1024,128]{1,0:T(8,128)(2,1)S(1)}, bf16[1024,128]{1,0:T(8,128)(2,1)}, u32[]{:S(2)}, u32[]{:S(2)}) collective-permute-start(bf16[1024,128]{1,0:T(8,128)(2,1)S(1)} %collective-permute-done.2.refs_4_), channel_id=1, source_target_pairs={{0,2},{2,4},{4,6},{6,0},{1,3},{3,5},{5,7},{7,1},{8,10},{10,12},{12... | collective-permute-start | bytes 786440 | tf_op jit(solution)/shard_map/ppermute | solution.py:29
  54.6 8.7 %collective-permute-start.11 = (bf16[1024,128]{1,0:T(8,128)(2,1)S(1)}, bf16[1024,128]{1,0:T(8,128)(2,1)}, u32[]{:S(2)}, u32[]{:S(2)}) collective-permute-start(bf16[1024,128]{1,0:T(8,128)(2,1)S(1)} %collective-permute-done.7.refs_9_), channel_id=1, source_target_pairs={{0,6},{2,0},{4,2},{6,4},{1,7},{3,1},{5,3},{7,5},{8,14},{10,8},{12,... | collective-permute-start | bytes 786440 | tf_op jit(solution)/shard_map/ppermute | solution.py:29
  57.3 9.2 %collective-permute-start.4 = (bf16[1024,128]{1,0:T(8,128)(2,1)S(1)}, bf16[1024,128]{1,0:T(8,128)(2,1)}, u32[]{:S(2)}, u32[]{:S(2)}) collective-permute-start(bf16[1024,128]{1,0:T(8,128)(2,1)S(1)} %collective-permute-done.2.refs_4_), channel_id=1, source_target_pairs={{0,1},{1,0},{2,3},{3,2},{4,5},{5,4},{6,7},{7,6},{8,9},{9,8},{10,11... | collective-permute-start | bytes 786440 | tf_op jit(solution)/shard_map/ppermute | solution.py:29
  57.3 9.2 %collective-permute-start.9 = (bf16[1024,128]{1,0:T(8,128)(2,1)S(1)}, bf16[1024,128]{1,0:T(8,128)(2,1)}, u32[]{:S(2)}, u32[]{:S(2)}) collective-permute-start(bf16[1024,128]{1,0:T(8,128)(2,1)S(1)} %collective-permute-done.7.refs_9_), channel_id=1, source_target_pairs={{0,1},{1,0},{2,3},{3,2},{4,5},{5,4},{6,7},{7,6},{8,9},{9,8},{10,11... | collective-permute-start | bytes 786440 | tf_op jit(solution)/shard_map/ppermute | solution.py:29
  57.8 8.7 %collective-permute-start.5 = (bf16[1024,128]{1,0:T(8,128)(2,1)S(1)}, bf16[1024,128]{1,0:T(8,128)(2,1)}, u32[]{:S(2)}, u32[]{:S(2)}) collective-permute-start(bf16[1024,128]{1,0:T(8,128)(2,1)S(1)} %collective-permute-done.3.refs_5_), channel_id=1, source_target_pairs={{0,1},{1,0},{2,3},{3,2},{4,5},{5,4},{6,7},{7,6},{8,9},{9,8},{10,11... | collective-permute-start | bytes 786440 | tf_op jit(solution)/shard_map/ppermute | solution.py:29
  61.8 4.7 %collective-permute-start.12 = (bf16[1024,128]{1,0:T(8,128)(2,1)}, bf16[1024,128]{1,0:T(8,128)(2,1)}, u32[]{:S(2)}, u32[]{:S(2)}) collective-permute-start(bf16[1024,128]{1,0:T(8,128)(2,1)} %collective-permute-done.10.refs_12_), channel_id=1, source_target_pairs={{0,1},{1,0},{2,3},{3,2},{4,5},{5,4},{6,7},{7,6},{8,9},{9,8},{10,11... | collective-permute-start | bytes 786440 | tf_op jit(solution)/shard_map/ppermute | solution.py:29
  63.4 3.1 %collective-permute-start.13 = (bf16[1024,128]{1,0:T(8,128)(2,1)}, bf16[1024,128]{1,0:T(8,128)(2,1)}, u32[]{:S(2)}, u32[]{:S(2)}) collective-permute-start(bf16[1024,128]{1,0:T(8,128)(2,1)} %collective-permute-done.11.refs_13_), channel_id=1, source_target_pairs={{0,1},{1,0},{2,3},{3,2},{4,5},{5,4},{6,7},{7,6},{8,9},{9,8},{10,11... | collective-permute-start | bytes 786440 | tf_op jit(solution)/shard_map/ppermute | solution.py:29
  75.5 16.1 %collective-permute-start.20 = (bf16[1024,256]{1,0:T(8,128)(2,1)}, bf16[1024,256]{1,0:T(8,128)(2,1)S(1)}, u32[]{:S(2)}, u32[]{:S(2)}) collective-permute-start(bf16[1024,256]{1,0:T(8,128)(2,1)} %get-tuple-element.8.refs_1_), channel_id=1, source_target_pairs={{0,6},{2,0},{4,2},{6,4},{1,7},{3,1},{5,3},{7,5},{8,14},{10,8},{12,... | collective-permute-start | bytes 1572872 | tf_op jit(solution)/shard_map/ppermute | solution.py:29
  79.2 16.4 %collective-permute-start.16 = (bf16[1024,256]{1,0:T(8,128)(2,1)}, bf16[1024,256]{1,0:T(8,128)(2,1)S(1)}, u32[]{:S(2)}, u32[]{:S(2)}) collective-permute-start(bf16[1024,256]{1,0:T(8,128)(2,1)} %get-tuple-element.8.refs_1_), channel_id=1, source_target_pairs={{0,2},{2,4},{4,6},{6,0},{1,3},{3,5},{5,7},{7,1},{8,10},{10,12},{12... | collective-permute-start | bytes 1572872 | tf_op jit(solution)/shard_map/ppermute | solution.py:29
  79.5 16.4 %collective-permute-start.14 = (bf16[1024,256]{1,0:T(8,128)(2,1)}, bf16[1024,256]{1,0:T(8,128)(2,1)S(1)}, u32[]{:S(2)}, u32[]{:S(2)}) collective-permute-start(bf16[1024,256]{1,0:T(8,128)(2,1)} %get-tuple-element.8.refs_1_), channel_id=1, source_target_pairs={{0,1},{1,0},{2,3},{3,2},{4,5},{5,4},{6,7},{7,6},{8,9},{9,8},{10,11... | collective-permute-start | bytes 1572872 | tf_op jit(solution)/shard_map/ppermute | solution.py:29
  79.6 22.7 %collective-permute-start.21 = (bf16[1024,256]{1,0:T(8,128)(2,1)}, bf16[1024,256]{1,0:T(8,128)(2,1)S(1)}, u32[]{:S(2)}, u32[]{:S(2)}) collective-permute-start(bf16[1024,256]{1,0:T(8,128)(2,1)} %get-tuple-element.9.refs_2_), channel_id=1, source_target_pairs={{0,6},{2,0},{4,2},{6,4},{1,7},{3,1},{5,3},{7,5},{8,14},{10,8},{12,... | collective-permute-start | bytes 1572872 | tf_op jit(solution)/shard_map/ppermute | solution.py:29
  82.7 24.2 %collective-permute-start.17 = (bf16[1024,256]{1,0:T(8,128)(2,1)}, bf16[1024,256]{1,0:T(8,128)(2,1)S(1)}, u32[]{:S(2)}, u32[]{:S(2)}) collective-permute-start(bf16[1024,256]{1,0:T(8,128)(2,1)} %get-tuple-element.9.refs_2_), channel_id=1, source_target_pairs={{0,2},{2,4},{4,6},{6,0},{1,3},{3,5},{5,7},{7,1},{8,10},{10,12},{12... | collective-permute-start | bytes 1572872 | tf_op jit(solution)/shard_map/ppermute | solution.py:29
  91.7 15.5 %collective-permute-start.15 = (bf16[1024,256]{1,0:T(8,128)(2,1)}, bf16[1024,256]{1,0:T(8,128)(2,1)S(1)}, u32[]{:S(2)}, u32[]{:S(2)}) collective-permute-start(bf16[1024,256]{1,0:T(8,128)(2,1)} %get-tuple-element.9.refs_2_), channel_id=1, source_target_pairs={{0,1},{1,0},{2,3},{3,2},{4,5},{5,4},{6,7},{7,6},{8,9},{9,8},{10,11... | collective-permute-start | bytes 1572872 | tf_op jit(solution)/shard_map/ppermute | solution.py:29
  95.6 23.7 %collective-permute-start.22 = (bf16[1024,256]{1,0:T(8,128)(2,1)S(1)}, bf16[1024,256]{1,0:T(8,128)(2,1)S(1)}, u32[]{:S(2)}, u32[]{:S(2)}) collective-permute-start(bf16[1024,256]{1,0:T(8,128)(2,1)S(1)} %collective-permute-done.20.refs_9_), channel_id=1, source_target_pairs={{0,1},{1,0},{2,3},{3,2},{4,5},{5,4},{6,7},{7,6},{8,9},{9,8},{10,11... | collective-permute-start | bytes 1572872 | tf_op jit(solution)/shard_map/ppermute | solution.py:29
  95.9 21.3 %collective-permute-start.24 = (bf16[1024,256]{1,0:T(8,128)(2,1)S(1)}, bf16[1024,256]{1,0:T(8,128)(2,1)S(1)}, u32[]{:S(2)}, u32[]{:S(2)}) collective-permute-start(bf16[1024,256]{1,0:T(8,128)(2,1)S(1)} %collective-permute-done.16.refs_5_), channel_id=1, source_target_pairs={{0,2},{2,4},{4,6},{6,0},{1,3},{3,5},{5,7},{7,1},{8,10},{10,12},{12... | collective-permute-start | bytes 1572872 | tf_op jit(solution)/shard_map/ppermute | solution.py:29
  102.3 17.9 %collective-permute-start.18 = (bf16[1024,256]{1,0:T(8,128)(2,1)S(1)}, bf16[1024,256]{1,0:T(8,128)(2,1)S(1)}, u32[]{:S(2)}, u32[]{:S(2)}) collective-permute-start(bf16[1024,256]{1,0:T(8,128)(2,1)S(1)} %collective-permute-done.16.refs_5_), channel_id=1, source_target_pairs={{0,1},{1,0},{2,3},{3,2},{4,5},{5,4},{6,7},{7,6},{8,9},{9,8},{10,11... | collective-permute-start | bytes 1572872 | tf_op jit(solution)/shard_map/ppermute | solution.py:29
  106.9 12.2 %collective-permute-start.25 = (bf16[1024,256]{1,0:T(8,128)(2,1)S(1)}, bf16[1024,256]{1,0:T(8,128)(2,1)S(1)}, u32[]{:S(2)}, u32[]{:S(2)}) collective-permute-start(bf16[1024,256]{1,0:T(8,128)(2,1)S(1)} %collective-permute-done.21.refs_10_), channel_id=1, source_target_pairs={{0,6},{2,0},{4,2},{6,4},{1,7},{3,1},{5,3},{7,5},{8,14},{10,8},{12,... | collective-permute-start | bytes 1572872 | tf_op jit(solution)/shard_map/ppermute | solution.py:29
  107.1 13.3 %collective-permute-start.23 = (bf16[1024,256]{1,0:T(8,128)(2,1)S(1)}, bf16[1024,256]{1,0:T(8,128)(2,1)S(1)}, u32[]{:S(2)}, u32[]{:S(2)}) collective-permute-start(bf16[1024,256]{1,0:T(8,128)(2,1)S(1)} %collective-permute-done.21.refs_10_), channel_id=1, source_target_pairs={{0,1},{1,0},{2,3},{3,2},{4,5},{5,4},{6,7},{7,6},{8,9},{9,8},{10,11... | collective-permute-start | bytes 1572872 | tf_op jit(solution)/shard_map/ppermute | solution.py:29
  117.2 3.4 %collective-permute-start.19 = (bf16[1024,256]{1,0:T(8,128)(2,1)S(1)}, bf16[1024,256]{1,0:T(8,128)(2,1)S(1)}, u32[]{:S(2)}, u32[]{:S(2)}) collective-permute-start(bf16[1024,256]{1,0:T(8,128)(2,1)S(1)} %collective-permute-done.17.refs_6_), channel_id=1, source_target_pairs={{0,1},{1,0},{2,3},{3,2},{4,5},{5,4},{6,7},{7,6},{8,9},{9,8},{10,11... | collective-permute-start | bytes 1572872 | tf_op jit(solution)/shard_map/ppermute | solution.py:29
  119.1 1.9 %collective-permute-start.26 = (bf16[1024,256]{1,0:T(8,128)(2,1)S(1)}, bf16[1024,256]{1,0:T(8,128)(2,1)S(1)}, u32[]{:S(2)}, u32[]{:S(2)}) collective-permute-start(bf16[1024,256]{1,0:T(8,128)(2,1)S(1)} %collective-permute-done.24.refs_13_), channel_id=1, source_target_pairs={{0,1},{1,0},{2,3},{3,2},{4,5},{5,4},{6,7},{7,6},{8,9},{9,8},{10,11... | collective-permute-start | bytes 1572872 | tf_op jit(solution)/shard_map/ppermute | solution.py:29
  119.3 2.4 %collective-permute-start.27 = (bf16[1024,256]{1,0:T(8,128)(2,1)S(1)}, bf16[1024,256]{1,0:T(8,128)(2,1)S(1)}, u32[]{:S(2)}, u32[]{:S(2)}) collective-permute-start(bf16[1024,256]{1,0:T(8,128)(2,1)S(1)} %collective-permute-done.25.refs_14_), channel_id=1, source_target_pairs={{0,1},{1,0},{2,3},{3,2},{4,5},{5,4},{6,7},{7,6},{8,9},{9,8},{10,11... | collective-permute-start | bytes 1572872 | tf_op jit(solution)/shard_map/ppermute | solution.py:29
  151.5 10.1 %all-to-all-start.1 = ((f32[8,2,1024]{2,1,0:T(2,128)}), f32[8,2,1024]{2,1,0:T(2,128)S(1)}, u32[]{:S(2)}, u32[]{:S(2)}) async-start(f32[8,2,1024]{2,1,0:T(2,128)} %vocab_stats.1), calls=%async_computation.1 | async-start | bytes 131072 | tf_op jit(solution)/shard_map/all_to_all | solution.py:390
  (23 other events, 253.4 us)
Sparse Core Ops, SparseCore 0:
  10.2 113.6 all-gather.1
